TPU v7x, 32 devices: a whole 2x2x4 slice. The times are simulated.
32 devices in a mesh: parts: 2 (over x), blocks: 16 (over z, y, core).
Axes of the slice: x: 2, y: 2, z: 4, core: 2. Of those that a mesh axis runs over, the one named last changes fastest.
Arguments:
- coords: float32 [640, 3, 32768], P('blocks', None, 'parts'), parts along dimension 2
- pairs: int32 [2, 2048], replicated, may hold values from 0 to 639
- res_slot: int32 [640], replicated, may hold values from 0 to 639, each once
Outputs:
- distances: bfloat16 [4, 32768, 1024], P(None, ('parts', 'blocks')), parts along dimension 1
There are 2 independent parts, one for each index of `parts`. A program takes and returns all parts, laid end to end along the dimension named above; an argument that names none is the same for every part. Nothing has to cross between parts.
All inputs are finite; a program needn't handle non-finite values.
Results may differ from a plain program's by a relative error of at most 0.0025.
Values may be sent and summed in bfloat16 or wider, within the bound.
No kernel may reach another device: no remote copies, remote signals or barrier semaphores. Data moves between devices by JAX's collectives and lax.ppermute only.
A program may use at most 192 MiB of HBM per device.

v0:
```python
import functools
import math

import jax
import jax.numpy as jnp
from jax import lax
from jax.experimental import pallas as pl
from jax.experimental.pallas import tpu as pltpu
from jax.sharding import PartitionSpec as P


ROUNDS = 4
VMEM_BYTES = 58 * 1024 * 1024


def permuted(shard, axis, to):
    count = lax.axis_size(axis)
    return lax.ppermute(shard, axis, [(i, to(i, count)) for i in range(count)])


def shift4(i, count):
    return (i + 4) % count


def swap1(i, count):
    return i ^ 1


def swap2(i, count):
    return i ^ 2


def largest_divisor(value, limit):
    return max(d for d in range(1, limit + 1) if value % d == 0)


def features_kernel(slots_ref, x_ref, *refs, steps, tile, pitch):
    *ft_refs, atoms_ref, squares_ref = refs
    step = pl.program_id(0)
    per_step, _, rows, frames = x_ref.shape
    lanes = frames // 8

    @pl.when(step < steps)
    def _():
        def regroup(g, carry):
            for component in range(3):
                for top in range(0, rows, 8):
                    for s in range(8):
                        start = ((step * per_step + g) * rows + top) * 24 + component * 8 + s
                        atoms_ref[pl.ds(start, 8, stride=24), :] = x_ref[
                            g, component, top:top + 8, s * lanes:(s + 1) * lanes]
            return carry

        lax.fori_loop(0, per_step, regroup, 0)

    @pl.when(step >= steps)
    def _():
        base = (step - steps) * tile
        unroll = 16

        def contacts(i, carry):
            for u in range(unroll):
                c = i * unroll + u
                first = slots_ref[0, base + c]
                second = slots_ref[1, base + c]
                squared = None
                for row in (0, 8, 16):
                    offset = (atoms_ref[pl.ds(pl.multiple_of(first + row, 8), 8), :]
                              - atoms_ref[pl.ds(pl.multiple_of(second + row, 8), 8), :])
                    squared = offset * offset if squared is None else squared + offset * offset
                squares_ref[pl.ds(c, 8, stride=pitch), :] = squared
            return carry

        lax.fori_loop(0, tile // unroll, contacts, 0)
        s = 0
        for ft_ref in ft_refs:
            for left in range(0, ft_ref.shape[1], lanes):
                squared = jnp.minimum(squares_ref[s * pitch:s * pitch + tile, :] + 0.01, 1e30)
                separation = squared * lax.rsqrt(squared)
                scale = math.log2(math.e) / 1.5
                feature = 1.0 / (1.0 + jnp.exp2(separation * scale - 8.0 * scale))
                ft_ref[:, left:left + lanes] = feature.astype(jnp.bfloat16)
                s += 1


def features_of(x, slots24, widths):
    groups, _, rows, frames = x.shape
    contacts = slots24.shape[1]
    per_step = largest_divisor(groups, max(1, 160 // rows))
    steps = groups // per_step
    tile = 512
    pitch = tile + 8
    return pl.pallas_call(
        functools.partial(features_kernel, steps=steps, tile=tile, pitch=pitch),
        grid_spec=pltpu.PrefetchScalarGridSpec(
            num_scalar_prefetch=1,
            grid=(steps + contacts // tile,),
            in_specs=[pl.BlockSpec((per_step, 3, rows, frames),
                                   lambda i, s: (jnp.minimum(i, steps - 1), 0, 0, 0))],
            out_specs=[pl.BlockSpec((tile, width), lambda i, s: (jnp.maximum(i - steps, 0), 0))
                       for width in widths],
            scratch_shapes=[
                pltpu.VMEM((groups * rows * 24, frames // 8), jnp.float32),
                pltpu.VMEM((8 * pitch, frames // 8), jnp.float32),
            ],
        ),
        out_shape=[jax.ShapeDtypeStruct((contacts, width), jnp.bfloat16) for width in widths],
        compiler_params=pltpu.CompilerParams(vmem_limit_bytes=VMEM_BYTES),
        name="features",
    )(slots24, x)


def own_kernel(*refs):
    *ft_refs, f_ref, norm_ref = refs

    @pl.when(pl.program_id(0) == 0)
    def _():
        norm_ref[...] = jnp.zeros_like(norm_ref)

    row = 0
    for ft_ref in ft_refs:
        width = ft_ref.shape[1]
        own = ft_ref[...].astype(jnp.float32).T
        f_ref[row:row + width, :] = own.astype(jnp.bfloat16)
        norm_ref[row:row + width, :] += jnp.sum(own * own, axis=1, keepdims=True)
        row += width


def own_features(fts):
    contacts = fts[0].shape[0]
    frames = sum(ft.shape[1] for ft in fts)
    tile = 512
    return pl.pallas_call(
        own_kernel,
        grid=(contacts // tile,),
        in_specs=[pl.BlockSpec((tile, ft.shape[1]), lambda i: (i, 0)) for ft in fts],
        out_specs=[
            pl.BlockSpec((frames, tile), lambda i: (0, i)),
            pl.BlockSpec((frames, 1), lambda i: (0, 0)),
        ],
        out_shape=[
            jax.ShapeDtypeStruct((frames, contacts), jnp.bfloat16),
            jax.ShapeDtypeStruct((frames, 1), jnp.float32),
        ],
        compiler_params=pltpu.CompilerParams(vmem_limit_bytes=VMEM_BYTES),
        name="own_features",
    )(*fts)


def pick_kernel(flag_ref, first_ref, second_ref, *refs):
    out_ref, sem = refs[-2:]

    @pl.when(flag_ref[0] == 1)
    def _():
        pltpu.make_async_copy(first_ref, out_ref, sem).start()

    @pl.when(flag_ref[0] != 1)
    def _():
        pltpu.make_async_copy(second_ref, out_ref, sem).start()

    pltpu.make_async_copy(first_ref, out_ref, sem).wait()


def pick(flag, first, second, after):
    anywhere = pl.BlockSpec(memory_space=pl.ANY)
    return pl.pallas_call(
        pick_kernel,
        in_specs=[pl.BlockSpec(memory_space=pltpu.SMEM)] + [anywhere] * (2 + len(after)),
        out_specs=anywhere,
        out_shape=jax.ShapeDtypeStruct(first.shape, first.dtype),
        scratch_shapes=[pltpu.SemaphoreType.DMA(())],
        name="pick",
    )(flag, first, second, *after)


def pack_kernel(flag_ref, v2_ref, first_ref, second_ref, *refs):
    out_ref, sems = refs[-2:]
    pltpu.make_async_copy(v2_ref, out_ref.at[0], sems.at[0]).start()

    @pl.when(flag_ref[0] == 1)
    def _():
        pltpu.make_async_copy(first_ref, out_ref.at[1], sems.at[1]).start()

    @pl.when(flag_ref[0] != 1)
    def _():
        pltpu.make_async_copy(second_ref, out_ref.at[1], sems.at[1]).start()

    pltpu.make_async_copy(v2_ref, out_ref.at[0], sems.at[0]).wait()
    pltpu.make_async_copy(first_ref, out_ref.at[1], sems.at[1]).wait()


def pack(flag, v2, first, second, after):
    anywhere = pl.BlockSpec(memory_space=pl.ANY)
    return pl.pallas_call(
        pack_kernel,
        in_specs=[pl.BlockSpec(memory_space=pltpu.SMEM)] + [anywhere] * (3 + len(after)),
        out_specs=anywhere,
        out_shape=jax.ShapeDtypeStruct((2,) + first.shape, first.dtype),
        scratch_shapes=[pltpu.SemaphoreType.DMA((2,))],
        name="pack",
    )(flag, v2, first, second, *after)


def distance_kernel(bit_ref, own_ref, norm_ref, v4_ref, v2_ref, vx_ref, *refs, aliased):
    refs = refs[1:] if aliased else refs
    out_ref, token_ref, vnorm_ref = refs
    bit = bit_ref[0]
    visitors = (
        lambda: vx_ref[bit],
        lambda: v2_ref[...],
        lambda: vx_ref[1 - bit],
        lambda: v4_ref[...],
    )

    @pl.when(pl.program_id(0) == 0)
    def _():
        for r, load in enumerate(visitors):
            wide = load().astype(jnp.float32)
            vnorm_ref[r, 0:1, :] = jnp.sum(wide * wide, axis=0, keepdims=True)
        token_ref[...] = jnp.zeros_like(token_ref)

    own = own_ref[...]
    own_norm = norm_ref[...]
    for r, load in enumerate(visitors):
        inter = jnp.dot(own, load(), preferred_element_type=jnp.float32)
        ratio = inter / (own_norm + vnorm_ref[r, 0:1, :] - inter + 1e-06)
        out_ref[r] = (1.0 - ratio).astype(jnp.bfloat16)


def distance_chunk(bit, own, norms, v4, v2, vx, out, start):
    frames, contacts = own.shape
    width = v4.shape[1]
    tile = 256
    block = start // width
    aliased = out is not None
    in_specs = [
        pl.BlockSpec(memory_space=pltpu.SMEM),
        pl.BlockSpec((tile, contacts), lambda i: (i, 0)),
        pl.BlockSpec((tile, 1), lambda i: (i, 0)),
        pl.BlockSpec((contacts, width), lambda i: (0, 0)),
        pl.BlockSpec((contacts, width), lambda i: (0, 0)),
        pl.BlockSpec((2, contacts, width), lambda i: (0, 0, 0)),
    ]
    args = [bit, own, norms, v4, v2, vx]
    if aliased:
        in_specs.append(pl.BlockSpec(memory_space=pl.ANY))
        args.append(out)
    return pl.pallas_call(
        functools.partial(distance_kernel, aliased=aliased),
        grid=(frames // tile,),
        in_specs=in_specs,
        out_specs=[
            pl.BlockSpec((ROUNDS, tile, width), lambda i: (0, i, block)),
            pl.BlockSpec((8, 128), lambda i: (0, 0)),
        ],
        out_shape=[
            jax.ShapeDtypeStruct((ROUNDS, frames, frames), jnp.bfloat16),
            jax.ShapeDtypeStruct((8, 128), jnp.float32),
        ],
        scratch_shapes=[pltpu.VMEM((ROUNDS, 8, width), jnp.float32)],
        input_output_aliases={6: 0} if aliased else {},
        compiler_params=pltpu.CompilerParams(vmem_limit_bytes=VMEM_BYTES),
    )(*args)


def contact_slots(pairs, res_slot):
    hits = pairs[:, :, None] == res_slot[None, None, :]
    places = jnp.arange(res_slot.shape[0], dtype=jnp.int32)
    return jnp.sum(jnp.where(hits, places, 0), axis=2, dtype=jnp.int32)


def exchanged(pieces):
    return lax.all_to_all(pieces, "blocks", split_axis=0, concat_axis=0, tiled=True)


def gathered_coords(coords, count):
    res_local, _, frames = coords.shape
    per_block = frames // count
    blocks = coords.reshape(res_local, 3, count, per_block)
    extent = jnp.max(jnp.abs(coords))
    scaled = 1.0 / per_block
    spread = jnp.sum(blocks * blocks, axis=3) * scaled - (jnp.sum(blocks, axis=3) * scaled) ** 2
    spread = jnp.min(jnp.mean(spread, axis=(0, 1)))
    fine = (extent <= 64.0) & (spread >= 6e-5 * extent * extent)
    pieces = blocks.transpose(2, 1, 0, 3)
    narrow = jnp.where(fine, pieces, jnp.inf).astype(jnp.float16)
    narrow = exchanged(narrow)
    all_fine = jnp.all(narrow[:, 0, 0, 0].astype(jnp.float32) < jnp.inf)
    return lax.cond(all_fine, lambda: narrow.astype(jnp.float32), lambda: exchanged(pieces))


def shards(coords, pairs, res_slot):
    count = lax.axis_size("blocks")
    index = lax.axis_index("blocks")
    res_local, _, frames = coords.shape
    per_block = frames // count
    lanes = per_block // 8
    residues = res_local * count
    widths = [lanes * n for n in (2, 2, 2, 1, 1)]

    arrived = gathered_coords(coords, count)
    if res_local % 8:
        arrived = arrived.transpose(0, 2, 1, 3).reshape(residues // 8, 8, 3, per_block)
        arrived = arrived.transpose(0, 2, 1, 3)
    slots24 = contact_slots(pairs, res_slot) * 24
    fts = features_of(arrived, slots24, widths)
    bit = (index & 1).astype(jnp.int32).reshape(1)
    low_core = 1 - bit
    low_pair = 1 - ((index >> 1) & 1).astype(jnp.int32).reshape(1)

    v4s = []
    for ft in fts:
        v4s.append(permuted(ft, "blocks", shift4))
    own, norms = own_features(fts)
    out = None
    tokens = []
    start = 0
    for j, (ft, v4) in enumerate(zip(fts, v4s)):
        after = tokens[j - 2:j - 1] if j >= 2 else [norms]
        v2 = permuted(pick(low_pair, ft, v4, after), "blocks", swap2)
        vx = permuted(pack(low_core, v2, ft, v4, []), "blocks", swap1)
        out, token = distance_chunk(bit, own, norms, v4, v2, vx, out, start)
        tokens.append(token)
        start += ft.shape[1]
    return out


def solution(mesh):
    in_specs = (P("blocks", None, "parts"), P(), P())
    out_specs = P(None, ("parts", "blocks"), None)
    return jax.shard_map(shards, mesh=mesh, in_specs=in_specs, out_specs=out_specs, check_vma=False)
```

profile of v0, /device:TPU:0, one launch (start us, length us, event | category | flops | bytes accessed | tf_op | source)
XLA Modules:
  0.0 687.9 jit_solution(18340236712531354447)
XLA Ops:
  0.0 4.5 abs_reduce_fusion
  4.5 1.0 copy-done.1
  5.5 6.5 copy.15
  12.0 0.0 copy-start
  12.0 3.2 copy-done
  15.2 1.2 multiply_reduce_fusion
  16.5 0.7 multiply_reduce_fusion.1
  19.8 4.4 select_convert_fusion
  24.2 0.0 copy-start.16
  24.2 0.0 copy-start.17
  24.2 4.3 copy.12
  28.5 7.5 %all-to-all-start.1 = ((f16[16,3,40,1024]{3,2,1,0:T(8,128)(2,1)}), f16[16,3,40,1024]{3,2,1,0:T(8,128)(2,1)}, u32[]{:S(2)}, u32[]{:S(2)}) async-start(f16[16,3,40,1024]{3,2,1,0:T(8,128)(2,1)} %copy.12), calls=%async_computation.1 | async-start | bytes 7864320 | tf_op jit(solution)/shard_map/all_to_all | solution.py:273
  36.0 1.6 select_reduce_fusion
  37.6 0.6 broadcast_multiply_fusion.slots_ref
  38.2 70.7 %all-to-all-done.1 = f16[16,3,40,1024]{3,2,1,0:T(8,128)(2,1)} async-done(((f16[16,3,40,1024]{3,2,1,0:T(8,128)(2,1)}), f16[16,3,40,1024]{3,2,1,0:T(8,128)(2,1)}, u32[]{:S(2)}, u32[]{:S(2)}) %all-to-all-start.1) | async-done | bytes 3932192 | tf_op jit(solution)/shard_map/all_to_all | solution.py:273
  108.9 1.4 compare_reduce_fusion
  111.0 6.2 conditional.1
  111.0 6.2 convert_element_type.9
  117.2 17.9 %features.1 = (bf16[2048,256]{1,0:T(8,128)(2,1)}, bf16[2048,256]{1,0:T(8,128)(2,1)}, bf16[2048,256]{1,0:T(8,128)(2,1)}, bf16[2048,128]{1,0:T(8,128)(2,1)}, bf16[2048,128]{1,0:T(8,128)(2,1)}) custom-call(s32[2,2048]{1,0:T(2,128)} %broadcast_multiply_fusion.slots_ref, f32[16,3,40,1024]{3,2,1,0:T(8,128)} %get-tuple-element.43.x_ref), custom_call_target="tpu_custom_call" | custom-call | tf_op jit(solution)/shard_map/features/pallas_call | solution.py:93
  135.1 14.1 %collective-permute-start.2 = (bf16[2048,256]{1,0:T(8,128)(2,1)}, bf16[2048,256]{1,0:T(8,128)(2,1)S(1)}, u32[]{:S(2)}, u32[]{:S(2)}) collective-permute-start(bf16[2048,256]{1,0:T(8,128)(2,1)} %get-tuple-element.25.refs_0_.first_ref), channel_id=1, source_target_pairs={{0,4},{1,5},{2,6},{3,7},{4,8},{5,9},{6,10},{7,11},{8,12},{9,13},{1... | collective-permute-start | bytes 3145736 | tf_op jit(solution)/shard_map/ppermute | solution.py:18
  149.2 5.9 own_features.1
  155.0 16.6 %collective-permute-done.2.second_ref.v4_ref = bf16[2048,256]{1,0:T(8,128)(2,1)S(1)} collective-permute-done((bf16[2048,256]{1,0:T(8,128)(2,1)}, bf16[2048,256]{1,0:T(8,128)(2,1)S(1)}, u32[]{:S(2)}, u32[]{:S(2)}) %collective-permute-start.2) | collective-permute-done | bytes 1048608 | tf_op jit(solution)/shard_map/ppermute | solution.py:18
  171.6 1.0 copy-done.4
  172.6 32.9 %pick.5 = bf16[2048,256]{1,0:T(8,128)(2,1)} custom-call(s32[1]{0:T(128)} %bitcast.2.flag_ref, bf16[2048,256]{1,0:T(8,128)(2,1)} %get-tuple-element.25.refs_0_.first_ref, bf16[2048,256]{1,0:T(8,128)(2,1)} %copy-done.4, f32[1024,1]{1,0:T(8,128)} %get-tuple-element.31.refs_0_.norm_ref), custom_call_target="tpu_custom_call" | custom-call | tf_op jit(solution)/shard_map/pick/pallas_call | solution.py:166
  205.5 5.3 collective-permute-start.3
  210.7 23.4 %collective-permute-done.3.v2_ref = bf16[2048,256]{1,0:T(8,128)(2,1)S(1)} collective-permute-done((bf16[2048,256]{1,0:T(8,128)(2,1)}, bf16[2048,256]{1,0:T(8,128)(2,1)S(1)}, u32[]{:S(2)}, u32[]{:S(2)}) %collective-permute-start.3) | collective-permute-done | bytes 1048608 | tf_op jit(solution)/shard_map/ppermute | solution.py:18
  234.1 1.0 copy-done.11
  235.1 64.6 %pack.5 = bf16[2,2048,256]{2,1,0:T(8,128)(2,1)} custom-call(s32[1]{0:T(128)S(6)} %sub.14.flag_ref, bf16[2048,256]{1,0:T(8,128)(2,1)} %copy-done.11, bf16[2048,256]{1,0:T(8,128)(2,1)} %get-tuple-element.25.refs_0_.first_ref, bf16[2048,256]{1,0:T(8,128)(2,1)} %copy-done.4), custom_call_target="tpu_custom_call" | custom-call | tf_op jit(solution)/shard_map/pack/pallas_call | solution.py:194
  299.7 0.1 collective-permute-start.4
  299.8 0.7 collective-permute-start.7
  300.5 0.5 collective-permute-start.1
  301.0 26.9 %collective-permute-done.7.second_ref.v4_ref = bf16[2048,256]{1,0:T(8,128)(2,1)S(1)} collective-permute-done((bf16[2048,256]{1,0:T(8,128)(2,1)}, bf16[2048,256]{1,0:T(8,128)(2,1)S(1)}, u32[]{:S(2)}, u32[]{:S(2)}) %collective-permute-start.7) | collective-permute-done | bytes 1048608 | tf_op jit(solution)/shard_map/ppermute | solution.py:18
  327.9 1.0 copy-done.3
  328.9 32.9 %pick.7 = bf16[2048,256]{1,0:T(8,128)(2,1)} custom-call(s32[1]{0:T(128)} %bitcast.2.flag_ref, bf16[2048,256]{1,0:T(8,128)(2,1)} %get-tuple-element.26.refs_1_.first_ref, bf16[2048,256]{1,0:T(8,128)(2,1)} %copy-done.3, f32[1024,1]{1,0:T(8,128)} %get-tuple-element.31.refs_0_.norm_ref), custom_call_target="tpu_custom_call" | custom-call | tf_op jit(solution)/shard_map/pick/pallas_call | solution.py:166
  361.8 1.8 collective-permute-start.8
  363.6 9.0 %shard_map.37 = (bf16[4,1024,1024]{2,1,0:T(8,128)(2,1)}, f32[8,128]{1,0:T(8,128)}) custom-call(s32[1]{0:T(128)} %bitcast.bit_ref, bf16[1024,2048]{1,0:T(8,128)(2,1)} %get-tuple-element.30.own_ref, f32[1024,1]{1,0:T(8,128)} %get-tuple-element.31.refs_0_.norm_ref, bf16[2048,256]{1,0:T(8,128)(2,1)} %copy-done.4, bf16[2048,256]{1,0:T(8,128)(2,1)} %copy-done.11, ...), custom_call_target="tpu_custom_call" | custom-call | tf_op jit(solution)/shard_map/pallas_call | solution.py:248
  372.6 1.0 copy-done.2
  373.6 32.9 %pick.6 = bf16[2048,256]{1,0:T(8,128)(2,1)} custom-call(s32[1]{0:T(128)} %bitcast.2.flag_ref, bf16[2048,256]{1,0:T(8,128)(2,1)} %get-tuple-element.27.refs_2_.first_ref, bf16[2048,256]{1,0:T(8,128)(2,1)} %copy-done.2, f32[8,128]{1,0:T(8,128)} %get-tuple-element.32.refs_0_), custom_call_target="tpu_custom_call" | custom-call | tf_op jit(solution)/shard_map/pick/pallas_call | solution.py:166
  406.5 0.3 collective-permute-start.5
  406.8 64.6 %pack.7 = bf16[2,2048,256]{2,1,0:T(8,128)(2,1)} custom-call(s32[1]{0:T(128)S(6)} %sub.14.flag_ref, bf16[2048,256]{1,0:T(8,128)(2,1)} %collective-permute-done.8.v2_ref, bf16[2048,256]{1,0:T(8,128)(2,1)} %get-tuple-element.26.refs_1_.first_ref, bf16[2048,256]{1,0:T(8,128)(2,1)} %copy-done.3), custom_call_target="tpu_custom_call" | custom-call | tf_op jit(solution)/shard_map/pack/pallas_call | solution.py:194
  471.5 0.1 collective-permute-start.9
  471.6 1.0 copy-done.10
  472.6 64.6 %pack.6 = bf16[2,2048,256]{2,1,0:T(8,128)(2,1)} custom-call(s32[1]{0:T(128)S(6)} %sub.14.flag_ref, bf16[2048,256]{1,0:T(8,128)(2,1)} %copy-done.10, bf16[2048,256]{1,0:T(8,128)(2,1)} %get-tuple-element.27.refs_2_.first_ref, bf16[2048,256]{1,0:T(8,128)(2,1)} %copy-done.2), custom_call_target="tpu_custom_call" | custom-call | tf_op jit(solution)/shard_map/pack/pallas_call | solution.py:194
  537.2 0.6 collective-permute-start.6
  537.8 0.3 collective-permute-start
  538.1 9.1 %shard_map.38 = (bf16[4,1024,1024]{2,1,0:T(8,128)(2,1)}, f32[8,128]{1,0:T(8,128)}) custom-call(s32[1]{0:T(128)} %bitcast.bit_ref, bf16[1024,2048]{1,0:T(8,128)(2,1)} %get-tuple-element.30.own_ref, f32[1024,1]{1,0:T(8,128)} %get-tuple-element.31.refs_0_.norm_ref, bf16[2048,256]{1,0:T(8,128)(2,1)} %copy-done.3, ...), custom_call_target="tpu_custom_call", output_to_operand_aliasing={{0}: (6, {})} | custom-call | tf_op jit(solution)/shard_map/pallas_call | solution.py:248
  547.2 7.2 %collective-permute-done.12.second_ref.v4_ref = bf16[2048,128]{1,0:T(8,128)(2,1)S(1)} collective-permute-done((bf16[2048,128]{1,0:T(8,128)(2,1)S(1)}, bf16[2048,128]{1,0:T(8,128)(2,1)S(1)}, u32[]{:S(2)}, u32[]{:S(2)}) %collective-permute-start.12) | collective-permute-done | bytes 524320 | tf_op jit(solution)/shard_map/ppermute | solution.py:18
  554.4 0.8 copy-done.7
  555.2 17.0 %pick.9 = bf16[2048,128]{1,0:T(8,128)(2,1)} custom-call(s32[1]{0:T(128)} %bitcast.2.flag_ref, bf16[2048,128]{1,0:T(8,128)(2,1)} %get-tuple-element.28.refs_3_.first_ref, bf16[2048,128]{1,0:T(8,128)(2,1)} %copy-done.7, f32[8,128]{1,0:T(8,128)} %get-tuple-element.36.refs_0_), custom_call_target="tpu_custom_call" | custom-call | tf_op jit(solution)/shard_map/pick/pallas_call | solution.py:166
  572.2 1.8 collective-permute-start.13
  574.0 9.0 %shard_map.39 = (bf16[4,1024,1024]{2,1,0:T(8,128)(2,1)}, f32[8,128]{1,0:T(8,128)}) custom-call(s32[1]{0:T(128)} %bitcast.bit_ref, bf16[1024,2048]{1,0:T(8,128)(2,1)} %get-tuple-element.30.own_ref, f32[1024,1]{1,0:T(8,128)} %get-tuple-element.31.refs_0_.norm_ref, bf16[2048,256]{1,0:T(8,128)(2,1)} %copy-done.2, ...), custom_call_target="tpu_custom_call", output_to_operand_aliasing={{0}: (6, {})} | custom-call | tf_op jit(solution)/shard_map/pallas_call | solution.py:248
  583.0 0.8 copy-done.6
  583.8 17.0 %pick.8 = bf16[2048,128]{1,0:T(8,128)(2,1)} custom-call(s32[1]{0:T(128)} %bitcast.2.flag_ref, bf16[2048,128]{1,0:T(8,128)(2,1)} %get-tuple-element.29.refs_4_.first_ref, bf16[2048,128]{1,0:T(8,128)(2,1)} %copy-done.6, f32[8,128]{1,0:T(8,128)} %get-tuple-element.35.refs_0_), custom_call_target="tpu_custom_call" | custom-call | tf_op jit(solution)/shard_map/pick/pallas_call | solution.py:166
  600.8 0.3 collective-permute-start.10
  601.2 0.8 copy-done.12
  602.0 32.9 %pack.9 = bf16[2,2048,128]{2,1,0:T(8,128)(2,1)} custom-call(s32[1]{0:T(128)S(6)} %sub.14.flag_ref, bf16[2048,128]{1,0:T(8,128)(2,1)} %copy-done.12, bf16[2048,128]{1,0:T(8,128)(2,1)} %get-tuple-element.28.refs_3_.first_ref, bf16[2048,128]{1,0:T(8,128)(2,1)} %copy-done.7), custom_call_target="tpu_custom_call" | custom-call | tf_op jit(solution)/shard_map/pack/pallas_call | solution.py:194
  634.9 0.1 collective-permute-start.14
  635.0 0.8 copy-done.13
  635.8 32.9 %pack.8 = bf16[2,2048,128]{2,1,0:T(8,128)(2,1)} custom-call(s32[1]{0:T(128)S(6)} %sub.14.flag_ref, bf16[2048,128]{1,0:T(8,128)(2,1)} %copy-done.13, bf16[2048,128]{1,0:T(8,128)(2,1)} %get-tuple-element.29.refs_4_.first_ref, bf16[2048,128]{1,0:T(8,128)(2,1)} %copy-done.6), custom_call_target="tpu_custom_call" | custom-call | tf_op jit(solution)/shard_map/pack/pallas_call | solution.py:194
  668.7 0.6 collective-permute-start.11
  669.2 1.0 copy-done.15
  670.2 8.3 %shard_map.40 = (bf16[4,1024,1024]{2,1,0:T(8,128)(2,1)}, f32[8,128]{1,0:T(8,128)}) custom-call(s32[1]{0:T(128)} %bitcast.bit_ref, bf16[1024,2048]{1,0:T(8,128)(2,1)} %get-tuple-element.30.own_ref, f32[1024,1]{1,0:T(8,128)} %get-tuple-element.31.refs_0_.norm_ref, bf16[2048,128]{1,0:T(8,128)(2,1)} %copy-done.7, ...), custom_call_target="tpu_custom_call", output_to_operand_aliasing={{0}: (6, {})} | custom-call | tf_op jit(solution)/shard_map/pallas_call | solution.py:248
  678.6 1.0 copy-done.14
  679.6 8.3 %shard_map.41 = (bf16[4,1024,1024]{2,1,0:T(8,128)(2,1)}, f32[8,128]{1,0:T(8,128)}) custom-call(s32[1]{0:T(128)} %bitcast.bit_ref, bf16[1024,2048]{1,0:T(8,128)(2,1)} %get-tuple-element.30.own_ref, f32[1024,1]{1,0:T(8,128)} %get-tuple-element.31.refs_0_.norm_ref, bf16[2048,128]{1,0:T(8,128)(2,1)} %copy-done.6, ...), custom_call_target="tpu_custom_call", output_to_operand_aliasing={{0}: (6, {})} | custom-call | tf_op jit(solution)/shard_map/pallas_call | solution.py:248
  (33 shorter events, 0.1 us)
Async XLA Ops:
  0.0 5.5 copy-start.1
  12.0 3.2 copy-start
  24.2 11.8 %copy-start.16 = (s32[2,2048]{1,0:T(2,128)S(1)}, s32[2,2048]{1,0:T(2,128)}, u32[]{:S(2)}) copy-start(s32[2,2048]{1,0:T(2,128)} %param.6) | copy-start | bytes 49156
  24.2 11.8 %copy-start.17 = (s32[640]{0:T(1024)S(1)}, s32[640]{0:T(1024)}, u32[]{:S(2)}) copy-start(s32[640]{0:T(1024)} %param.7) | copy-start | bytes 7684
  28.5 80.5 %all-to-all-start.1 = ((f16[16,3,40,1024]{3,2,1,0:T(8,128)(2,1)}), f16[16,3,40,1024]{3,2,1,0:T(8,128)(2,1)}, u32[]{:S(2)}, u32[]{:S(2)}) async-start(f16[16,3,40,1024]{3,2,1,0:T(8,128)(2,1)} %copy.12), calls=%async_computation.1 | async-start | bytes 7864320 | tf_op jit(solution)/shard_map/all_to_all | solution.py:273
  135.1 165.4 %copy-start.5 = (bf16[2048,256]{1,0:T(8,128)(2,1)S(1)}, bf16[2048,256]{1,0:T(8,128)(2,1)}, u32[]{:S(2)}) copy-start(bf16[2048,256]{1,0:T(8,128)(2,1)} %get-tuple-element.27.refs_2_.first_ref) | copy-start | bytes 3145732
  135.1 36.5 %collective-permute-start.2 = (bf16[2048,256]{1,0:T(8,128)(2,1)}, bf16[2048,256]{1,0:T(8,128)(2,1)S(1)}, u32[]{:S(2)}, u32[]{:S(2)}) collective-permute-start(bf16[2048,256]{1,0:T(8,128)(2,1)} %get-tuple-element.25.refs_0_.first_ref), channel_id=1, source_target_pairs={{0,4},{1,5},{2,6},{3,7},{4,8},{5,9},{6,10},{7,11},{8,12},{9,13},{1... | collective-permute-start | bytes 3145736 | tf_op jit(solution)/shard_map/ppermute | solution.py:18
  171.6 1.0 copy-start.4
  205.5 28.6 %collective-permute-start.3 = (bf16[2048,256]{1,0:T(8,128)(2,1)}, bf16[2048,256]{1,0:T(8,128)(2,1)S(1)}, u32[]{:S(2)}, u32[]{:S(2)}) collective-permute-start(bf16[2048,256]{1,0:T(8,128)(2,1)} %pick.5), channel_id=1, source_target_pairs={{0,2},{1,3},{2,0},{3,1},{4,6},{5,7},{6,4},{7,5},{8,10},{9,11},{10,... | collective-permute-start | bytes 3145736 | tf_op jit(solution)/shard_map/ppermute | solution.py:18
  234.1 1.0 copy-start.11
  299.7 63.9 %collective-permute-start.4 = (bf16[2,2048,256]{2,1,0:T(8,128)(2,1)}, bf16[2,2048,256]{2,1,0:T(8,128)(2,1)}, u32[]{:S(2)}, u32[]{:S(2)}) collective-permute-start(bf16[2,2048,256]{2,1,0:T(8,128)(2,1)} %pack.5), channel_id=1, source_target_pairs={{0,1},{1,0},{2,3},{3,2},{4,5},{5,4},{6,7},{7,6},{8,9},{9,8},{10,11... | collective-permute-start | bytes 6291464 | tf_op jit(solution)/shard_map/ppermute | solution.py:18
  299.8 28.1 %collective-permute-start.7 = (bf16[2048,256]{1,0:T(8,128)(2,1)}, bf16[2048,256]{1,0:T(8,128)(2,1)S(1)}, u32[]{:S(2)}, u32[]{:S(2)}) collective-permute-start(bf16[2048,256]{1,0:T(8,128)(2,1)} %get-tuple-element.26.refs_1_.first_ref), channel_id=1, source_target_pairs={{0,4},{1,5},{2,6},{3,7},{4,8},{5,9},{6,10},{7,11},{8,12},{9,13},{1... | collective-permute-start | bytes 3145736 | tf_op jit(solution)/shard_map/ppermute | solution.py:18
  300.5 72.1 %collective-permute-start.1 = (bf16[2048,256]{1,0:T(8,128)(2,1)S(1)}, bf16[2048,256]{1,0:T(8,128)(2,1)S(1)}, u32[]{:S(2)}, u32[]{:S(2)}) collective-permute-start(bf16[2048,256]{1,0:T(8,128)(2,1)S(1)} %copy-done.5), channel_id=1, source_target_pairs={{0,4},{1,5},{2,6},{3,7},{4,8},{5,9},{6,10},{7,11},{8,12},{9,13},{1... | collective-permute-start | bytes 3145736 | tf_op jit(solution)/shard_map/ppermute | solution.py:18
  327.9 1.0 copy-start.3
  361.8 45.1 %collective-permute-start.8 = (bf16[2048,256]{1,0:T(8,128)(2,1)}, bf16[2048,256]{1,0:T(8,128)(2,1)}, u32[]{:S(2)}, u32[]{:S(2)}) collective-permute-start(bf16[2048,256]{1,0:T(8,128)(2,1)} %pick.7), channel_id=1, source_target_pairs={{0,2},{1,3},{2,0},{3,1},{4,6},{5,7},{6,4},{7,5},{8,10},{9,11},{10,... | collective-permute-start | bytes 3145736 | tf_op jit(solution)/shard_map/ppermute | solution.py:18
  372.6 165.2 %copy-start.9 = (bf16[2048,128]{1,0:T(8,128)(2,1)S(1)}, bf16[2048,128]{1,0:T(8,128)(2,1)}, u32[]{:S(2)}) copy-start(bf16[2048,128]{1,0:T(8,128)(2,1)} %get-tuple-element.28.refs_3_.first_ref) | copy-start | bytes 1572868
  372.6 165.2 %copy-start.8 = (bf16[2048,128]{1,0:T(8,128)(2,1)S(1)}, bf16[2048,128]{1,0:T(8,128)(2,1)}, u32[]{:S(2)}) copy-start(bf16[2048,128]{1,0:T(8,128)(2,1)} %get-tuple-element.29.refs_4_.first_ref) | copy-start | bytes 1572868
  372.6 1.0 copy-start.2
  406.5 65.1 %collective-permute-start.5 = (bf16[2048,256]{1,0:T(8,128)(2,1)}, bf16[2048,256]{1,0:T(8,128)(2,1)S(1)}, u32[]{:S(2)}, u32[]{:S(2)}) collective-permute-start(bf16[2048,256]{1,0:T(8,128)(2,1)} %pick.6), channel_id=1, source_target_pairs={{0,2},{1,3},{2,0},{3,1},{4,6},{5,7},{6,4},{7,5},{8,10},{9,11},{10,... | collective-permute-start | bytes 3145736 | tf_op jit(solution)/shard_map/ppermute | solution.py:18
  471.5 66.6 %collective-permute-start.9 = (bf16[2,2048,256]{2,1,0:T(8,128)(2,1)}, bf16[2,2048,256]{2,1,0:T(8,128)(2,1)}, u32[]{:S(2)}, u32[]{:S(2)}) collective-permute-start(bf16[2,2048,256]{2,1,0:T(8,128)(2,1)} %pack.7), channel_id=1, source_target_pairs={{0,1},{1,0},{2,3},{3,2},{4,5},{5,4},{6,7},{7,6},{8,9},{9,8},{10,11... | collective-permute-start | bytes 6291464 | tf_op jit(solution)/shard_map/ppermute | solution.py:18
  471.6 1.0 copy-start.10
  537.2 36.8 %collective-permute-start.6 = (bf16[2,2048,256]{2,1,0:T(8,128)(2,1)}, bf16[2,2048,256]{2,1,0:T(8,128)(2,1)}, u32[]{:S(2)}, u32[]{:S(2)}) collective-permute-start(bf16[2,2048,256]{2,1,0:T(8,128)(2,1)} %pack.6), channel_id=1, source_target_pairs={{0,1},{1,0},{2,3},{3,2},{4,5},{5,4},{6,7},{7,6},{8,9},{9,8},{10,11... | collective-permute-start | bytes 6291464 | tf_op jit(solution)/shard_map/ppermute | solution.py:18
  537.8 16.6 %collective-permute-start.12 = (bf16[2048,128]{1,0:T(8,128)(2,1)S(1)}, bf16[2048,128]{1,0:T(8,128)(2,1)S(1)}, u32[]{:S(2)}, u32[]{:S(2)}) collective-permute-start(bf16[2048,128]{1,0:T(8,128)(2,1)S(1)} %copy-done.9), channel_id=1, source_target_pairs={{0,4},{1,5},{2,6},{3,7},{4,8},{5,9},{6,10},{7,11},{8,12},{9,13},{1... | collective-permute-start | bytes 1572872 | tf_op jit(solution)/shard_map/ppermute | solution.py:18
  537.8 45.2 %collective-permute-start = (bf16[2048,128]{1,0:T(8,128)(2,1)S(1)}, bf16[2048,128]{1,0:T(8,128)(2,1)S(1)}, u32[]{:S(2)}, u32[]{:S(2)}) collective-permute-start(bf16[2048,128]{1,0:T(8,128)(2,1)S(1)} %copy-done.8), channel_id=1, source_target_pairs={{0,4},{1,5},{2,6},{3,7},{4,8},{5,9},{6,10},{7,11},{8,12},{9,13},{1... | collective-permute-start | bytes 1572872 | tf_op jit(solution)/shard_map/ppermute | solution.py:18
  554.4 0.8 copy-start.7
  572.2 29.0 %collective-permute-start.13 = (bf16[2048,128]{1,0:T(8,128)(2,1)}, bf16[2048,128]{1,0:T(8,128)(2,1)S(1)}, u32[]{:S(2)}, u32[]{:S(2)}) collective-permute-start(bf16[2048,128]{1,0:T(8,128)(2,1)} %pick.9), channel_id=1, source_target_pairs={{0,2},{1,3},{2,0},{3,1},{4,6},{5,7},{6,4},{7,5},{8,10},{9,11},{10,... | collective-permute-start | bytes 1572872 | tf_op jit(solution)/shard_map/ppermute | solution.py:18
  583.0 0.8 copy-start.6
  600.8 34.1 %collective-permute-start.10 = (bf16[2048,128]{1,0:T(8,128)(2,1)}, bf16[2048,128]{1,0:T(8,128)(2,1)S(1)}, u32[]{:S(2)}, u32[]{:S(2)}) collective-permute-start(bf16[2048,128]{1,0:T(8,128)(2,1)} %pick.8), channel_id=1, source_target_pairs={{0,2},{1,3},{2,0},{3,1},{4,6},{5,7},{6,4},{7,5},{8,10},{9,11},{10,... | collective-permute-start | bytes 1572872 | tf_op jit(solution)/shard_map/ppermute | solution.py:18
  601.2 0.8 copy-start.12
  634.9 34.4 %collective-permute-start.14 = (bf16[2,2048,128]{2,1,0:T(8,128)(2,1)}, bf16[2,2048,128]{2,1,0:T(8,128)(2,1)S(1)}, u32[]{:S(2)}, u32[]{:S(2)}) collective-permute-start(bf16[2,2048,128]{2,1,0:T(8,128)(2,1)} %pack.9), channel_id=1, source_target_pairs={{0,1},{1,0},{2,3},{3,2},{4,5},{5,4},{6,7},{7,6},{8,9},{9,8},{10,11... | collective-permute-start | bytes 3145736 | tf_op jit(solution)/shard_map/ppermute | solution.py:18
  635.0 0.8 copy-start.13
  668.7 9.9 %collective-permute-start.11 = (bf16[2,2048,128]{2,1,0:T(8,128)(2,1)}, bf16[2,2048,128]{2,1,0:T(8,128)(2,1)S(1)}, u32[]{:S(2)}, u32[]{:S(2)}) collective-permute-start(bf16[2,2048,128]{2,1,0:T(8,128)(2,1)} %pack.8), channel_id=1, source_target_pairs={{0,1},{1,0},{2,3},{3,2},{4,5},{5,4},{6,7},{7,6},{8,9},{9,8},{10,11... | collective-permute-start | bytes 3145736 | tf_op jit(solution)/shard_map/ppermute | solution.py:18
  669.2 1.0 copy-start.15
  678.5 1.0 copy-start.14
where the time goes:
time: 689 us; the launch traced here: 688 us
  Pallas kernels  460 us (67%)
  waiting for transfers between devices  145 us (21%)
  starting transfers between devices  33.9 us (5%)
  local copies, waits for them, and re-layouts  25.1 us (4%)
  other arithmetic  20.7 us (3%)
    pallas_call x5, Pallas kernels, pack(): pl.pallas_call(pack_kernel, in_specs=[pl.BlockSpec(memory_space=pltpu.SME...  260 us
    pallas_call x5, Pallas kernels, pick(): pl.pallas_call(pick_kernel, in_specs=[pl.BlockSpec(memory_space=pltpu.SME...  133 us
    ppermute x15, waiting for transfers between devices, permuted(): return lax.ppermute(shard, axis, [(i, to(i, count)) for i in range(count)])  74.1 us
    all_to_all x1, waiting for transfers between devices, exchanged(): lax.all_to_all(pieces, 'blocks', split_axis=0, concat_axis=0, tiled=True)  70.7 us
    pallas_call x5, Pallas kernels, distance_chunk(): pl.pallas_call(functools.partial(distance_kernel, aliased=aliased), grid=...  43.8 us
    ppermute x15, starting transfers between devices, permuted(): return lax.ppermute(shard, axis, [(i, to(i, count)) for i in range(count)])  26.4 us
    unnamed x37, local copies, waits for them, and re-layouts  20.9 us
    pallas_call x1, Pallas kernels, features_of(): pl.pallas_call(functools.partial(features_kernel, steps=steps, tile=tile,...  17.9 us
  transfers between devices with their start and end apart: 16, of which 5 were waited for; matrix products, arithmetic and copies ran while one was open for 0% of the time, Pallas kernels for 49%

commit v1 on v0

--- a/solution.py
+++ b/solution.py
@@ -148,17 +148,28 @@
 
 
 def pick_kernel(flag_ref, first_ref, second_ref, *refs):
-    out_ref, sem = refs[-2:]
+    out_ref, rows_ref, in_sems, out_sems = refs[-4:]
+    parts = in_sems.shape[0]
+    size = rows_ref.shape[0] // parts
+    spans = [pl.ds(k * size, size) for k in range(parts)]
+
+    def fetch(source_ref):
+        for k, span in enumerate(spans):
+            pltpu.make_async_copy(source_ref.at[span], rows_ref.at[span], in_sems.at[k]).start()
 
     @pl.when(flag_ref[0] == 1)
     def _():
-        pltpu.make_async_copy(first_ref, out_ref, sem).start()
+        fetch(first_ref)
 
     @pl.when(flag_ref[0] != 1)
     def _():
-        pltpu.make_async_copy(second_ref, out_ref, sem).start()
-
-    pltpu.make_async_copy(first_ref, out_ref, sem).wait()
+        fetch(second_ref)
+
+    for k, span in enumerate(spans):
+        pltpu.make_async_copy(first_ref.at[span], rows_ref.at[span], in_sems.at[k]).wait()
+        pltpu.make_async_copy(rows_ref.at[span], out_ref.at[span], out_sems.at[k]).start()
+    for k, span in enumerate(spans):
+        pltpu.make_async_copy(rows_ref.at[span], out_ref.at[span], out_sems.at[k]).wait()
 
 
 def pick(flag, first, second, after):
@@ -168,47 +179,20 @@
         in_specs=[pl.BlockSpec(memory_space=pltpu.SMEM)] + [anywhere] * (2 + len(after)),
         out_specs=anywhere,
         out_shape=jax.ShapeDtypeStruct(first.shape, first.dtype),
-        scratch_shapes=[pltpu.SemaphoreType.DMA(())],
+        scratch_shapes=[pltpu.VMEM(first.shape, first.dtype), pltpu.SemaphoreType.DMA((4,)),
+                        pltpu.SemaphoreType.DMA((4,))],
         name="pick",
     )(flag, first, second, *after)
 
 
-def pack_kernel(flag_ref, v2_ref, first_ref, second_ref, *refs):
-    out_ref, sems = refs[-2:]
-    pltpu.make_async_copy(v2_ref, out_ref.at[0], sems.at[0]).start()
-
-    @pl.when(flag_ref[0] == 1)
-    def _():
-        pltpu.make_async_copy(first_ref, out_ref.at[1], sems.at[1]).start()
-
-    @pl.when(flag_ref[0] != 1)
-    def _():
-        pltpu.make_async_copy(second_ref, out_ref.at[1], sems.at[1]).start()
-
-    pltpu.make_async_copy(v2_ref, out_ref.at[0], sems.at[0]).wait()
-    pltpu.make_async_copy(first_ref, out_ref.at[1], sems.at[1]).wait()
-
-
-def pack(flag, v2, first, second, after):
-    anywhere = pl.BlockSpec(memory_space=pl.ANY)
-    return pl.pallas_call(
-        pack_kernel,
-        in_specs=[pl.BlockSpec(memory_space=pltpu.SMEM)] + [anywhere] * (3 + len(after)),
-        out_specs=anywhere,
-        out_shape=jax.ShapeDtypeStruct((2,) + first.shape, first.dtype),
-        scratch_shapes=[pltpu.SemaphoreType.DMA((2,))],
-        name="pack",
-    )(flag, v2, first, second, *after)
-
-
-def distance_kernel(bit_ref, own_ref, norm_ref, v4_ref, v2_ref, vx_ref, *refs, aliased):
+def distance_kernel(bit_ref, own_ref, norm_ref, v4_ref, v2_ref, vx_ref, vy_ref, *refs, aliased):
     refs = refs[1:] if aliased else refs
     out_ref, token_ref, vnorm_ref = refs
-    bit = bit_ref[0]
+    high_core = bit_ref[0] == 1
     visitors = (
-        lambda: vx_ref[bit],
+        lambda: jnp.where(high_core, vy_ref[...], vx_ref[...]),
         lambda: v2_ref[...],
-        lambda: vx_ref[1 - bit],
+        lambda: jnp.where(high_core, vx_ref[...], vy_ref[...]),
         lambda: v4_ref[...],
     )
 
@@ -227,7 +211,7 @@
         out_ref[r] = (1.0 - ratio).astype(jnp.bfloat16)
 
 
-def distance_chunk(bit, own, norms, v4, v2, vx, out, start):
+def distance_chunk(bit, own, norms, v4, v2, vx, vy, out, start):
     frames, contacts = own.shape
     width = v4.shape[1]
     tile = 256
@@ -237,11 +221,8 @@
         pl.BlockSpec(memory_space=pltpu.SMEM),
         pl.BlockSpec((tile, contacts), lambda i: (i, 0)),
         pl.BlockSpec((tile, 1), lambda i: (i, 0)),
-        pl.BlockSpec((contacts, width), lambda i: (0, 0)),
-        pl.BlockSpec((contacts, width), lambda i: (0, 0)),
-        pl.BlockSpec((2, contacts, width), lambda i: (0, 0, 0)),
-    ]
-    args = [bit, own, norms, v4, v2, vx]
+    ] + [pl.BlockSpec((contacts, width), lambda i: (0, 0))] * 4
+    args = [bit, own, norms, v4, v2, vx, vy]
     if aliased:
         in_specs.append(pl.BlockSpec(memory_space=pl.ANY))
         args.append(out)
@@ -258,7 +239,7 @@
             jax.ShapeDtypeStruct((8, 128), jnp.float32),
         ],
         scratch_shapes=[pltpu.VMEM((ROUNDS, 8, width), jnp.float32)],
-        input_output_aliases={6: 0} if aliased else {},
+        input_output_aliases={7: 0} if aliased else {},
         compiler_params=pltpu.CompilerParams(vmem_limit_bytes=VMEM_BYTES),
     )(*args)
 
@@ -269,22 +250,60 @@
     return jnp.sum(jnp.where(hits, places, 0), axis=2, dtype=jnp.int32)
 
 
+def split_kernel(x_ref, pieces_ref, fine_ref, extent_ref, spread_ref):
+    step = pl.program_id(0)
+    count, _, _, frames = pieces_ref.shape
+
+    @pl.when(step == 0)
+    def _():
+        extent_ref[...] = jnp.zeros_like(extent_ref)
+        spread_ref[...] = jnp.full_like(spread_ref, jnp.inf)
+
+    for k in range(count):
+        x = x_ref[:, :, k * frames:(k + 1) * frames]
+        pieces_ref[k] = x
+        extent_ref[...] = jnp.maximum(extent_ref[...], jnp.max(jnp.abs(x), axis=(0, 2), keepdims=True)[0])
+        mean = jnp.sum(x, axis=2, keepdims=True) * (1.0 / frames)
+        square = jnp.sum(x * x, axis=2, keepdims=True) * (1.0 / frames)
+        spread = jnp.mean(square - mean * mean, axis=(0, 1), keepdims=True)[0]
+        spread_ref[...] = jnp.minimum(spread_ref[...], spread)
+
+    @pl.when(step == pl.num_programs(0) - 1)
+    def _():
+        extent = jnp.max(extent_ref[...], axis=0, keepdims=True)
+        fine = (extent <= 64.0) & (spread_ref[...] >= 6e-5 * extent * extent)
+        fine_ref[...] = jnp.where(fine, 1.0, 0.0)
+
+
+def split_blocks(coords, count):
+    _, rows, frames = coords.shape
+    per_block = frames // count
+    per_step = 2 if count % 2 == 0 else 1
+    return pl.pallas_call(
+        split_kernel,
+        grid=(count // per_step,),
+        in_specs=[pl.BlockSpec((3, rows, per_step * per_block), lambda i: (0, 0, i))],
+        out_specs=[
+            pl.BlockSpec((per_step, 3, rows, per_block), lambda i: (i, 0, 0, 0)),
+            pl.BlockSpec((1, 1), lambda i: (0, 0)),
+        ],
+        out_shape=[
+            jax.ShapeDtypeStruct((count, 3, rows, per_block), jnp.float32),
+            jax.ShapeDtypeStruct((1, 1), jnp.float32),
+        ],
+        scratch_shapes=[pltpu.VMEM((rows, 1), jnp.float32), pltpu.VMEM((1, 1), jnp.float32)],
+        compiler_params=pltpu.CompilerParams(vmem_limit_bytes=VMEM_BYTES),
+        name="split_blocks",
+    )(coords)
+
+
 def exchanged(pieces):
     return lax.all_to_all(pieces, "blocks", split_axis=0, concat_axis=0, tiled=True)
 
 
 def gathered_coords(coords, count):
-    res_local, _, frames = coords.shape
-    per_block = frames // count
-    blocks = coords.reshape(res_local, 3, count, per_block)
-    extent = jnp.max(jnp.abs(coords))
-    scaled = 1.0 / per_block
-    spread = jnp.sum(blocks * blocks, axis=3) * scaled - (jnp.sum(blocks, axis=3) * scaled) ** 2
-    spread = jnp.min(jnp.mean(spread, axis=(0, 1)))
-    fine = (extent <= 64.0) & (spread >= 6e-5 * extent * extent)
-    pieces = blocks.transpose(2, 1, 0, 3)
-    narrow = jnp.where(fine, pieces, jnp.inf).astype(jnp.float16)
-    narrow = exchanged(narrow)
+    pieces, fine = split_blocks(coords.transpose(1, 0, 2), count)
+    narrow = exchanged(jnp.where(fine[0, 0] > 0.5, pieces, jnp.inf).astype(jnp.float16))
     all_fine = jnp.all(narrow[:, 0, 0, 0].astype(jnp.float32) < jnp.inf)
     return lax.cond(all_fine, lambda: narrow.astype(jnp.float32), lambda: exchanged(pieces))
 
@@ -318,8 +337,9 @@
     for j, (ft, v4) in enumerate(zip(fts, v4s)):
         after = tokens[j - 2:j - 1] if j >= 2 else [norms]
         v2 = permuted(pick(low_pair, ft, v4, after), "blocks", swap2)
-        vx = permuted(pack(low_core, v2, ft, v4, []), "blocks", swap1)
-        out, token = distance_chunk(bit, own, norms, v4, v2, vx, out, start)
+        vx = permuted(v2, "blocks", swap1)
+        vy = permuted(pick(low_core, ft, v4, []), "blocks", swap1)
+        out, token = distance_chunk(bit, own, norms, v4, v2, vx, vy, out, start)
         tokens.append(token)
         start += ft.shape[1]
     return out

time: 689 us -> 312 us (0.45)
  Pallas kernels: 460 us -> 96.5 us
  local copies, waits for them, and re-layouts: 25.1 us -> 6.58 us
  waiting for transfers between devices: 145 us -> 156 us
    pallas_call x5 -> x1, Pallas kernels: 260 us -> 9.32 us  [split_blocks(): pl.pallas_call(split_kernel, grid=(count // per_step,), in_specs=[pl.Bloc...]
    pallas_call x5 -> x10, Pallas kernels: 133 us -> 19.3 us  [pick(): pl.pallas_call(pick_kernel, in_specs=[pl.BlockSpec(memory_space=pltpu.SME...]
    unnamed x37 -> x34, local copies, waits for them, and re-layouts: 20.9 us -> 6.58 us
    ppermute x15 -> x20, waiting for transfers between devices: 74.1 us -> 85.1 us  [permuted(): return lax.ppermute(shard, axis, [(i, to(i, count)) for i in range(count)])]
    ppermute x15 -> x20, starting transfers between devices: 26.4 us -> 27.2 us  [permuted(): return lax.ppermute(shard, axis, [(i, to(i, count)) for i in range(count)])]
  transfers between devices with their start and end apart: 16 -> 21, of which waited for: 5 -> 8; matrix products, arithmetic and copies ran while one was open for 0% -> 1% of each run, Pallas kernels for 49% -> 19%
where the time goes in v1:
time: 312 us; the launch traced here: 311 us
  waiting for transfers between devices  156 us (50%)
  Pallas kernels  96.5 us (31%)
  starting transfers between devices  34.6 us (11%)
  other arithmetic  16.2 us (5%)
  local copies, waits for them, and re-layouts  6.58 us (2%)
    ppermute x20, waiting for transfers between devices, permuted(): return lax.ppermute(shard, axis, [(i, to(i, count)) for i in range(count)])  85.1 us
    all_to_all x1, waiting for transfers between devices, exchanged(): lax.all_to_all(pieces, 'blocks', split_axis=0, concat_axis=0, tiled=True)  70.7 us
    pallas_call x5, Pallas kernels, distance_chunk(): pl.pallas_call(functools.partial(distance_kernel, aliased=aliased), grid=...  44.2 us
    ppermute x20, starting transfers between devices, permuted(): return lax.ppermute(shard, axis, [(i, to(i, count)) for i in range(count)])  27.2 us
    pallas_call x10, Pallas kernels, pick(): pl.pallas_call(pick_kernel, in_specs=[pl.BlockSpec(memory_space=pltpu.SME...  19.3 us
    pallas_call x1, Pallas kernels, features_of(): pl.pallas_call(functools.partial(features_kernel, steps=steps, tile=tile,...  17.9 us
    pallas_call x1, Pallas kernels, split_blocks(): pl.pallas_call(split_kernel, grid=(count // per_step,), in_specs=[pl.Bloc...  9.32 us
    all_to_all x1, starting transfers between devices, exchanged(): lax.all_to_all(pieces, 'blocks', split_axis=0, concat_axis=0, tiled=True)  7.46 us
  transfers between devices with their start and end apart: 21, of which 8 were waited for; matrix products, arithmetic and copies ran while one was open for 1% of the time, Pallas kernels for 19%

profile of v1, /device:TPU:0, one launch (start us, length us, event | category | flops | bytes accessed | tf_op | source)
XLA Modules:
  0.0 311.2 jit_solution(13617599850597518937)
XLA Ops:
  0.0 9.3 %split_blocks.1 = (f32[16,3,40,1024]{3,2,1,0:T(8,128)}, f32[1,1]{1,0:T(1,128)}) custom-call(f32[3,40,16384]{2,1,0:T(8,128)} %bitcast.4), custom_call_target="tpu_custom_call" | custom-call | tf_op jit(solution)/shard_map/split_blocks/pallas_call | solution.py:282
  9.9 0.0 copy-start.15
  9.9 0.0 copy-start.16
  9.9 6.3 %select_convert_fusion = f16[16,3,40,1024]{3,2,1,0:T(8,128)(2,1)} fusion(f32[16,3,40,1024]{3,2,1,0:T(8,128)} %get-tuple-element.28, pred[]{:T(512)} %bitcast.2), kind=kLoop, calls=%fused_computation.1 | loop fusion | flops 3932160 | bytes 11796481 | tf_op jit(solution)/shard_map/convert_element_type | solution.py:306
  16.2 7.5 %all-to-all-start.1 = ((f16[16,3,40,1024]{3,2,1,0:T(8,128)(2,1)}), f16[16,3,40,1024]{3,2,1,0:T(8,128)(2,1)}, u32[]{:S(2)}, u32[]{:S(2)}) async-start(f16[16,3,40,1024]{3,2,1,0:T(8,128)(2,1)} %select_convert_fusion), calls=%async_computation.1 | async-start | bytes 7864320 | tf_op jit(solution)/shard_map/all_to_all | solution.py:301
  23.7 1.6 select_reduce_fusion
  25.3 0.6 broadcast_multiply_fusion.slots_ref
  26.0 70.7 %all-to-all-done.1 = f16[16,3,40,1024]{3,2,1,0:T(8,128)(2,1)} async-done(((f16[16,3,40,1024]{3,2,1,0:T(8,128)(2,1)}), f16[16,3,40,1024]{3,2,1,0:T(8,128)(2,1)}, u32[]{:S(2)}, u32[]{:S(2)}) %all-to-all-start.1) | async-done | bytes 3932192 | tf_op jit(solution)/shard_map/all_to_all | solution.py:301
  96.7 1.4 compare_reduce_fusion
  98.7 6.2 %conditional.1 = (f32[16,3,40,1024]{3,2,1,0:T(8,128)}) conditional(s32[]{:T(128)} %convert_element_type.15, f32[16,3,40,1024]{3,2,1,0:T(8,128)} %get-tuple-element.28, f16[16,3,40,1024]{3,2,1,0:T(8,128)(2,1)} %all-to-all-done.1), branch_computations={%region_2.3_spmd, %region_3.4_spmd} | conditional | flops 1966080 | bytes 15728648 | solution.py:308
  98.7 6.2 %convert_element_type.9 = f32[16,3,40,1024]{3,2,1,0:T(8,128)} convert(f16[16,3,40,1024]{3,2,1,0:T(8,128)(2,1)} %param.1) | non-fusion elementwise | flops 1966080 | bytes 11796480 | tf_op jit(solution)/shard_map/cond/branch_1_fun/convert_element_type | solution.py:308
  104.9 17.9 %features.1 = (bf16[2048,256]{1,0:T(8,128)(2,1)}, bf16[2048,256]{1,0:T(8,128)(2,1)}, bf16[2048,256]{1,0:T(8,128)(2,1)}, bf16[2048,128]{1,0:T(8,128)(2,1)}, bf16[2048,128]{1,0:T(8,128)(2,1)}) custom-call(s32[2,2048]{1,0:T(2,128)} %broadcast_multiply_fusion.slots_ref, f32[16,3,40,1024]{3,2,1,0:T(8,128)} %get-tuple-element.44.x_ref), custom_call_target="tpu_custom_call" | custom-call | tf_op jit(solution)/shard_map/features/pallas_call | solution.py:93
  122.8 14.1 %collective-permute-start.2 = (bf16[2048,256]{1,0:T(8,128)(2,1)}, bf16[2048,256]{1,0:T(8,128)(2,1)S(1)}, u32[]{:S(2)}, u32[]{:S(2)}) collective-permute-start(bf16[2048,256]{1,0:T(8,128)(2,1)} %get-tuple-element.29.refs_0_.first_ref), channel_id=1, source_target_pairs={{0,4},{1,5},{2,6},{3,7},{4,8},{5,9},{6,10},{7,11},{8,12},{9,13},{1... | collective-permute-start | bytes 3145736 | tf_op jit(solution)/shard_map/ppermute | solution.py:18
  136.9 5.8 %own_features.1 = (bf16[1024,2048]{1,0:T(8,128)(2,1)}, f32[1024,1]{1,0:T(8,128)}) custom-call(bf16[2048,256]{1,0:T(8,128)(2,1)} %get-tuple-element.29.refs_0_.first_ref, bf16[2048,256]{1,0:T(8,128)(2,1)} %get-tuple-element.30.refs_1_.first_ref, bf16[2048,256]{1,0:T(8,128)(2,1)} %get-tuple-element.31.refs_2_.first_ref, ...), custom_call_target="tpu_custom_call" | custom-call | tf_op jit(solution)/shard_map/own_features/pallas_call | solution.py:133
  142.7 16.6 %collective-permute-done.2.second_ref.v4_ref = bf16[2048,256]{1,0:T(8,128)(2,1)S(1)} collective-permute-done((bf16[2048,256]{1,0:T(8,128)(2,1)}, bf16[2048,256]{1,0:T(8,128)(2,1)S(1)}, u32[]{:S(2)}, u32[]{:S(2)}) %collective-permute-start.2) | collective-permute-done | bytes 1048608 | tf_op jit(solution)/shard_map/ppermute | solution.py:18
  159.3 1.0 copy-done.2
  160.3 2.0 pick.10
  162.3 5.3 %collective-permute-start.3 = (bf16[2048,256]{1,0:T(8,128)(2,1)}, bf16[2048,256]{1,0:T(8,128)(2,1)}, u32[]{:S(2)}, u32[]{:S(2)}) collective-permute-start(bf16[2048,256]{1,0:T(8,128)(2,1)} %pick.10), channel_id=1, source_target_pairs={{0,2},{1,3},{2,0},{3,1},{4,6},{5,7},{6,4},{7,5},{8,10},{9,11},{10,... | collective-permute-start | bytes 3145736 | tf_op jit(solution)/shard_map/ppermute | solution.py:18
  167.6 0.9 collective-permute-start.9
  168.5 2.0 pick.11
  170.5 0.1 collective-permute-start.5
  170.6 20.5 %collective-permute-done.3.v2_ref = bf16[2048,256]{1,0:T(8,128)(2,1)} collective-permute-done((bf16[2048,256]{1,0:T(8,128)(2,1)}, bf16[2048,256]{1,0:T(8,128)(2,1)}, u32[]{:S(2)}, u32[]{:S(2)}) %collective-permute-start.3) | collective-permute-done | bytes 1048608 | tf_op jit(solution)/shard_map/ppermute | solution.py:18
  191.1 0.0 collective-permute-start.4
  191.1 0.6 collective-permute-start.1
  191.7 2.5 collective-permute-done.9.second_ref.v4_ref
  194.2 1.0 copy-done.1
  195.2 2.0 pick.14
  197.2 0.4 collective-permute-start.10
  197.6 0.0 collective-permute-done.5.vy_ref
  197.6 0.0 collective-permute-done.4.vx_ref
  197.7 9.1 %shard_map.37 = (bf16[4,1024,1024]{2,1,0:T(8,128)(2,1)}, f32[8,128]{1,0:T(8,128)}) custom-call(s32[1]{0:T(128)} %bitcast.bit_ref, bf16[1024,2048]{1,0:T(8,128)(2,1)} %get-tuple-element.34.own_ref, f32[1024,1]{1,0:T(8,128)} %get-tuple-element.35.refs_0_.norm_ref, bf16[2048,256]{1,0:T(8,128)(2,1)} %copy-done.2, ...), custom_call_target="tpu_custom_call" | custom-call | tf_op jit(solution)/shard_map/pallas_call | solution.py:229
  206.8 11.7 %collective-permute-done.1.second_ref.v4_ref = bf16[2048,256]{1,0:T(8,128)(2,1)S(1)} collective-permute-done((bf16[2048,256]{1,0:T(8,128)(2,1)S(1)}, bf16[2048,256]{1,0:T(8,128)(2,1)S(1)}, u32[]{:S(2)}, u32[]{:S(2)}) %collective-permute-start.1) | collective-permute-done | bytes 1048608 | tf_op jit(solution)/shard_map/ppermute | solution.py:18
  218.4 1.0 copy-done
  219.4 2.0 pick.12
  221.5 1.8 collective-permute-start.6
  223.3 2.0 pick.15
  225.3 0.1 collective-permute-start.12
  225.4 0.5 collective-permute-start.11
  225.9 2.0 pick.13
  227.9 0.2 collective-permute-start.8
  228.0 18.4 %collective-permute-done.6.v2_ref = bf16[2048,256]{1,0:T(8,128)(2,1)S(1)} collective-permute-done((bf16[2048,256]{1,0:T(8,128)(2,1)}, bf16[2048,256]{1,0:T(8,128)(2,1)S(1)}, u32[]{:S(2)}, u32[]{:S(2)}) %collective-permute-start.6) | collective-permute-done | bytes 1048608 | tf_op jit(solution)/shard_map/ppermute | solution.py:18
  246.5 0.1 collective-permute-start.16
  246.6 0.2 collective-permute-start
  246.8 9.0 %shard_map.38 = (bf16[4,1024,1024]{2,1,0:T(8,128)(2,1)}, f32[8,128]{1,0:T(8,128)}) custom-call(s32[1]{0:T(128)} %bitcast.bit_ref, bf16[1024,2048]{1,0:T(8,128)(2,1)} %get-tuple-element.34.own_ref, f32[1024,1]{1,0:T(8,128)} %get-tuple-element.35.refs_0_.norm_ref, bf16[2048,256]{1,0:T(8,128)(2,1)} %copy-done.1, ...), custom_call_target="tpu_custom_call", output_to_operand_aliasing={{0}: (7, {})} | custom-call | tf_op jit(solution)/shard_map/pallas_call | solution.py:229
  255.8 7.3 %collective-permute-done.16.second_ref.v4_ref = bf16[2048,128]{1,0:T(8,128)(2,1)S(1)} collective-permute-done((bf16[2048,128]{1,0:T(8,128)(2,1)S(1)}, bf16[2048,128]{1,0:T(8,128)(2,1)S(1)}, u32[]{:S(2)}, u32[]{:S(2)}) %collective-permute-start.16) | collective-permute-done | bytes 524320 | tf_op jit(solution)/shard_map/ppermute | solution.py:18
  263.1 0.8 copy-done.5
  263.9 1.8 pick.18
  265.7 1.8 collective-permute-start.17
  267.6 9.0 %shard_map.39 = (bf16[4,1024,1024]{2,1,0:T(8,128)(2,1)}, f32[8,128]{1,0:T(8,128)}) custom-call(s32[1]{0:T(128)} %bitcast.bit_ref, bf16[1024,2048]{1,0:T(8,128)(2,1)} %get-tuple-element.34.own_ref, f32[1024,1]{1,0:T(8,128)} %get-tuple-element.35.refs_0_.norm_ref, bf16[2048,256]{1,0:T(8,128)(2,1)} %copy-done, ...), custom_call_target="tpu_custom_call", output_to_operand_aliasing={{0}: (7, {})} | custom-call | tf_op jit(solution)/shard_map/pallas_call | solution.py:229
  276.6 0.8 copy-done.4
  277.4 1.8 pick.16
  279.2 0.4 collective-permute-start.13
  279.6 1.8 pick.19
  281.4 0.1 collective-permute-start.19
  281.5 0.5 collective-permute-start.18
  282.0 1.8 pick.17
  283.8 0.3 collective-permute-start.15
  284.1 8.0 %collective-permute-done.13.v2_ref = bf16[2048,128]{1,0:T(8,128)(2,1)S(1)} collective-permute-done((bf16[2048,128]{1,0:T(8,128)(2,1)}, bf16[2048,128]{1,0:T(8,128)(2,1)S(1)}, u32[]{:S(2)}, u32[]{:S(2)}) %collective-permute-start.13) | collective-permute-done | bytes 524320 | tf_op jit(solution)/shard_map/ppermute | solution.py:18
  292.2 0.8 copy-done.12
  293.0 0.1 copy-done.14
  293.2 8.5 %shard_map.40 = (bf16[4,1024,1024]{2,1,0:T(8,128)(2,1)}, f32[8,128]{1,0:T(8,128)}) custom-call(s32[1]{0:T(128)} %bitcast.bit_ref, bf16[1024,2048]{1,0:T(8,128)(2,1)} %get-tuple-element.34.own_ref, f32[1024,1]{1,0:T(8,128)} %get-tuple-element.35.refs_0_.norm_ref, bf16[2048,128]{1,0:T(8,128)(2,1)} %copy-done.5, ...), custom_call_target="tpu_custom_call", output_to_operand_aliasing={{0}: (7, {})} | custom-call | tf_op jit(solution)/shard_map/pallas_call | solution.py:229
  301.7 0.8 copy-done.11
  302.5 0.2 copy-done.13
  302.6 8.5 %shard_map.41 = (bf16[4,1024,1024]{2,1,0:T(8,128)(2,1)}, f32[8,128]{1,0:T(8,128)}) custom-call(s32[1]{0:T(128)} %bitcast.bit_ref, bf16[1024,2048]{1,0:T(8,128)(2,1)} %get-tuple-element.34.own_ref, f32[1024,1]{1,0:T(8,128)} %get-tuple-element.35.refs_0_.norm_ref, bf16[2048,128]{1,0:T(8,128)(2,1)} %copy-done.4, ...), custom_call_target="tpu_custom_call", output_to_operand_aliasing={{0}: (7, {})} | custom-call | tf_op jit(solution)/shard_map/pallas_call | solution.py:229
  (36 shorter events, 0.1 us)
Async XLA Ops:
  9.9 13.8 %copy-start.15 = (s32[2,2048]{1,0:T(2,128)S(1)}, s32[2,2048]{1,0:T(2,128)}, u32[]{:S(2)}) copy-start(s32[2,2048]{1,0:T(2,128)} %param.6) | copy-start | bytes 49156
  9.9 13.8 %copy-start.16 = (s32[640]{0:T(1024)S(1)}, s32[640]{0:T(1024)}, u32[]{:S(2)}) copy-start(s32[640]{0:T(1024)} %param.7) | copy-start | bytes 7684
  16.2 80.5 %all-to-all-start.1 = ((f16[16,3,40,1024]{3,2,1,0:T(8,128)(2,1)}), f16[16,3,40,1024]{3,2,1,0:T(8,128)(2,1)}, u32[]{:S(2)}, u32[]{:S(2)}) async-start(f16[16,3,40,1024]{3,2,1,0:T(8,128)(2,1)} %select_convert_fusion), calls=%async_computation.1 | async-start | bytes 7864320 | tf_op jit(solution)/shard_map/all_to_all | solution.py:301
  122.8 68.3 %copy-start.3 = (bf16[2048,256]{1,0:T(8,128)(2,1)S(1)}, bf16[2048,256]{1,0:T(8,128)(2,1)}, u32[]{:S(2)}) copy-start(bf16[2048,256]{1,0:T(8,128)(2,1)} %get-tuple-element.31.refs_2_.first_ref) | copy-start | bytes 3145732
  122.8 36.5 %collective-permute-start.2 = (bf16[2048,256]{1,0:T(8,128)(2,1)}, bf16[2048,256]{1,0:T(8,128)(2,1)S(1)}, u32[]{:S(2)}, u32[]{:S(2)}) collective-permute-start(bf16[2048,256]{1,0:T(8,128)(2,1)} %get-tuple-element.29.refs_0_.first_ref), channel_id=1, source_target_pairs={{0,4},{1,5},{2,6},{3,7},{4,8},{5,9},{6,10},{7,11},{8,12},{9,13},{1... | collective-permute-start | bytes 3145736 | tf_op jit(solution)/shard_map/ppermute | solution.py:18
  159.3 1.0 copy-start.2
  162.3 28.7 %collective-permute-start.3 = (bf16[2048,256]{1,0:T(8,128)(2,1)}, bf16[2048,256]{1,0:T(8,128)(2,1)}, u32[]{:S(2)}, u32[]{:S(2)}) collective-permute-start(bf16[2048,256]{1,0:T(8,128)(2,1)} %pick.10), channel_id=1, source_target_pairs={{0,2},{1,3},{2,0},{3,1},{4,6},{5,7},{6,4},{7,5},{8,10},{9,11},{10,... | collective-permute-start | bytes 3145736 | tf_op jit(solution)/shard_map/ppermute | solution.py:18
  167.6 26.6 %collective-permute-start.9 = (bf16[2048,256]{1,0:T(8,128)(2,1)}, bf16[2048,256]{1,0:T(8,128)(2,1)S(1)}, u32[]{:S(2)}, u32[]{:S(2)}) collective-permute-start(bf16[2048,256]{1,0:T(8,128)(2,1)} %get-tuple-element.30.refs_1_.first_ref), channel_id=1, source_target_pairs={{0,4},{1,5},{2,6},{3,7},{4,8},{5,9},{6,10},{7,11},{8,12},{9,13},{1... | collective-permute-start | bytes 3145736 | tf_op jit(solution)/shard_map/ppermute | solution.py:18
  170.5 27.1 %collective-permute-start.5 = (bf16[2048,256]{1,0:T(8,128)(2,1)}, bf16[2048,256]{1,0:T(8,128)(2,1)}, u32[]{:S(2)}, u32[]{:S(2)}) collective-permute-start(bf16[2048,256]{1,0:T(8,128)(2,1)} %pick.11), channel_id=1, source_target_pairs={{0,1},{1,0},{2,3},{3,2},{4,5},{5,4},{6,7},{7,6},{8,9},{9,8},{10,11... | collective-permute-start | bytes 3145736 | tf_op jit(solution)/shard_map/ppermute | solution.py:18
  191.1 6.6 %collective-permute-start.4 = (bf16[2048,256]{1,0:T(8,128)(2,1)}, bf16[2048,256]{1,0:T(8,128)(2,1)}, u32[]{:S(2)}, u32[]{:S(2)}) collective-permute-start(bf16[2048,256]{1,0:T(8,128)(2,1)} %collective-permute-done.3.v2_ref), channel_id=1, source_target_pairs={{0,1},{1,0},{2,3},{3,2},{4,5},{5,4},{6,7},{7,6},{8,9},{9,8},{10,11... | collective-permute-start | bytes 3145736 | tf_op jit(solution)/shard_map/ppermute | solution.py:18
  191.1 27.4 %collective-permute-start.1 = (bf16[2048,256]{1,0:T(8,128)(2,1)S(1)}, bf16[2048,256]{1,0:T(8,128)(2,1)S(1)}, u32[]{:S(2)}, u32[]{:S(2)}) collective-permute-start(bf16[2048,256]{1,0:T(8,128)(2,1)S(1)} %copy-done.3), channel_id=1, source_target_pairs={{0,4},{1,5},{2,6},{3,7},{4,8},{5,9},{6,10},{7,11},{8,12},{9,13},{1... | collective-permute-start | bytes 3145736 | tf_op jit(solution)/shard_map/ppermute | solution.py:18
  194.2 1.0 copy-start.1
  197.2 28.2 %collective-permute-start.10 = (bf16[2048,256]{1,0:T(8,128)(2,1)}, bf16[2048,256]{1,0:T(8,128)(2,1)}, u32[]{:S(2)}, u32[]{:S(2)}) collective-permute-start(bf16[2048,256]{1,0:T(8,128)(2,1)} %pick.14), channel_id=1, source_target_pairs={{0,2},{1,3},{2,0},{3,1},{4,6},{5,7},{6,4},{7,5},{8,10},{9,11},{10,... | collective-permute-start | bytes 3145736 | tf_op jit(solution)/shard_map/ppermute | solution.py:18
  197.6 48.8 %copy-start.7 = (bf16[2048,128]{1,0:T(8,128)(2,1)S(1)}, bf16[2048,128]{1,0:T(8,128)(2,1)}, u32[]{:S(2)}) copy-start(bf16[2048,128]{1,0:T(8,128)(2,1)} %get-tuple-element.32.refs_3_.first_ref) | copy-start | bytes 1572868
  197.7 48.9 %copy-start.6 = (bf16[2048,128]{1,0:T(8,128)(2,1)S(1)}, bf16[2048,128]{1,0:T(8,128)(2,1)}, u32[]{:S(2)}) copy-start(bf16[2048,128]{1,0:T(8,128)(2,1)} %get-tuple-element.33.refs_4_.first_ref) | copy-start | bytes 1572868
  218.4 1.0 copy-start
  221.5 25.0 %collective-permute-start.6 = (bf16[2048,256]{1,0:T(8,128)(2,1)}, bf16[2048,256]{1,0:T(8,128)(2,1)S(1)}, u32[]{:S(2)}, u32[]{:S(2)}) collective-permute-start(bf16[2048,256]{1,0:T(8,128)(2,1)} %pick.12), channel_id=1, source_target_pairs={{0,2},{1,3},{2,0},{3,1},{4,6},{5,7},{6,4},{7,5},{8,10},{9,11},{10,... | collective-permute-start | bytes 3145736 | tf_op jit(solution)/shard_map/ppermute | solution.py:18
  225.3 21.2 %collective-permute-start.12 = (bf16[2048,256]{1,0:T(8,128)(2,1)}, bf16[2048,256]{1,0:T(8,128)(2,1)}, u32[]{:S(2)}, u32[]{:S(2)}) collective-permute-start(bf16[2048,256]{1,0:T(8,128)(2,1)} %pick.15), channel_id=1, source_target_pairs={{0,1},{1,0},{2,3},{3,2},{4,5},{5,4},{6,7},{7,6},{8,9},{9,8},{10,11... | collective-permute-start | bytes 3145736 | tf_op jit(solution)/shard_map/ppermute | solution.py:18
  225.4 21.4 %collective-permute-start.11 = (bf16[2048,256]{1,0:T(8,128)(2,1)}, bf16[2048,256]{1,0:T(8,128)(2,1)}, u32[]{:S(2)}, u32[]{:S(2)}) collective-permute-start(bf16[2048,256]{1,0:T(8,128)(2,1)} %collective-permute-done.10.v2_ref), channel_id=1, source_target_pairs={{0,1},{1,0},{2,3},{3,2},{4,5},{5,4},{6,7},{7,6},{8,9},{9,8},{10,11... | collective-permute-start | bytes 3145736 | tf_op jit(solution)/shard_map/ppermute | solution.py:18
  227.9 39.7 %collective-permute-start.8 = (bf16[2048,256]{1,0:T(8,128)(2,1)}, bf16[2048,256]{1,0:T(8,128)(2,1)}, u32[]{:S(2)}, u32[]{:S(2)}) collective-permute-start(bf16[2048,256]{1,0:T(8,128)(2,1)} %pick.13), channel_id=1, source_target_pairs={{0,1},{1,0},{2,3},{3,2},{4,5},{5,4},{6,7},{7,6},{8,9},{9,8},{10,11... | collective-permute-start | bytes 3145736 | tf_op jit(solution)/shard_map/ppermute | solution.py:18
  246.5 9.4 %copy-start.8 = (bf16[2048,256]{1,0:T(8,128)(2,1)}, bf16[2048,256]{1,0:T(8,128)(2,1)S(1)}, u32[]{:S(2)}) copy-start(bf16[2048,256]{1,0:T(8,128)(2,1)S(1)} %collective-permute-done.6.v2_ref) | copy-start | bytes 3145732
  246.5 21.1 %collective-permute-start.7 = (bf16[2048,256]{1,0:T(8,128)(2,1)S(1)}, bf16[2048,256]{1,0:T(8,128)(2,1)}, u32[]{:S(2)}, u32[]{:S(2)}) collective-permute-start(bf16[2048,256]{1,0:T(8,128)(2,1)S(1)} %collective-permute-done.6.v2_ref), channel_id=1, source_target_pairs={{0,1},{1,0},{2,3},{3,2},{4,5},{5,4},{6,7},{7,6},{8,9},{9,8},{10,11... | collective-permute-start | bytes 3145736 | tf_op jit(solution)/shard_map/ppermute | solution.py:18
  246.5 16.6 %collective-permute-start.16 = (bf16[2048,128]{1,0:T(8,128)(2,1)S(1)}, bf16[2048,128]{1,0:T(8,128)(2,1)S(1)}, u32[]{:S(2)}, u32[]{:S(2)}) collective-permute-start(bf16[2048,128]{1,0:T(8,128)(2,1)S(1)} %copy-done.7), channel_id=1, source_target_pairs={{0,4},{1,5},{2,6},{3,7},{4,8},{5,9},{6,10},{7,11},{8,12},{9,13},{1... | collective-permute-start | bytes 1572872 | tf_op jit(solution)/shard_map/ppermute | solution.py:18
  246.6 30.0 %collective-permute-start = (bf16[2048,128]{1,0:T(8,128)(2,1)S(1)}, bf16[2048,128]{1,0:T(8,128)(2,1)S(1)}, u32[]{:S(2)}, u32[]{:S(2)}) collective-permute-start(bf16[2048,128]{1,0:T(8,128)(2,1)S(1)} %copy-done.6), channel_id=1, source_target_pairs={{0,4},{1,5},{2,6},{3,7},{4,8},{5,9},{6,10},{7,11},{8,12},{9,13},{1... | collective-permute-start | bytes 1572872 | tf_op jit(solution)/shard_map/ppermute | solution.py:18
  263.1 0.8 copy-start.5
  265.7 15.7 %collective-permute-start.17 = (bf16[2048,128]{1,0:T(8,128)(2,1)}, bf16[2048,128]{1,0:T(8,128)(2,1)S(1)}, u32[]{:S(2)}, u32[]{:S(2)}) collective-permute-start(bf16[2048,128]{1,0:T(8,128)(2,1)} %pick.18), channel_id=1, source_target_pairs={{0,2},{1,3},{2,0},{3,1},{4,6},{5,7},{6,4},{7,5},{8,10},{9,11},{10,... | collective-permute-start | bytes 1572872 | tf_op jit(solution)/shard_map/ppermute | solution.py:18
  276.6 0.8 copy-start.4
  279.2 12.9 %collective-permute-start.13 = (bf16[2048,128]{1,0:T(8,128)(2,1)}, bf16[2048,128]{1,0:T(8,128)(2,1)S(1)}, u32[]{:S(2)}, u32[]{:S(2)}) collective-permute-start(bf16[2048,128]{1,0:T(8,128)(2,1)} %pick.16), channel_id=1, source_target_pairs={{0,2},{1,3},{2,0},{3,1},{4,6},{5,7},{6,4},{7,5},{8,10},{9,11},{10,... | collective-permute-start | bytes 1572872 | tf_op jit(solution)/shard_map/ppermute | solution.py:18
  281.4 10.7 %collective-permute-start.19 = (bf16[2048,128]{1,0:T(8,128)(2,1)}, bf16[2048,128]{1,0:T(8,128)(2,1)S(1)}, u32[]{:S(2)}, u32[]{:S(2)}) collective-permute-start(bf16[2048,128]{1,0:T(8,128)(2,1)} %pick.19), channel_id=1, source_target_pairs={{0,1},{1,0},{2,3},{3,2},{4,5},{5,4},{6,7},{7,6},{8,9},{9,8},{10,11... | collective-permute-start | bytes 1572872 | tf_op jit(solution)/shard_map/ppermute | solution.py:18
  281.5 10.7 %copy-start.9 = (bf16[2048,128]{1,0:T(8,128)(2,1)}, bf16[2048,128]{1,0:T(8,128)(2,1)S(1)}, u32[]{:S(2)}) copy-start(bf16[2048,128]{1,0:T(8,128)(2,1)S(1)} %collective-permute-done.17.v2_ref) | copy-start | bytes 1572868
  281.5 10.6 %collective-permute-start.18 = (bf16[2048,128]{1,0:T(8,128)(2,1)S(1)}, bf16[2048,128]{1,0:T(8,128)(2,1)S(1)}, u32[]{:S(2)}, u32[]{:S(2)}) collective-permute-start(bf16[2048,128]{1,0:T(8,128)(2,1)S(1)} %collective-permute-done.17.v2_ref), channel_id=1, source_target_pairs={{0,1},{1,0},{2,3},{3,2},{4,5},{5,4},{6,7},{7,6},{8,9},{9,8},{10,11... | collective-permute-start | bytes 1572872 | tf_op jit(solution)/shard_map/ppermute | solution.py:18
  283.8 17.9 %collective-permute-start.15 = (bf16[2048,128]{1,0:T(8,128)(2,1)}, bf16[2048,128]{1,0:T(8,128)(2,1)S(1)}, u32[]{:S(2)}, u32[]{:S(2)}) collective-permute-start(bf16[2048,128]{1,0:T(8,128)(2,1)} %pick.17), channel_id=1, source_target_pairs={{0,1},{1,0},{2,3},{3,2},{4,5},{5,4},{6,7},{7,6},{8,9},{9,8},{10,11... | collective-permute-start | bytes 1572872 | tf_op jit(solution)/shard_map/ppermute | solution.py:18
  292.1 9.6 %copy-start.10 = (bf16[2048,128]{1,0:T(8,128)(2,1)}, bf16[2048,128]{1,0:T(8,128)(2,1)S(1)}, u32[]{:S(2)}) copy-start(bf16[2048,128]{1,0:T(8,128)(2,1)S(1)} %collective-permute-done.13.v2_ref) | copy-start | bytes 1572868
  292.1 9.6 %collective-permute-start.14 = (bf16[2048,128]{1,0:T(8,128)(2,1)S(1)}, bf16[2048,128]{1,0:T(8,128)(2,1)S(1)}, u32[]{:S(2)}, u32[]{:S(2)}) collective-permute-start(bf16[2048,128]{1,0:T(8,128)(2,1)S(1)} %collective-permute-done.13.v2_ref), channel_id=1, source_target_pairs={{0,1},{1,0},{2,3},{3,2},{4,5},{5,4},{6,7},{7,6},{8,9},{9,8},{10,11... | collective-permute-start | bytes 1572872 | tf_op jit(solution)/shard_map/ppermute | solution.py:18
  292.1 0.9 copy-start.12
  292.1 1.0 copy-start.14
  301.7 0.8 copy-start.11
  301.7 1.0 copy-start.13

commit v2 on v1

--- a/solution.py
+++ b/solution.py
@@ -11,6 +11,8 @@
 
 ROUNDS = 4
 VMEM_BYTES = 58 * 1024 * 1024
+UNIT = 1.0 / 512.0
+BAD = -32768
 
 
 def permuted(shard, axis, to):
@@ -34,7 +36,7 @@
     return max(d for d in range(1, limit + 1) if value % d == 0)
 
 
-def features_kernel(slots_ref, x_ref, *refs, steps, tile, pitch):
+def features_kernel(slots_ref, x_ref, *refs, steps, tile, pitch, starts, unit):
     *ft_refs, atoms_ref, squares_ref = refs
     step = pl.program_id(0)
     per_step, _, rows, frames = x_ref.shape
@@ -44,11 +46,14 @@
     def _():
         def regroup(g, carry):
             for component in range(3):
+                x = x_ref[g, component]
+                if x.dtype != jnp.float32:
+                    x = x.astype(jnp.int32).astype(jnp.float32)
                 for top in range(0, rows, 8):
                     for s in range(8):
                         start = ((step * per_step + g) * rows + top) * 24 + component * 8 + s
-                        atoms_ref[pl.ds(start, 8, stride=24), :] = x_ref[
-                            g, component, top:top + 8, s * lanes:(s + 1) * lanes]
+                        atoms_ref[pl.ds(start, 8, stride=24), :] = x[
+                            top:top + 8, s * lanes:(s + 1) * lanes]
             return carry
 
         lax.fori_loop(0, per_step, regroup, 0)
@@ -72,18 +77,18 @@
             return carry
 
         lax.fori_loop(0, tile // unroll, contacts, 0)
-        s = 0
-        for ft_ref in ft_refs:
+        for ft_ref, start in zip(ft_refs, starts):
             for left in range(0, ft_ref.shape[1], lanes):
-                squared = jnp.minimum(squares_ref[s * pitch:s * pitch + tile, :] + 0.01, 1e30)
+                s = (start + left) // lanes
+                squared = squares_ref[s * pitch:s * pitch + tile, :] * (unit * unit) + 0.01
+                squared = jnp.minimum(squared, 1e30)
                 separation = squared * lax.rsqrt(squared)
                 scale = math.log2(math.e) / 1.5
                 feature = 1.0 / (1.0 + jnp.exp2(separation * scale - 8.0 * scale))
                 ft_ref[:, left:left + lanes] = feature.astype(jnp.bfloat16)
-                s += 1
-
-
-def features_of(x, slots24, widths):
+
+
+def features_of(x, slots24, starts, widths, unit):
     groups, _, rows, frames = x.shape
     contacts = slots24.shape[1]
     per_step = largest_divisor(groups, max(1, 160 // rows))
@@ -91,7 +96,8 @@
     tile = 512
     pitch = tile + 8
     return pl.pallas_call(
-        functools.partial(features_kernel, steps=steps, tile=tile, pitch=pitch),
+        functools.partial(features_kernel, steps=steps, tile=tile, pitch=pitch,
+                          starts=starts, unit=unit),
         grid_spec=pltpu.PrefetchScalarGridSpec(
             num_scalar_prefetch=1,
             grid=(steps + contacts // tile,),
@@ -110,28 +116,26 @@
     )(slots24, x)
 
 
-def own_kernel(*refs):
+def own_kernel(*refs, starts):
     *ft_refs, f_ref, norm_ref = refs
 
     @pl.when(pl.program_id(0) == 0)
     def _():
         norm_ref[...] = jnp.zeros_like(norm_ref)
 
-    row = 0
-    for ft_ref in ft_refs:
+    for ft_ref, row in zip(ft_refs, starts):
         width = ft_ref.shape[1]
         own = ft_ref[...].astype(jnp.float32).T
         f_ref[row:row + width, :] = own.astype(jnp.bfloat16)
         norm_ref[row:row + width, :] += jnp.sum(own * own, axis=1, keepdims=True)
-        row += width
-
-
-def own_features(fts):
+
+
+def own_features(fts, starts):
     contacts = fts[0].shape[0]
     frames = sum(ft.shape[1] for ft in fts)
     tile = 512
     return pl.pallas_call(
-        own_kernel,
+        functools.partial(own_kernel, starts=starts),
         grid=(contacts // tile,),
         in_specs=[pl.BlockSpec((tile, ft.shape[1]), lambda i: (i, 0)) for ft in fts],
         out_specs=[
@@ -188,27 +192,27 @@
 def distance_kernel(bit_ref, own_ref, norm_ref, v4_ref, v2_ref, vx_ref, vy_ref, *refs, aliased):
     refs = refs[1:] if aliased else refs
     out_ref, token_ref, vnorm_ref = refs
-    high_core = bit_ref[0] == 1
-    visitors = (
-        lambda: jnp.where(high_core, vy_ref[...], vx_ref[...]),
-        lambda: v2_ref[...],
-        lambda: jnp.where(high_core, vx_ref[...], vy_ref[...]),
-        lambda: v4_ref[...],
-    )
 
     @pl.when(pl.program_id(0) == 0)
     def _():
-        for r, load in enumerate(visitors):
-            wide = load().astype(jnp.float32)
+        for r, ref in enumerate((vx_ref, v2_ref, vy_ref, v4_ref)):
+            wide = ref[...].astype(jnp.float32)
             vnorm_ref[r, 0:1, :] = jnp.sum(wide * wide, axis=0, keepdims=True)
         token_ref[...] = jnp.zeros_like(token_ref)
 
-    own = own_ref[...]
-    own_norm = norm_ref[...]
-    for r, load in enumerate(visitors):
-        inter = jnp.dot(own, load(), preferred_element_type=jnp.float32)
-        ratio = inter / (own_norm + vnorm_ref[r, 0:1, :] - inter + 1e-06)
-        out_ref[r] = (1.0 - ratio).astype(jnp.bfloat16)
+    def rounds(places):
+        for r, ref in enumerate((vx_ref, v2_ref, vy_ref, v4_ref)):
+            inter = jnp.dot(own_ref[...], ref[...], preferred_element_type=jnp.float32)
+            ratio = inter / (norm_ref[...] + vnorm_ref[r, 0:1, :] - inter + 1e-06)
+            out_ref[places[r]] = (1.0 - ratio).astype(jnp.bfloat16)
+
+    @pl.when(bit_ref[0] == 1)
+    def _():
+        rounds((2, 1, 0, 3))
+
+    @pl.when(bit_ref[0] != 1)
+    def _():
+        rounds((0, 1, 2, 3))
 
 
 def distance_chunk(bit, own, norms, v4, v2, vx, vy, out, start):
@@ -250,19 +254,21 @@
     return jnp.sum(jnp.where(hits, places, 0), axis=2, dtype=jnp.int32)
 
 
-def split_kernel(x_ref, pieces_ref, fine_ref, extent_ref, spread_ref):
+def split_kernel(x_ref, pieces_ref, extent_ref, spread_ref):
     step = pl.program_id(0)
-    count, _, _, frames = pieces_ref.shape
+    _, _, _, frames = pieces_ref.shape
+    per_step = x_ref.shape[2] // frames
 
     @pl.when(step == 0)
     def _():
         extent_ref[...] = jnp.zeros_like(extent_ref)
         spread_ref[...] = jnp.full_like(spread_ref, jnp.inf)
 
-    for k in range(count):
+    for k in range(per_step):
         x = x_ref[:, :, k * frames:(k + 1) * frames]
-        pieces_ref[k] = x
-        extent_ref[...] = jnp.maximum(extent_ref[...], jnp.max(jnp.abs(x), axis=(0, 2), keepdims=True)[0])
+        coded = jnp.clip(jnp.round(x * (1.0 / UNIT)), -32767.0, 32767.0)
+        pieces_ref[step * per_step + k] = coded.astype(jnp.int32).astype(jnp.int16)
+        extent_ref[...] = jnp.maximum(extent_ref[...], jnp.max(jnp.abs(x), axis=0))
         mean = jnp.sum(x, axis=2, keepdims=True) * (1.0 / frames)
         square = jnp.sum(x * x, axis=2, keepdims=True) * (1.0 / frames)
         spread = jnp.mean(square - mean * mean, axis=(0, 1), keepdims=True)[0]
@@ -270,9 +276,11 @@
 
     @pl.when(step == pl.num_programs(0) - 1)
     def _():
-        extent = jnp.max(extent_ref[...], axis=0, keepdims=True)
-        fine = (extent <= 64.0) & (spread_ref[...] >= 6e-5 * extent * extent)
-        fine_ref[...] = jnp.where(fine, 1.0, 0.0)
+        fine = (jnp.max(extent_ref[...]) <= 32767.0 * UNIT) & (jnp.min(spread_ref[...]) >= 0.05)
+
+        @pl.when(jnp.logical_not(fine))
+        def _():
+            pieces_ref[...] = jnp.full(pieces_ref.shape, BAD, jnp.int32).astype(jnp.int16)
 
 
 def split_blocks(coords, count):
@@ -283,46 +291,47 @@
         split_kernel,
         grid=(count // per_step,),
         in_specs=[pl.BlockSpec((3, rows, per_step * per_block), lambda i: (0, 0, i))],
-        out_specs=[
-            pl.BlockSpec((per_step, 3, rows, per_block), lambda i: (i, 0, 0, 0)),
-            pl.BlockSpec((1, 1), lambda i: (0, 0)),
-        ],
-        out_shape=[
-            jax.ShapeDtypeStruct((count, 3, rows, per_block), jnp.float32),
-            jax.ShapeDtypeStruct((1, 1), jnp.float32),
-        ],
-        scratch_shapes=[pltpu.VMEM((rows, 1), jnp.float32), pltpu.VMEM((1, 1), jnp.float32)],
+        out_specs=pl.BlockSpec((count, 3, rows, per_block), lambda i: (0, 0, 0, 0)),
+        out_shape=jax.ShapeDtypeStruct((count, 3, rows, per_block), jnp.int16),
+        scratch_shapes=[pltpu.VMEM((rows, per_block), jnp.float32), pltpu.VMEM((1, 1), jnp.float32)],
         compiler_params=pltpu.CompilerParams(vmem_limit_bytes=VMEM_BYTES),
         name="split_blocks",
     )(coords)
 
 
 def exchanged(pieces):
-    return lax.all_to_all(pieces, "blocks", split_axis=0, concat_axis=0, tiled=True)
-
-
-def gathered_coords(coords, count):
-    pieces, fine = split_blocks(coords.transpose(1, 0, 2), count)
-    narrow = exchanged(jnp.where(fine[0, 0] > 0.5, pieces, jnp.inf).astype(jnp.float16))
-    all_fine = jnp.all(narrow[:, 0, 0, 0].astype(jnp.float32) < jnp.inf)
-    return lax.cond(all_fine, lambda: narrow.astype(jnp.float32), lambda: exchanged(pieces))
+    got = lax.all_to_all(pieces, "blocks", split_axis=0, concat_axis=0, tiled=True)
+    count, _, rows, per_block = got.shape
+    if rows % 8:
+        got = got.transpose(0, 2, 1, 3).reshape(count * rows // 8, 8, 3, per_block)
+        got = got.transpose(0, 2, 1, 3)
+    return got
+
+
+def contact_features(coords, slots24, starts, widths):
+    count = lax.axis_size("blocks")
+    narrow = exchanged(split_blocks(coords.transpose(1, 0, 2), count))
+    all_fine = jnp.all(narrow[:, 0, 0, 0] != BAD)
+
+    def coarse():
+        return features_of(narrow, slots24, starts, widths, UNIT)
+
+    def exact():
+        pieces = coords.reshape(coords.shape[0], 3, count, -1).transpose(2, 1, 0, 3)
+        return features_of(exchanged(pieces), slots24, starts, widths, 1.0)
+
+    return lax.cond(all_fine, coarse, exact)
 
 
 def shards(coords, pairs, res_slot):
-    count = lax.axis_size("blocks")
     index = lax.axis_index("blocks")
-    res_local, _, frames = coords.shape
-    per_block = frames // count
-    lanes = per_block // 8
-    residues = res_local * count
-    widths = [lanes * n for n in (2, 2, 2, 1, 1)]
-
-    arrived = gathered_coords(coords, count)
-    if res_local % 8:
-        arrived = arrived.transpose(0, 2, 1, 3).reshape(residues // 8, 8, 3, per_block)
-        arrived = arrived.transpose(0, 2, 1, 3)
+    lanes = coords.shape[2] // lax.axis_size("blocks") // 8
+    widths = [lanes * n for n in (1, 2, 2, 2, 1)]
+    starts = [lanes * n for n in (0, 2, 4, 6, 1)]
+
     slots24 = contact_slots(pairs, res_slot) * 24
-    fts = features_of(arrived, slots24, widths)
+    fts = contact_features(coords, slots24, starts, widths)
+
     bit = (index & 1).astype(jnp.int32).reshape(1)
     low_core = 1 - bit
     low_pair = 1 - ((index >> 1) & 1).astype(jnp.int32).reshape(1)
@@ -330,18 +339,19 @@
     v4s = []
     for ft in fts:
         v4s.append(permuted(ft, "blocks", shift4))
-    own, norms = own_features(fts)
+    own, norms = own_features(fts, starts)
+
     out = None
     tokens = []
-    start = 0
     for j, (ft, v4) in enumerate(zip(fts, v4s)):
         after = tokens[j - 2:j - 1] if j >= 2 else [norms]
-        v2 = permuted(pick(low_pair, ft, v4, after), "blocks", swap2)
+        sent = pick(low_pair, ft, v4, after)
+        v2 = permuted(sent, "blocks", swap2)
+        sent = pick(low_core, ft, v4, [])
+        vy = permuted(sent, "blocks", swap1)
         vx = permuted(v2, "blocks", swap1)
-        vy = permuted(pick(low_core, ft, v4, []), "blocks", swap1)
-        out, token = distance_chunk(bit, own, norms, v4, v2, vx, vy, out, start)
+        out, token = distance_chunk(bit, own, norms, v4, v2, vx, vy, out, starts[j])
         tokens.append(token)
-        start += ft.shape[1]
     return out
 
 

time: 312 us -> 295 us (0.946)
  other arithmetic: 16.2 us -> 3.06 us
  Pallas kernels: 96.5 us -> 90.4 us
  starting transfers between devices: 34.6 us -> 40.6 us
    convert_element_type x2 -> x0, other arithmetic: 12.5 us -> none  [the longest x1 6.29 us: gathered_coords(): jnp.where(fine[0, 0] > 0.5, pieces, jnp.inf).astype(jnp.float16)]
    ppermute x20, starting transfers between devices: 27.2 us -> 33.1 us  [permuted(): return lax.ppermute(shard, axis, [(i, to(i, count)) for i in range(count)])]
    pallas_call x10, Pallas kernels: 19.3 us -> 15.4 us  [pick(): pl.pallas_call(pick_kernel, in_specs=[pl.BlockSpec(memory_space=pltpu.SME...]
    unnamed x34 -> x28, local copies, waits for them, and re-layouts: 6.58 us -> 5.84 us
  transfers between devices with their start and end apart: 21 -> 21, of which waited for: 8 -> 9; matrix products, arithmetic and copies ran while one was open for 1% -> 1% of each run, Pallas kernels for 19% -> 19%
where the time goes in v2:
time: 295 us
  waiting for transfers between devices  154 us (52%)
  Pallas kernels  90.4 us (31%)
  starting transfers between devices  40.6 us (14%)
  local copies, waits for them, and re-layouts  5.84 us (2%)
  other arithmetic  3.06 us (1%)
    ppermute x20, waiting for transfers between devices, permuted(): return lax.ppermute(shard, axis, [(i, to(i, count)) for i in range(count)])  82.4 us
    all_to_all x1, waiting for transfers between devices, exchanged(): lax.all_to_all(pieces, 'blocks', split_axis=0, concat_axis=0, tiled=True)  71.3 us
    pallas_call x5, Pallas kernels, distance_chunk(): pl.pallas_call(functools.partial(distance_kernel, aliased=aliased), grid=...  44.5 us
    ppermute x20, starting transfers between devices, permuted(): return lax.ppermute(shard, axis, [(i, to(i, count)) for i in range(count)])  33.1 us
    pallas_call x1, Pallas kernels, features_of(): pl.pallas_call(functools.partial(features_kernel, steps=steps, tile=tile,...  16.6 us
    pallas_call x10, Pallas kernels, pick(): pl.pallas_call(pick_kernel, in_specs=[pl.BlockSpec(memory_space=pltpu.SME...  15.4 us
    pallas_call x1, Pallas kernels, split_blocks(): pl.pallas_call(split_kernel, grid=(count // per_step,), in_specs=[pl.Bloc...  8.6 us
    all_to_all x1, starting transfers between devices, exchanged(): lax.all_to_all(pieces, 'blocks', split_axis=0, concat_axis=0, tiled=True)  7.46 us
  transfers between devices with their start and end apart: 21, of which 9 were waited for; matrix products, arithmetic and copies ran while one was open for 1% of the time, Pallas kernels for 19%

profile of v2, /device:TPU:0, one launch (start us, length us, event | category | flops | bytes accessed | tf_op | source)
XLA Modules:
  0.0 294.5 jit_solution(17340273676264570006)
XLA Ops:
  0.0 8.6 %split_blocks.1 = s16[16,3,40,1024]{3,2,1,0:T(8,128)(2,1)} custom-call(f32[3,40,16384]{2,1,0:T(8,128)} %bitcast.10), custom_call_target="tpu_custom_call" | custom-call | tf_op jit(solution)/shard_map/split_blocks/pallas_call | solution.py:290
  8.6 7.5 %all-to-all-start.1 = ((s16[16,3,40,1024]{3,2,1,0:T(8,128)(2,1)}), s16[16,3,40,1024]{3,2,1,0:T(8,128)(2,1)}, u32[]{:S(2)}, u32[]{:S(2)}) async-start(s16[16,3,40,1024]{3,2,1,0:T(8,128)(2,1)} %split_blocks.1), calls=%async_computation.1 | async-start | bytes 7864320 | tf_op jit(solution)/shard_map/all_to_all | solution.py:303
  16.1 1.6 select_reduce_fusion
  17.7 71.3 %all-to-all-done.1 = s16[16,3,40,1024]{3,2,1,0:T(8,128)(2,1)} async-done(((s16[16,3,40,1024]{3,2,1,0:T(8,128)(2,1)}), s16[16,3,40,1024]{3,2,1,0:T(8,128)(2,1)}, u32[]{:S(2)}, u32[]{:S(2)}) %all-to-all-start.1) | async-done | bytes 3932192 | tf_op jit(solution)/shard_map/all_to_all | solution.py:303
  89.1 1.4 compare_reduce_fusion
  91.1 16.6 %conditional.1 = ((bf16[2048,128]{1,0:T(8,128)(2,1)}, bf16[2048,256]{1,0:T(8,128)(2,1)S(1)}, bf16[2048,256]{1,0:T(8,128)(2,1)S(1)}, bf16[2048,256]{1,0:T(8,128)(2,1)}, bf16[2048,128]{1,0:T(8,128)(2,1)})) conditional(s32[]{:T(128)} %convert_element_type.3, (f32[40,3,16384]{2,0,1:T(8,128)}, s32[2,2048]{1,0:T(2,128)S(1)}) %tuple.11, ...), branch_computations={%region_2.3_spmd, %region_3.4_spmd} | conditional | bytes 31457288 | solution.py:323
  91.1 16.6 %features.3 = (bf16[2048,128]{1,0:T(8,128)(2,1)}, bf16[2048,256]{1,0:T(8,128)(2,1)S(1)}, bf16[2048,256]{1,0:T(8,128)(2,1)S(1)}, bf16[2048,256]{1,0:T(8,128)(2,1)}, bf16[2048,128]{1,0:T(8,128)(2,1)}) custom-call(s32[2,2048]{1,0:T(2,128)S(1)} %get-tuple-element.15.slots_ref, s16[16,3,40,1024]{3,2,1,0:T(8,128)(2,1)} %get-tuple-element.16.x_ref), custom_call_target="tpu_custom_call" | custom-call | tf_op jit(solution)/shard_map/cond/branch_1_fun/features/pallas_call | solution.py:98
  107.7 14.1 %collective-permute-start.9 = (bf16[2048,256]{1,0:T(8,128)(2,1)S(1)}, bf16[2048,256]{1,0:T(8,128)(2,1)S(1)}, u32[]{:S(2)}, u32[]{:S(2)}) collective-permute-start(bf16[2048,256]{1,0:T(8,128)(2,1)S(1)} %get-tuple-element.33.refs_1_.first_ref), channel_id=1, source_target_pairs={{0,4},{1,5},{2,6},{3,7},{4,8},{5,9},{6,10},{7,11},{8,12},{9,13},{1... | collective-permute-start | bytes 3145736 | tf_op jit(solution)/shard_map/ppermute | solution.py:20
  121.8 3.3 %collective-permute-start.2 = (bf16[2048,128]{1,0:T(8,128)(2,1)}, bf16[2048,128]{1,0:T(8,128)(2,1)}, u32[]{:S(2)}, u32[]{:S(2)}) collective-permute-start(bf16[2048,128]{1,0:T(8,128)(2,1)} %get-tuple-element.32.refs_0_.first_ref), channel_id=1, source_target_pairs={{0,4},{1,5},{2,6},{3,7},{4,8},{5,9},{6,10},{7,11},{8,12},{9,13},{1... | collective-permute-start | bytes 1572872 | tf_op jit(solution)/shard_map/ppermute | solution.py:20
  125.1 5.2 %own_features.1 = (bf16[1024,2048]{1,0:T(8,128)(2,1)}, f32[1024,1]{1,0:T(8,128)}) custom-call(bf16[2048,128]{1,0:T(8,128)(2,1)} %get-tuple-element.32.refs_0_.first_ref, bf16[2048,256]{1,0:T(8,128)(2,1)S(1)} %get-tuple-element.33.refs_1_.first_ref, bf16[2048,256]{1,0:T(8,128)(2,1)S(1)} %get-tuple-element.34.refs_2_.first_ref, ...), custom_call_target="tpu_custom_call" | custom-call | tf_op jit(solution)/shard_map/own_features/pallas_call | solution.py:137
  130.3 24.9 %collective-permute-done.2.second_ref.v4_ref = bf16[2048,128]{1,0:T(8,128)(2,1)} collective-permute-done((bf16[2048,128]{1,0:T(8,128)(2,1)}, bf16[2048,128]{1,0:T(8,128)(2,1)}, u32[]{:S(2)}, u32[]{:S(2)}) %collective-permute-start.2) | collective-permute-done | bytes 524320 | tf_op jit(solution)/shard_map/ppermute | solution.py:20
  155.2 1.8 pick.10
  157.1 5.4 %collective-permute-start.3 = (bf16[2048,128]{1,0:T(8,128)(2,1)}, bf16[2048,128]{1,0:T(8,128)(2,1)}, u32[]{:S(2)}, u32[]{:S(2)}) collective-permute-start(bf16[2048,128]{1,0:T(8,128)(2,1)} %pick.10), channel_id=1, source_target_pairs={{0,2},{1,3},{2,0},{3,1},{4,6},{5,7},{6,4},{7,5},{8,10},{9,11},{10,... | collective-permute-start | bytes 1572872 | tf_op jit(solution)/shard_map/ppermute | solution.py:20
  162.4 0.9 collective-permute-start.1
  163.3 0.0 collective-permute-done.9.second_ref.v4_ref
  163.3 1.0 copy-done.1
  164.4 1.1 pick.14
  165.5 1.0 collective-permute-start.10
  166.5 1.8 pick.11
  168.4 0.1 collective-permute-start.5
  168.4 7.1 %collective-permute-done.3.v2_ref = bf16[2048,128]{1,0:T(8,128)(2,1)} collective-permute-done((bf16[2048,128]{1,0:T(8,128)(2,1)}, bf16[2048,128]{1,0:T(8,128)(2,1)}, u32[]{:S(2)}, u32[]{:S(2)}) %collective-permute-start.3) | collective-permute-done | bytes 524320 | tf_op jit(solution)/shard_map/ppermute | solution.py:20
  175.5 0.0 collective-permute-start.4
  175.5 1.1 pick.15
  176.7 0.0 collective-permute-done.5.vy_ref
  176.7 1.1 collective-permute-done.4.vx_ref
  177.8 8.3 %shard_map.37 = (bf16[4,1024,1024]{2,1,0:T(8,128)(2,1)}, f32[8,128]{1,0:T(8,128)}) custom-call(s32[1]{0:T(128)} %bitcast.1.bit_ref, bf16[1024,2048]{1,0:T(8,128)(2,1)} %get-tuple-element.37.own_ref, f32[1024,1]{1,0:T(8,128)} %get-tuple-element.38.refs_0_.norm_ref, bf16[2048,128]{1,0:T(8,128)(2,1)} %collective-permute-done.2.second_ref.v4_ref, ...), custom_call_target="tpu_custom_call" | custom-call | tf_op jit(solution)/shard_map/pallas_call | solution.py:233
  186.1 2.9 collective-permute-done.1.second_ref.v4_ref
  189.1 1.0 copy-done
  190.1 1.1 pick.12
  191.2 1.3 collective-permute-start.6
  192.5 5.5 %collective-permute-done.10.v2_ref = bf16[2048,256]{1,0:T(8,128)(2,1)} collective-permute-done((bf16[2048,256]{1,0:T(8,128)(2,1)}, bf16[2048,256]{1,0:T(8,128)(2,1)}, u32[]{:S(2)}, u32[]{:S(2)}) %collective-permute-start.10) | collective-permute-done | bytes 1048608 | tf_op jit(solution)/shard_map/ppermute | solution.py:20
  198.0 0.0 collective-permute-start.11
  198.0 0.9 collective-permute-start.16
  198.9 1.3 pick.13
  200.3 1.0 collective-permute-start.8
  201.2 18.3 %collective-permute-done.6.v2_ref = bf16[2048,256]{1,0:T(8,128)(2,1)S(1)} collective-permute-done((bf16[2048,256]{1,0:T(8,128)(2,1)}, bf16[2048,256]{1,0:T(8,128)(2,1)S(1)}, u32[]{:S(2)}, u32[]{:S(2)}) %collective-permute-start.6) | collective-permute-done | bytes 1048608 | tf_op jit(solution)/shard_map/ppermute | solution.py:20
  219.5 0.0 collective-permute-start.7
  219.5 0.0 collective-permute-done.12.vy_ref
  219.5 0.0 collective-permute-done.11.vx_ref
  219.5 9.6 %shard_map.38 = (bf16[4,1024,1024]{2,1,0:T(8,128)(2,1)}, f32[8,128]{1,0:T(8,128)}) custom-call(s32[1]{0:T(128)} %bitcast.1.bit_ref, bf16[1024,2048]{1,0:T(8,128)(2,1)} %get-tuple-element.37.own_ref, f32[1024,1]{1,0:T(8,128)} %get-tuple-element.38.refs_0_.norm_ref, bf16[2048,256]{1,0:T(8,128)(2,1)} %copy-done.1, ...), custom_call_target="tpu_custom_call", output_to_operand_aliasing={{0}: (7, {})} | custom-call | tf_op jit(solution)/shard_map/pallas_call | solution.py:233
  229.1 0.0 collective-permute-done.16.second_ref.v4_ref
  229.1 1.0 copy-done.2
  230.1 2.0 pick.18
  232.1 1.8 collective-permute-start.17
  234.0 0.6 collective-permute-start
  234.6 2.0 pick.19
  236.6 0.1 collective-permute-start.19
  236.7 0.0 collective-permute-done.8.vy_ref
  236.7 9.2 %shard_map.39 = (bf16[4,1024,1024]{2,1,0:T(8,128)(2,1)}, f32[8,128]{1,0:T(8,128)}) custom-call(s32[1]{0:T(128)} %bitcast.1.bit_ref, bf16[1024,2048]{1,0:T(8,128)(2,1)} %get-tuple-element.37.own_ref, f32[1024,1]{1,0:T(8,128)} %get-tuple-element.38.refs_0_.norm_ref, bf16[2048,256]{1,0:T(8,128)(2,1)} %copy-done, ...), custom_call_target="tpu_custom_call", output_to_operand_aliasing={{0}: (7, {})} | custom-call | tf_op jit(solution)/shard_map/pallas_call | solution.py:233
  245.8 11.9 %collective-permute-done.17.v2_ref = bf16[2048,256]{1,0:T(8,128)(2,1)} collective-permute-done((bf16[2048,256]{1,0:T(8,128)(2,1)}, bf16[2048,256]{1,0:T(8,128)(2,1)}, u32[]{:S(2)}, u32[]{:S(2)}) %collective-permute-start.17) | collective-permute-done | bytes 1048608 | tf_op jit(solution)/shard_map/ppermute | solution.py:20
  257.7 0.8 copy-done.5
  258.5 1.5 pick.16
  260.1 2.1 collective-permute-start.13
  262.2 1.5 pick.17
  263.7 0.6 collective-permute-start.15
  264.3 10.7 %collective-permute-done.13.v2_ref = bf16[2048,128]{1,0:T(8,128)(2,1)S(1)} collective-permute-done((bf16[2048,128]{1,0:T(8,128)(2,1)}, bf16[2048,128]{1,0:T(8,128)(2,1)S(1)}, u32[]{:S(2)}, u32[]{:S(2)}) %collective-permute-start.13) | collective-permute-done | bytes 524320 | tf_op jit(solution)/shard_map/ppermute | solution.py:20
  275.0 0.0 collective-permute-start.14
  275.0 0.0 collective-permute-done.19.vy_ref
  275.0 1.0 copy-done.8
  276.0 9.1 %shard_map.40 = (bf16[4,1024,1024]{2,1,0:T(8,128)(2,1)}, f32[8,128]{1,0:T(8,128)}) custom-call(s32[1]{0:T(128)} %bitcast.1.bit_ref, bf16[1024,2048]{1,0:T(8,128)(2,1)} %get-tuple-element.37.own_ref, f32[1024,1]{1,0:T(8,128)} %get-tuple-element.38.refs_0_.norm_ref, bf16[2048,256]{1,0:T(8,128)(2,1)} %copy-done.2, ...), custom_call_target="tpu_custom_call", output_to_operand_aliasing={{0}: (7, {})} | custom-call | tf_op jit(solution)/shard_map/pallas_call | solution.py:233
  285.2 0.0 collective-permute-done.15.vy_ref
  285.2 0.8 copy-done.10
  286.0 0.2 copy-done.11
  286.2 8.3 %shard_map.41 = (bf16[4,1024,1024]{2,1,0:T(8,128)(2,1)}, f32[8,128]{1,0:T(8,128)}) custom-call(s32[1]{0:T(128)} %bitcast.1.bit_ref, bf16[1024,2048]{1,0:T(8,128)(2,1)} %get-tuple-element.37.own_ref, f32[1024,1]{1,0:T(8,128)} %get-tuple-element.38.refs_0_.norm_ref, bf16[2048,128]{1,0:T(8,128)(2,1)} %copy-done.5, ...), custom_call_target="tpu_custom_call", output_to_operand_aliasing={{0}: (7, {})} | custom-call | tf_op jit(solution)/shard_map/pallas_call | solution.py:233
  (28 shorter events, 0.1 us)
Async XLA Ops:
  0.0 16.1 %copy-start.12 = (s32[2,2048]{1,0:T(2,128)S(1)}, s32[2,2048]{1,0:T(2,128)}, u32[]{:S(2)}) copy-start(s32[2,2048]{1,0:T(2,128)} %param.6) | copy-start | bytes 49156
  0.0 16.1 %copy-start.13 = (s32[640]{0:T(1024)S(1)}, s32[640]{0:T(1024)}, u32[]{:S(2)}) copy-start(s32[640]{0:T(1024)} %param.7) | copy-start | bytes 7684
  8.6 80.5 %all-to-all-start.1 = ((s16[16,3,40,1024]{3,2,1,0:T(8,128)(2,1)}), s16[16,3,40,1024]{3,2,1,0:T(8,128)(2,1)}, u32[]{:S(2)}, u32[]{:S(2)}) async-start(s16[16,3,40,1024]{3,2,1,0:T(8,128)(2,1)} %split_blocks.1), calls=%async_computation.1 | async-start | bytes 7864320 | tf_op jit(solution)/shard_map/all_to_all | solution.py:303
  107.7 49.4 %copy-start.3 = (bf16[2048,256]{1,0:T(8,128)(2,1)}, bf16[2048,256]{1,0:T(8,128)(2,1)S(1)}, u32[]{:S(2)}) copy-start(bf16[2048,256]{1,0:T(8,128)(2,1)S(1)} %get-tuple-element.34.refs_2_.first_ref) | copy-start | bytes 3145732
  107.7 55.6 %collective-permute-start.9 = (bf16[2048,256]{1,0:T(8,128)(2,1)S(1)}, bf16[2048,256]{1,0:T(8,128)(2,1)S(1)}, u32[]{:S(2)}, u32[]{:S(2)}) collective-permute-start(bf16[2048,256]{1,0:T(8,128)(2,1)S(1)} %get-tuple-element.33.refs_1_.first_ref), channel_id=1, source_target_pairs={{0,4},{1,5},{2,6},{3,7},{4,8},{5,9},{6,10},{7,11},{8,12},{9,13},{1... | collective-permute-start | bytes 3145736 | tf_op jit(solution)/shard_map/ppermute | solution.py:20
  121.8 33.5 %collective-permute-start.2 = (bf16[2048,128]{1,0:T(8,128)(2,1)}, bf16[2048,128]{1,0:T(8,128)(2,1)}, u32[]{:S(2)}, u32[]{:S(2)}) collective-permute-start(bf16[2048,128]{1,0:T(8,128)(2,1)} %get-tuple-element.32.refs_0_.first_ref), channel_id=1, source_target_pairs={{0,4},{1,5},{2,6},{3,7},{4,8},{5,9},{6,10},{7,11},{8,12},{9,13},{1... | collective-permute-start | bytes 1572872 | tf_op jit(solution)/shard_map/ppermute | solution.py:20
  157.1 18.5 %collective-permute-start.3 = (bf16[2048,128]{1,0:T(8,128)(2,1)}, bf16[2048,128]{1,0:T(8,128)(2,1)}, u32[]{:S(2)}, u32[]{:S(2)}) collective-permute-start(bf16[2048,128]{1,0:T(8,128)(2,1)} %pick.10), channel_id=1, source_target_pairs={{0,2},{1,3},{2,0},{3,1},{4,6},{5,7},{6,4},{7,5},{8,10},{9,11},{10,... | collective-permute-start | bytes 1572872 | tf_op jit(solution)/shard_map/ppermute | solution.py:20
  162.4 26.6 %collective-permute-start.1 = (bf16[2048,256]{1,0:T(8,128)(2,1)}, bf16[2048,256]{1,0:T(8,128)(2,1)S(1)}, u32[]{:S(2)}, u32[]{:S(2)}) collective-permute-start(bf16[2048,256]{1,0:T(8,128)(2,1)} %copy-done.3), channel_id=1, source_target_pairs={{0,4},{1,5},{2,6},{3,7},{4,8},{5,9},{6,10},{7,11},{8,12},{9,13},{1... | collective-permute-start | bytes 3145736 | tf_op jit(solution)/shard_map/ppermute | solution.py:20
  163.3 1.0 copy-start.1
  165.5 24.6 %copy-start.4 = (bf16[2048,256]{1,0:T(8,128)(2,1)S(1)}, bf16[2048,256]{1,0:T(8,128)(2,1)}, u32[]{:S(2)}) copy-start(bf16[2048,256]{1,0:T(8,128)(2,1)} %copy-done.3) | copy-start | bytes 3145732
  165.5 32.5 %collective-permute-start.10 = (bf16[2048,256]{1,0:T(8,128)(2,1)}, bf16[2048,256]{1,0:T(8,128)(2,1)}, u32[]{:S(2)}, u32[]{:S(2)}) collective-permute-start(bf16[2048,256]{1,0:T(8,128)(2,1)} %pick.14), channel_id=1, source_target_pairs={{0,2},{1,3},{2,0},{3,1},{4,6},{5,7},{6,4},{7,5},{8,10},{9,11},{10,... | collective-permute-start | bytes 3145736 | tf_op jit(solution)/shard_map/ppermute | solution.py:20
  168.4 8.3 %collective-permute-start.5 = (bf16[2048,128]{1,0:T(8,128)(2,1)}, bf16[2048,128]{1,0:T(8,128)(2,1)}, u32[]{:S(2)}, u32[]{:S(2)}) collective-permute-start(bf16[2048,128]{1,0:T(8,128)(2,1)} %pick.11), channel_id=1, source_target_pairs={{0,1},{1,0},{2,3},{3,2},{4,5},{5,4},{6,7},{7,6},{8,9},{9,8},{10,11... | collective-permute-start | bytes 1572872 | tf_op jit(solution)/shard_map/ppermute | solution.py:20
  175.5 2.3 collective-permute-start.4
  189.0 1.0 copy-start
  191.2 28.3 %collective-permute-start.6 = (bf16[2048,256]{1,0:T(8,128)(2,1)}, bf16[2048,256]{1,0:T(8,128)(2,1)S(1)}, u32[]{:S(2)}, u32[]{:S(2)}) collective-permute-start(bf16[2048,256]{1,0:T(8,128)(2,1)} %pick.12), channel_id=1, source_target_pairs={{0,2},{1,3},{2,0},{3,1},{4,6},{5,7},{6,4},{7,5},{8,10},{9,11},{10,... | collective-permute-start | bytes 3145736 | tf_op jit(solution)/shard_map/ppermute | solution.py:20
  192.5 27.0 %collective-permute-start.12 = (bf16[2048,256]{1,0:T(8,128)(2,1)}, bf16[2048,256]{1,0:T(8,128)(2,1)}, u32[]{:S(2)}, u32[]{:S(2)}) collective-permute-start(bf16[2048,256]{1,0:T(8,128)(2,1)} %pick.15), channel_id=1, source_target_pairs={{0,1},{1,0},{2,3},{3,2},{4,5},{5,4},{6,7},{7,6},{8,9},{9,8},{10,11... | collective-permute-start | bytes 3145736 | tf_op jit(solution)/shard_map/ppermute | solution.py:20
  198.0 21.5 %collective-permute-start.11 = (bf16[2048,256]{1,0:T(8,128)(2,1)}, bf16[2048,256]{1,0:T(8,128)(2,1)}, u32[]{:S(2)}, u32[]{:S(2)}) collective-permute-start(bf16[2048,256]{1,0:T(8,128)(2,1)} %collective-permute-done.10.v2_ref), channel_id=1, source_target_pairs={{0,1},{1,0},{2,3},{3,2},{4,5},{5,4},{6,7},{7,6},{8,9},{9,8},{10,11... | collective-permute-start | bytes 3145736 | tf_op jit(solution)/shard_map/ppermute | solution.py:20
  198.0 31.1 %collective-permute-start.16 = (bf16[2048,256]{1,0:T(8,128)(2,1)}, bf16[2048,256]{1,0:T(8,128)(2,1)S(1)}, u32[]{:S(2)}, u32[]{:S(2)}) collective-permute-start(bf16[2048,256]{1,0:T(8,128)(2,1)} %get-tuple-element.35.refs_3_.first_ref), channel_id=1, source_target_pairs={{0,4},{1,5},{2,6},{3,7},{4,8},{5,9},{6,10},{7,11},{8,12},{9,13},{1... | collective-permute-start | bytes 3145736 | tf_op jit(solution)/shard_map/ppermute | solution.py:20
  200.3 36.4 %collective-permute-start.8 = (bf16[2048,256]{1,0:T(8,128)(2,1)}, bf16[2048,256]{1,0:T(8,128)(2,1)}, u32[]{:S(2)}, u32[]{:S(2)}) collective-permute-start(bf16[2048,256]{1,0:T(8,128)(2,1)} %pick.13), channel_id=1, source_target_pairs={{0,1},{1,0},{2,3},{3,2},{4,5},{5,4},{6,7},{7,6},{8,9},{9,8},{10,11... | collective-permute-start | bytes 3145736 | tf_op jit(solution)/shard_map/ppermute | solution.py:20
  219.5 9.6 %copy-start.7 = (bf16[2048,256]{1,0:T(8,128)(2,1)}, bf16[2048,256]{1,0:T(8,128)(2,1)S(1)}, u32[]{:S(2)}) copy-start(bf16[2048,256]{1,0:T(8,128)(2,1)S(1)} %collective-permute-done.6.v2_ref) | copy-start | bytes 3145732
  219.5 17.2 %collective-permute-start.7 = (bf16[2048,256]{1,0:T(8,128)(2,1)S(1)}, bf16[2048,256]{1,0:T(8,128)(2,1)}, u32[]{:S(2)}, u32[]{:S(2)}) collective-permute-start(bf16[2048,256]{1,0:T(8,128)(2,1)S(1)} %collective-permute-done.6.v2_ref), channel_id=1, source_target_pairs={{0,1},{1,0},{2,3},{3,2},{4,5},{5,4},{6,7},{7,6},{8,9},{9,8},{10,11... | collective-permute-start | bytes 3145736 | tf_op jit(solution)/shard_map/ppermute | solution.py:20
  219.5 14.4 %copy-start.6 = (bf16[2048,128]{1,0:T(8,128)(2,1)S(1)}, bf16[2048,128]{1,0:T(8,128)(2,1)}, u32[]{:S(2)}) copy-start(bf16[2048,128]{1,0:T(8,128)(2,1)} %get-tuple-element.36.refs_4_.first_ref) | copy-start | bytes 1572868
  229.1 1.0 copy-start.2
  232.1 25.6 %collective-permute-start.17 = (bf16[2048,256]{1,0:T(8,128)(2,1)}, bf16[2048,256]{1,0:T(8,128)(2,1)}, u32[]{:S(2)}, u32[]{:S(2)}) collective-permute-start(bf16[2048,256]{1,0:T(8,128)(2,1)} %pick.18), channel_id=1, source_target_pairs={{0,2},{1,3},{2,0},{3,1},{4,6},{5,7},{6,4},{7,5},{8,10},{9,11},{10,... | collective-permute-start | bytes 3145736 | tf_op jit(solution)/shard_map/ppermute | solution.py:20
  234.0 23.8 %collective-permute-start = (bf16[2048,128]{1,0:T(8,128)(2,1)S(1)}, bf16[2048,128]{1,0:T(8,128)(2,1)S(1)}, u32[]{:S(2)}, u32[]{:S(2)}) collective-permute-start(bf16[2048,128]{1,0:T(8,128)(2,1)S(1)} %copy-done.6), channel_id=1, source_target_pairs={{0,4},{1,5},{2,6},{3,7},{4,8},{5,9},{6,10},{7,11},{8,12},{9,13},{1... | collective-permute-start | bytes 1572872 | tf_op jit(solution)/shard_map/ppermute | solution.py:20
  236.6 38.4 %collective-permute-start.19 = (bf16[2048,256]{1,0:T(8,128)(2,1)}, bf16[2048,256]{1,0:T(8,128)(2,1)}, u32[]{:S(2)}, u32[]{:S(2)}) collective-permute-start(bf16[2048,256]{1,0:T(8,128)(2,1)} %pick.19), channel_id=1, source_target_pairs={{0,1},{1,0},{2,3},{3,2},{4,5},{5,4},{6,7},{7,6},{8,9},{9,8},{10,11... | collective-permute-start | bytes 3145736 | tf_op jit(solution)/shard_map/ppermute | solution.py:20
  257.7 17.3 %collective-permute-start.18 = (bf16[2048,256]{1,0:T(8,128)(2,1)}, bf16[2048,256]{1,0:T(8,128)(2,1)S(1)}, u32[]{:S(2)}, u32[]{:S(2)}) collective-permute-start(bf16[2048,256]{1,0:T(8,128)(2,1)} %collective-permute-done.17.v2_ref), channel_id=1, source_target_pairs={{0,1},{1,0},{2,3},{3,2},{4,5},{5,4},{6,7},{7,6},{8,9},{9,8},{10,11... | collective-permute-start | bytes 3145736 | tf_op jit(solution)/shard_map/ppermute | solution.py:20
  257.7 0.8 copy-start.5
  260.1 14.9 %collective-permute-start.13 = (bf16[2048,128]{1,0:T(8,128)(2,1)}, bf16[2048,128]{1,0:T(8,128)(2,1)S(1)}, u32[]{:S(2)}, u32[]{:S(2)}) collective-permute-start(bf16[2048,128]{1,0:T(8,128)(2,1)} %pick.16), channel_id=1, source_target_pairs={{0,2},{1,3},{2,0},{3,1},{4,6},{5,7},{6,4},{7,5},{8,10},{9,11},{10,... | collective-permute-start | bytes 1572872 | tf_op jit(solution)/shard_map/ppermute | solution.py:20
  263.7 21.5 %collective-permute-start.15 = (bf16[2048,128]{1,0:T(8,128)(2,1)}, bf16[2048,128]{1,0:T(8,128)(2,1)S(1)}, u32[]{:S(2)}, u32[]{:S(2)}) collective-permute-start(bf16[2048,128]{1,0:T(8,128)(2,1)} %pick.17), channel_id=1, source_target_pairs={{0,1},{1,0},{2,3},{3,2},{4,5},{5,4},{6,7},{7,6},{8,9},{9,8},{10,11... | collective-permute-start | bytes 1572872 | tf_op jit(solution)/shard_map/ppermute | solution.py:20
  275.0 10.2 %copy-start.9 = (bf16[2048,128]{1,0:T(8,128)(2,1)}, bf16[2048,128]{1,0:T(8,128)(2,1)S(1)}, u32[]{:S(2)}) copy-start(bf16[2048,128]{1,0:T(8,128)(2,1)S(1)} %collective-permute-done.13.v2_ref) | copy-start | bytes 1572868
  275.0 10.2 %collective-permute-start.14 = (bf16[2048,128]{1,0:T(8,128)(2,1)S(1)}, bf16[2048,128]{1,0:T(8,128)(2,1)S(1)}, u32[]{:S(2)}, u32[]{:S(2)}) collective-permute-start(bf16[2048,128]{1,0:T(8,128)(2,1)S(1)} %collective-permute-done.13.v2_ref), channel_id=1, source_target_pairs={{0,1},{1,0},{2,3},{3,2},{4,5},{5,4},{6,7},{7,6},{8,9},{9,8},{10,11... | collective-permute-start | bytes 1572872 | tf_op jit(solution)/shard_map/ppermute | solution.py:20
  275.0 1.0 copy-start.8
  285.2 0.8 copy-start.10
  285.2 1.0 copy-start.11

commit v3 on v2

--- a/solution.py
+++ b/solution.py
@@ -10,7 +10,7 @@
 
 
 ROUNDS = 4
-VMEM_BYTES = 58 * 1024 * 1024
+VMEM_BYTES = 24 * 1024 * 1024
 UNIT = 1.0 / 512.0
 BAD = -32768
 
@@ -185,6 +185,7 @@
         out_shape=jax.ShapeDtypeStruct(first.shape, first.dtype),
         scratch_shapes=[pltpu.VMEM(first.shape, first.dtype), pltpu.SemaphoreType.DMA((4,)),
                         pltpu.SemaphoreType.DMA((4,))],
+        compiler_params=pltpu.CompilerParams(vmem_limit_bytes=VMEM_BYTES // 4),
         name="pick",
     )(flag, first, second, *after)
 
@@ -248,6 +249,58 @@
     )(*args)
 
 
+def half_kernel(places_ref, own_ref, norm_ref, first_ref, second_ref, *refs, aliased):
+    refs = refs[1:] if aliased else refs
+    out_ref, token_ref, vnorm_ref = refs
+    token_ref[...] = jnp.zeros_like(token_ref)
+    for which, ref in enumerate((first_ref, second_ref)):
+        @pl.when(pl.program_id(0) == which)
+        def _():
+            @pl.when(pl.program_id(1) == 0)
+            def _():
+                wide = ref[...].astype(jnp.float32)
+                vnorm_ref[0:1, :] = jnp.sum(wide * wide, axis=0, keepdims=True)
+
+            inter = jnp.dot(own_ref[...], ref[...], preferred_element_type=jnp.float32)
+            ratio = inter / (norm_ref[...] + vnorm_ref[0:1, :] - inter + 1e-06)
+            out_ref[0] = (1.0 - ratio).astype(jnp.bfloat16)
+
+
+def distance_half(places, own, norms, first, second, out, start):
+    frames, contacts = own.shape
+    width = first.shape[1]
+    tile = 512
+    block = start // width
+    aliased = out is not None
+    in_specs = [
+        pl.BlockSpec((tile, contacts), lambda r, i, p: (i, 0)),
+        pl.BlockSpec((tile, 1), lambda r, i, p: (i, 0)),
+    ] + [pl.BlockSpec((contacts, width), lambda r, i, p: (0, 0))] * 2
+    args = [own, norms, first, second]
+    if aliased:
+        in_specs.append(pl.BlockSpec(memory_space=pl.ANY))
+        args.append(out)
+    return pl.pallas_call(
+        functools.partial(half_kernel, aliased=aliased),
+        grid_spec=pltpu.PrefetchScalarGridSpec(
+            num_scalar_prefetch=1,
+            grid=(2, frames // tile),
+            in_specs=in_specs,
+            out_specs=[
+                pl.BlockSpec((1, tile, width), lambda r, i, p: (p[r], i, block)),
+                pl.BlockSpec((8, 128), lambda r, i, p: (0, 0)),
+            ],
+            scratch_shapes=[pltpu.VMEM((8, width), jnp.float32)],
+        ),
+        out_shape=[
+            jax.ShapeDtypeStruct((ROUNDS, frames, frames), jnp.bfloat16),
+            jax.ShapeDtypeStruct((8, 128), jnp.float32),
+        ],
+        input_output_aliases={5: 0} if aliased else {},
+        compiler_params=pltpu.CompilerParams(vmem_limit_bytes=VMEM_BYTES),
+    )(places, *args)
+
+
 def contact_slots(pairs, res_slot):
     hits = pairs[:, :, None] == res_slot[None, None, :]
     places = jnp.arange(res_slot.shape[0], dtype=jnp.int32)
@@ -286,7 +339,7 @@
 def split_blocks(coords, count):
     _, rows, frames = coords.shape
     per_block = frames // count
-    per_step = 2 if count % 2 == 0 else 1
+    per_step = largest_divisor(count, 4)
     return pl.pallas_call(
         split_kernel,
         grid=(count // per_step,),
@@ -294,7 +347,7 @@
         out_specs=pl.BlockSpec((count, 3, rows, per_block), lambda i: (0, 0, 0, 0)),
         out_shape=jax.ShapeDtypeStruct((count, 3, rows, per_block), jnp.int16),
         scratch_shapes=[pltpu.VMEM((rows, per_block), jnp.float32), pltpu.VMEM((1, 1), jnp.float32)],
-        compiler_params=pltpu.CompilerParams(vmem_limit_bytes=VMEM_BYTES),
+        compiler_params=pltpu.CompilerParams(vmem_limit_bytes=58 * 1024 * 1024),
         name="split_blocks",
     )(coords)
 
@@ -326,8 +379,8 @@
 def shards(coords, pairs, res_slot):
     index = lax.axis_index("blocks")
     lanes = coords.shape[2] // lax.axis_size("blocks") // 8
-    widths = [lanes * n for n in (1, 2, 2, 2, 1)]
-    starts = [lanes * n for n in (0, 2, 4, 6, 1)]
+    widths = [lanes * n for n in (1, 1, 2, 2, 2)]
+    starts = [lanes * n for n in (0, 1, 2, 4, 6)]
 
     slots24 = contact_slots(pairs, res_slot) * 24
     fts = contact_features(coords, slots24, starts, widths)
@@ -350,7 +403,15 @@
         sent = pick(low_core, ft, v4, [])
         vy = permuted(sent, "blocks", swap1)
         vx = permuted(v2, "blocks", swap1)
-        out, token = distance_chunk(bit, own, norms, v4, v2, vx, vy, out, starts[j])
+        if j + 1 < len(fts):
+            out, token = distance_chunk(bit, own, norms, v4, v2, vx, vy, out, starts[j])
+        else:
+            three = jnp.full((1,), 3, jnp.int32)
+            one = jnp.full((1,), 1, jnp.int32)
+            places = jnp.concatenate([three, 2 - 2 * bit])
+            out, token = distance_half(places, own, norms, v4, vy, out, starts[j])
+            places = jnp.concatenate([one, 2 * bit])
+            out, token = distance_half(places, own, norms, v2, vx, out, starts[j])
         tokens.append(token)
     return out
 

time: 295 us -> 275 us (0.932)
  Pallas kernels: 90.4 us -> 70.5 us
  waiting for transfers between devices: 154 us -> 164 us
  starting transfers between devices: 40.6 us -> 32.1 us
    pallas_call x5 -> x4, Pallas kernels: 44.5 us -> 25.9 us  [distance_chunk(): pl.pallas_call(functools.partial(distance_kernel, aliased=aliased), grid=...]
    ppermute x20, waiting for transfers between devices: 82.4 us -> 92.5 us  [permuted(): return lax.ppermute(shard, axis, [(i, to(i, count)) for i in range(count)])]
    pallas_call x0 -> x2, Pallas kernels: none -> 9.19 us  [distance_half(): pl.pallas_call(functools.partial(half_kernel, aliased=aliased), grid_spec...]
    ppermute x20, starting transfers between devices: 33.1 us -> 24.7 us  [permuted(): return lax.ppermute(shard, axis, [(i, to(i, count)) for i in range(count)])]
    pallas_call x10, Pallas kernels: 15.4 us -> 7.82 us  [pick(): pl.pallas_call(pick_kernel, in_specs=[pl.BlockSpec(memory_space=pltpu.SME...]
  transfers between devices with their start and end apart: 21 -> 21, of which waited for: 9 -> 13; matrix products, arithmetic and copies ran while one was open for 1% -> 1% of each run, Pallas kernels for 19% -> 15%
where the time goes in v3:
time: 275 us
  waiting for transfers between devices  164 us (60%)
  Pallas kernels  70.5 us (26%)
  starting transfers between devices  32.1 us (12%)
  local copies, waits for them, and re-layouts  4.23 us (2%)
  other arithmetic  3.21 us (1%)
    ppermute x20, waiting for transfers between devices, permuted(): return lax.ppermute(shard, axis, [(i, to(i, count)) for i in range(count)])  92.5 us
    all_to_all x1, waiting for transfers between devices, exchanged(): lax.all_to_all(pieces, 'blocks', split_axis=0, concat_axis=0, tiled=True)  71.3 us
    pallas_call x4, Pallas kernels, distance_chunk(): pl.pallas_call(functools.partial(distance_kernel, aliased=aliased), grid=...  25.9 us
    ppermute x20, starting transfers between devices, permuted(): return lax.ppermute(shard, axis, [(i, to(i, count)) for i in range(count)])  24.7 us
    pallas_call x1, Pallas kernels, features_of(): pl.pallas_call(functools.partial(features_kernel, steps=steps, tile=tile,...  16.6 us
    pallas_call x2, Pallas kernels, distance_half(): pl.pallas_call(functools.partial(half_kernel, aliased=aliased), grid_spec...  9.19 us
    pallas_call x10, Pallas kernels, pick(): pl.pallas_call(pick_kernel, in_specs=[pl.BlockSpec(memory_space=pltpu.SME...  7.82 us
    all_to_all x1, starting transfers between devices, exchanged(): lax.all_to_all(pieces, 'blocks', split_axis=0, concat_axis=0, tiled=True)  7.46 us
  transfers between devices with their start and end apart: 21, of which 13 were waited for; matrix products, arithmetic and copies ran while one was open for 1% of the time, Pallas kernels for 15%

profile of v3, /device:TPU:0, one launch (start us, length us, event | category | flops | bytes accessed | tf_op | source)
XLA Modules:
  0.0 274.8 jit_solution(8249574271270224658)
XLA Ops:
  0.0 7.0 %split_blocks.1 = s16[16,3,40,1024]{3,2,1,0:T(8,128)(2,1)} custom-call(f32[3,40,16384]{2,1,0:T(8,128)} %bitcast.10), custom_call_target="tpu_custom_call" | custom-call | tf_op jit(solution)/shard_map/split_blocks/pallas_call | solution.py:343
  7.0 7.5 %all-to-all-start.1 = ((s16[16,3,40,1024]{3,2,1,0:T(8,128)(2,1)}), s16[16,3,40,1024]{3,2,1,0:T(8,128)(2,1)}, u32[]{:S(2)}, u32[]{:S(2)}) async-start(s16[16,3,40,1024]{3,2,1,0:T(8,128)(2,1)} %split_blocks.1), calls=%async_computation.1 | async-start | bytes 7864320 | tf_op jit(solution)/shard_map/all_to_all | solution.py:356
  14.5 1.6 select_reduce_fusion
  16.1 71.3 %all-to-all-done.1 = s16[16,3,40,1024]{3,2,1,0:T(8,128)(2,1)} async-done(((s16[16,3,40,1024]{3,2,1,0:T(8,128)(2,1)}), s16[16,3,40,1024]{3,2,1,0:T(8,128)(2,1)}, u32[]{:S(2)}, u32[]{:S(2)}) %all-to-all-start.1) | async-done | bytes 3932192 | tf_op jit(solution)/shard_map/all_to_all | solution.py:356
  87.4 1.4 compare_reduce_fusion
  89.5 16.6 %conditional.1 = ((bf16[2048,128]{1,0:T(8,128)(2,1)}, bf16[2048,128]{1,0:T(8,128)(2,1)}, bf16[2048,256]{1,0:T(8,128)(2,1)S(1)}, bf16[2048,256]{1,0:T(8,128)(2,1)S(1)}, bf16[2048,256]{1,0:T(8,128)(2,1)})) conditional(s32[]{:T(128)} %convert_element_type.3, (f32[40,3,16384]{2,0,1:T(8,128)}, s32[2,2048]{1,0:T(2,128)S(1)}) %tuple.11, ...), branch_computations={%region_2.3_spmd, %region_3.4_spmd} | conditional | bytes 31457288 | solution.py:376
  89.5 16.6 %features.3 = (bf16[2048,128]{1,0:T(8,128)(2,1)}, bf16[2048,128]{1,0:T(8,128)(2,1)}, bf16[2048,256]{1,0:T(8,128)(2,1)S(1)}, bf16[2048,256]{1,0:T(8,128)(2,1)S(1)}, bf16[2048,256]{1,0:T(8,128)(2,1)}) custom-call(s32[2,2048]{1,0:T(2,128)S(1)} %get-tuple-element.15.slots_ref, s16[16,3,40,1024]{3,2,1,0:T(8,128)(2,1)} %get-tuple-element.16.x_ref), custom_call_target="tpu_custom_call" | custom-call | tf_op jit(solution)/shard_map/cond/branch_1_fun/features/pallas_call | solution.py:98
  106.1 14.1 %collective-permute-start.2 = (bf16[2048,128]{1,0:T(8,128)(2,1)}, bf16[2048,128]{1,0:T(8,128)(2,1)S(1)}, u32[]{:S(2)}, u32[]{:S(2)}) collective-permute-start(bf16[2048,128]{1,0:T(8,128)(2,1)} %get-tuple-element.33.refs_0_.first_ref), channel_id=1, source_target_pairs={{0,4},{1,5},{2,6},{3,7},{4,8},{5,9},{6,10},{7,11},{8,12},{9,13},{1... | collective-permute-start | bytes 1572872 | tf_op jit(solution)/shard_map/ppermute | solution.py:20
  120.2 4.0 %own_features.1 = (bf16[1024,2048]{1,0:T(8,128)(2,1)S(1)}, f32[1024,1]{1,0:T(8,128)S(1)}) custom-call(bf16[2048,128]{1,0:T(8,128)(2,1)} %get-tuple-element.33.refs_0_.first_ref, bf16[2048,128]{1,0:T(8,128)(2,1)} %get-tuple-element.34.refs_1_.first_ref, bf16[2048,256]{1,0:T(8,128)(2,1)S(1)} %get-tuple-element.35.refs_2_.first_ref, ...), custom_call_target="tpu_custom_call" | custom-call | tf_op jit(solution)/shard_map/own_features/pallas_call | solution.py:137
  124.2 0.0 copy-start
  124.3 2.0 copy-done
  126.3 5.1 %collective-permute-done.2.second_ref.v4_ref = bf16[2048,128]{1,0:T(8,128)(2,1)S(1)} collective-permute-done((bf16[2048,128]{1,0:T(8,128)(2,1)}, bf16[2048,128]{1,0:T(8,128)(2,1)S(1)}, u32[]{:S(2)}, u32[]{:S(2)}) %collective-permute-start.2) | collective-permute-done | bytes 524320 | tf_op jit(solution)/shard_map/ppermute | solution.py:20
  131.4 1.6 pick.10
  133.0 5.0 %collective-permute-start.3 = (bf16[2048,128]{1,0:T(8,128)(2,1)S(1)}, bf16[2048,128]{1,0:T(8,128)(2,1)S(1)}, u32[]{:S(2)}, u32[]{:S(2)}) collective-permute-start(bf16[2048,128]{1,0:T(8,128)(2,1)S(1)} %pick.10), channel_id=1, source_target_pairs={{0,2},{1,3},{2,0},{3,1},{4,6},{5,7},{6,4},{7,5},{8,10},{9,11},{10,... | collective-permute-start | bytes 1572872 | tf_op jit(solution)/shard_map/ppermute | solution.py:20
  138.1 0.9 collective-permute-start.1
  139.0 1.7 pick.11
  140.7 0.1 collective-permute-start.5
  140.8 9.2 %collective-permute-done.3.v2_ref = bf16[2048,128]{1,0:T(8,128)(2,1)S(1)} collective-permute-done((bf16[2048,128]{1,0:T(8,128)(2,1)S(1)}, bf16[2048,128]{1,0:T(8,128)(2,1)S(1)}, u32[]{:S(2)}, u32[]{:S(2)}) %collective-permute-start.3) | collective-permute-done | bytes 524320 | tf_op jit(solution)/shard_map/ppermute | solution.py:20
  150.0 0.0 collective-permute-start.4
  150.0 0.0 collective-permute-done.5.vy_ref
  150.0 1.9 collective-permute-done.4.vx_ref
  151.9 2.2 copy-done.1
  154.1 6.4 %shard_map.37 = (bf16[4,1024,1024]{2,1,0:T(8,128)(2,1)}, f32[8,128]{1,0:T(8,128)S(1)}) custom-call(s32[1]{0:T(128)} %bitcast.1.bit_ref, bf16[1024,2048]{1,0:T(8,128)(2,1)S(1)} %copy-done.1, f32[1024,1]{1,0:T(8,128)S(1)} %get-tuple-element.39.refs_0_.norm_ref, bf16[2048,128]{1,0:T(8,128)(2,1)S(1)} %collective-permute-done.2.second_ref.v4_ref, ...), custom_call_target="tpu_custom_call" | custom-call | tf_op jit(solution)/shard_map/pallas_call | solution.py:234
  160.5 4.2 %collective-permute-done.1.second_ref.v4_ref = bf16[2048,256]{1,0:T(8,128)(2,1)S(1)} collective-permute-done((bf16[2048,256]{1,0:T(8,128)(2,1)}, bf16[2048,256]{1,0:T(8,128)(2,1)S(1)}, u32[]{:S(2)}, u32[]{:S(2)}) %collective-permute-start.1) | collective-permute-done | bytes 1048608 | tf_op jit(solution)/shard_map/ppermute | solution.py:20
  164.7 0.2 pick.12
  164.9 0.4 collective-permute-start.6
  165.3 0.0 collective-permute-start.9
  165.3 14.3 %collective-permute-done.9.second_ref.v4_ref = bf16[2048,128]{1,0:T(8,128)(2,1)S(1)} collective-permute-done((bf16[2048,128]{1,0:T(8,128)(2,1)S(1)}, bf16[2048,128]{1,0:T(8,128)(2,1)S(1)}, u32[]{:S(2)}, u32[]{:S(2)}) %collective-permute-start.9) | collective-permute-done | bytes 524320 | tf_op jit(solution)/shard_map/ppermute | solution.py:20
  179.7 1.4 pick.14
  181.1 1.5 collective-permute-start.10
  182.5 1.4 pick.15
  183.9 0.1 collective-permute-start.12
  184.0 0.1 collective-permute-start.16
  184.1 0.2 pick.13
  184.4 0.5 collective-permute-start.8
  184.8 6.2 %collective-permute-done.6.v2_ref = bf16[2048,256]{1,0:T(8,128)(2,1)S(1)} collective-permute-done((bf16[2048,256]{1,0:T(8,128)(2,1)S(1)}, bf16[2048,256]{1,0:T(8,128)(2,1)S(1)}, u32[]{:S(2)}, u32[]{:S(2)}) %collective-permute-start.6) | collective-permute-done | bytes 1048608 | tf_op jit(solution)/shard_map/ppermute | solution.py:20
  191.0 0.0 collective-permute-start.7
  191.0 8.9 %collective-permute-done.10.v2_ref = bf16[2048,128]{1,0:T(8,128)(2,1)S(1)} collective-permute-done((bf16[2048,128]{1,0:T(8,128)(2,1)S(1)}, bf16[2048,128]{1,0:T(8,128)(2,1)S(1)}, u32[]{:S(2)}, u32[]{:S(2)}) %collective-permute-start.10) | collective-permute-done | bytes 524320 | tf_op jit(solution)/shard_map/ppermute | solution.py:20
  200.0 0.0 collective-permute-start
  200.0 0.1 collective-permute-start.11
  200.1 1.9 collective-permute-done.11.vx_ref
  202.0 6.4 %shard_map.38 = (bf16[4,1024,1024]{2,1,0:T(8,128)(2,1)}, f32[8,128]{1,0:T(8,128)S(1)}) custom-call(s32[1]{0:T(128)} %bitcast.1.bit_ref, bf16[1024,2048]{1,0:T(8,128)(2,1)S(1)} %copy-done.1, f32[1024,1]{1,0:T(8,128)S(1)} %get-tuple-element.39.refs_0_.norm_ref, ...), custom_call_target="tpu_custom_call", output_to_operand_aliasing={{0}: (7, {})} | custom-call | tf_op jit(solution)/shard_map/pallas_call | solution.py:234
  208.4 3.6 %collective-permute-done.16.second_ref.v4_ref = bf16[2048,256]{1,0:T(8,128)(2,1)S(1)} collective-permute-done((bf16[2048,256]{1,0:T(8,128)(2,1)S(1)}, bf16[2048,256]{1,0:T(8,128)(2,1)S(1)}, u32[]{:S(2)}, u32[]{:S(2)}) %collective-permute-start.16) | collective-permute-done | bytes 1048608 | tf_op jit(solution)/shard_map/ppermute | solution.py:20
  211.9 0.2 pick.18
  212.2 0.7 collective-permute-start.17
  212.9 0.0 collective-permute-done.8.vy_ref
  212.9 0.0 collective-permute-done.7.vx_ref
  212.9 6.5 %shard_map.39 = (bf16[4,1024,1024]{2,1,0:T(8,128)(2,1)}, f32[8,128]{1,0:T(8,128)S(1)}) custom-call(s32[1]{0:T(128)} %bitcast.1.bit_ref, bf16[1024,2048]{1,0:T(8,128)(2,1)S(1)} %copy-done.1, f32[1024,1]{1,0:T(8,128)S(1)} %get-tuple-element.39.refs_0_.norm_ref, ...), custom_call_target="tpu_custom_call", output_to_operand_aliasing={{0}: (7, {})} | custom-call | tf_op jit(solution)/shard_map/pallas_call | solution.py:234
  219.4 14.5 %collective-permute-done.second_ref.first_ref = bf16[2048,256]{1,0:T(8,128)(2,1)S(1)} collective-permute-done((bf16[2048,256]{1,0:T(8,128)(2,1)S(1)}, bf16[2048,256]{1,0:T(8,128)(2,1)S(1)}, u32[]{:S(2)}, u32[]{:S(2)}) %collective-permute-start) | collective-permute-done | bytes 1048608 | tf_op jit(solution)/shard_map/ppermute | solution.py:20
  233.9 0.2 pick.16
  234.1 0.7 collective-permute-start.13
  234.8 0.2 pick.19
  235.0 0.1 collective-permute-start.19
  235.1 1.2 collective-permute-done.17.v2_ref
  236.3 0.5 pick.17
  236.8 0.6 collective-permute-start.15
  237.4 21.4 %collective-permute-done.13.first_ref = bf16[2048,256]{1,0:T(8,128)(2,1)S(1)} collective-permute-done((bf16[2048,256]{1,0:T(8,128)(2,1)S(1)}, bf16[2048,256]{1,0:T(8,128)(2,1)S(1)}, u32[]{:S(2)}, u32[]{:S(2)}) %collective-permute-start.13) | collective-permute-done | bytes 1048608 | tf_op jit(solution)/shard_map/ppermute | solution.py:20
  258.8 0.0 collective-permute-start.14
  258.8 0.1 pad_add_fusion.places_ref
  258.9 0.1 pad_add_fusion.1.places_ref
  259.0 0.0 collective-permute-done.18.vx_ref
  259.0 6.6 %shard_map.40 = (bf16[4,1024,1024]{2,1,0:T(8,128)(2,1)}, f32[8,128]{1,0:T(8,128)}) custom-call(s32[1]{0:T(128)} %bitcast.1.bit_ref, bf16[1024,2048]{1,0:T(8,128)(2,1)S(1)} %copy-done.1, f32[1024,1]{1,0:T(8,128)S(1)} %get-tuple-element.39.refs_0_.norm_ref, ...), custom_call_target="tpu_custom_call", output_to_operand_aliasing={{0}: (7, {})} | custom-call | tf_op jit(solution)/shard_map/pallas_call | solution.py:234
  265.6 4.6 %shard_map.41 = (bf16[4,1024,1024]{2,1,0:T(8,128)(2,1)}, f32[8,128]{1,0:T(8,128)}) custom-call(s32[2]{0:T(128)S(1)} %pad_add_fusion.1.places_ref, bf16[1024,2048]{1,0:T(8,128)(2,1)S(1)} %copy-done.1, f32[1024,1]{1,0:T(8,128)S(1)} %get-tuple-element.39.refs_0_.norm_ref, ...), custom_call_target="tpu_custom_call", output_to_operand_aliasing={{0}: (5, {})} | custom-call | tf_op jit(solution)/shard_map/pallas_call | solution.py:283
  270.2 4.6 %shard_map.42 = (bf16[4,1024,1024]{2,1,0:T(8,128)(2,1)}, f32[8,128]{1,0:T(8,128)}) custom-call(s32[2]{0:T(128)S(1)} %pad_add_fusion.places_ref, bf16[1024,2048]{1,0:T(8,128)(2,1)S(1)} %copy-done.1, f32[1024,1]{1,0:T(8,128)S(1)} %get-tuple-element.39.refs_0_.norm_ref, ...), custom_call_target="tpu_custom_call", output_to_operand_aliasing={{0}: (5, {})} | custom-call | tf_op jit(solution)/shard_map/pallas_call | solution.py:283
  (23 shorter events, 0.1 us)
Async XLA Ops:
  0.0 14.5 %copy-start.8 = (s32[2,2048]{1,0:T(2,128)S(1)}, s32[2,2048]{1,0:T(2,128)}, u32[]{:S(2)}) copy-start(s32[2,2048]{1,0:T(2,128)} %param.6) | copy-start | bytes 49156
  0.0 14.5 %copy-start.9 = (s32[640]{0:T(1024)S(1)}, s32[640]{0:T(1024)}, u32[]{:S(2)}) copy-start(s32[640]{0:T(1024)} %param.7) | copy-start | bytes 7684
  7.0 80.5 %all-to-all-start.1 = ((s16[16,3,40,1024]{3,2,1,0:T(8,128)(2,1)}), s16[16,3,40,1024]{3,2,1,0:T(8,128)(2,1)}, u32[]{:S(2)}, u32[]{:S(2)}) async-start(s16[16,3,40,1024]{3,2,1,0:T(8,128)(2,1)} %split_blocks.1), calls=%async_computation.1 | async-start | bytes 7864320 | tf_op jit(solution)/shard_map/all_to_all | solution.py:356
  106.1 25.3 %copy-start.4 = (bf16[2048,256]{1,0:T(8,128)(2,1)}, bf16[2048,256]{1,0:T(8,128)(2,1)S(1)}, u32[]{:S(2)}) copy-start(bf16[2048,256]{1,0:T(8,128)(2,1)S(1)} %get-tuple-element.36.refs_3_.first_ref) | copy-start | bytes 3145732
  106.1 26.9 %copy-start.2 = (bf16[2048,256]{1,0:T(8,128)(2,1)}, bf16[2048,256]{1,0:T(8,128)(2,1)S(1)}, u32[]{:S(2)}) copy-start(bf16[2048,256]{1,0:T(8,128)(2,1)S(1)} %get-tuple-element.35.refs_2_.first_ref) | copy-start | bytes 3145732
  106.1 25.3 %collective-permute-start.2 = (bf16[2048,128]{1,0:T(8,128)(2,1)}, bf16[2048,128]{1,0:T(8,128)(2,1)S(1)}, u32[]{:S(2)}, u32[]{:S(2)}) collective-permute-start(bf16[2048,128]{1,0:T(8,128)(2,1)} %get-tuple-element.33.refs_0_.first_ref), channel_id=1, source_target_pairs={{0,4},{1,5},{2,6},{3,7},{4,8},{5,9},{6,10},{7,11},{8,12},{9,13},{1... | collective-permute-start | bytes 1572872 | tf_op jit(solution)/shard_map/ppermute | solution.py:20
  124.2 2.0 copy-start
  133.0 17.0 %collective-permute-start.3 = (bf16[2048,128]{1,0:T(8,128)(2,1)S(1)}, bf16[2048,128]{1,0:T(8,128)(2,1)S(1)}, u32[]{:S(2)}, u32[]{:S(2)}) collective-permute-start(bf16[2048,128]{1,0:T(8,128)(2,1)S(1)} %pick.10), channel_id=1, source_target_pairs={{0,2},{1,3},{2,0},{3,1},{4,6},{5,7},{6,4},{7,5},{8,10},{9,11},{10,... | collective-permute-start | bytes 1572872 | tf_op jit(solution)/shard_map/ppermute | solution.py:20
  138.1 26.6 %collective-permute-start.1 = (bf16[2048,256]{1,0:T(8,128)(2,1)}, bf16[2048,256]{1,0:T(8,128)(2,1)S(1)}, u32[]{:S(2)}, u32[]{:S(2)}) collective-permute-start(bf16[2048,256]{1,0:T(8,128)(2,1)} %copy-done.2), channel_id=1, source_target_pairs={{0,4},{1,5},{2,6},{3,7},{4,8},{5,9},{6,10},{7,11},{8,12},{9,13},{1... | collective-permute-start | bytes 3145736 | tf_op jit(solution)/shard_map/ppermute | solution.py:20
  139.0 25.7 %copy-start.3 = (bf16[2048,256]{1,0:T(8,128)(2,1)S(1)}, bf16[2048,256]{1,0:T(8,128)(2,1)}, u32[]{:S(2)}) copy-start(bf16[2048,256]{1,0:T(8,128)(2,1)} %copy-done.2) | copy-start | bytes 3145732
  139.0 26.4 %copy-start.7 = (bf16[2048,128]{1,0:T(8,128)(2,1)S(1)}, bf16[2048,128]{1,0:T(8,128)(2,1)}, u32[]{:S(2)}) copy-start(bf16[2048,128]{1,0:T(8,128)(2,1)} %get-tuple-element.34.refs_1_.first_ref) | copy-start | bytes 1572868
  140.7 9.3 %collective-permute-start.5 = (bf16[2048,128]{1,0:T(8,128)(2,1)S(1)}, bf16[2048,128]{1,0:T(8,128)(2,1)S(1)}, u32[]{:S(2)}, u32[]{:S(2)}) collective-permute-start(bf16[2048,128]{1,0:T(8,128)(2,1)S(1)} %pick.11), channel_id=1, source_target_pairs={{0,1},{1,0},{2,3},{3,2},{4,5},{5,4},{6,7},{7,6},{8,9},{9,8},{10,11... | collective-permute-start | bytes 1572872 | tf_op jit(solution)/shard_map/ppermute | solution.py:20
  150.0 1.9 collective-permute-start.4
  151.9 2.2 copy-start.1
  154.1 29.9 %copy-start.5 = (bf16[2048,256]{1,0:T(8,128)(2,1)S(1)}, bf16[2048,256]{1,0:T(8,128)(2,1)}, u32[]{:S(2)}) copy-start(bf16[2048,256]{1,0:T(8,128)(2,1)} %copy-done.4) | copy-start | bytes 3145732
  154.1 45.9 %copy-start.6 = (bf16[2048,256]{1,0:T(8,128)(2,1)S(1)}, bf16[2048,256]{1,0:T(8,128)(2,1)}, u32[]{:S(2)}) copy-start(bf16[2048,256]{1,0:T(8,128)(2,1)} %get-tuple-element.37.refs_4_.first_ref) | copy-start | bytes 3145732
  164.9 26.1 %collective-permute-start.6 = (bf16[2048,256]{1,0:T(8,128)(2,1)S(1)}, bf16[2048,256]{1,0:T(8,128)(2,1)S(1)}, u32[]{:S(2)}, u32[]{:S(2)}) collective-permute-start(bf16[2048,256]{1,0:T(8,128)(2,1)S(1)} %pick.12), channel_id=1, source_target_pairs={{0,2},{1,3},{2,0},{3,1},{4,6},{5,7},{6,4},{7,5},{8,10},{9,11},{10,... | collective-permute-start | bytes 3145736 | tf_op jit(solution)/shard_map/ppermute | solution.py:20
  165.3 14.3 %collective-permute-start.9 = (bf16[2048,128]{1,0:T(8,128)(2,1)S(1)}, bf16[2048,128]{1,0:T(8,128)(2,1)S(1)}, u32[]{:S(2)}, u32[]{:S(2)}) collective-permute-start(bf16[2048,128]{1,0:T(8,128)(2,1)S(1)} %copy-done.7), channel_id=1, source_target_pairs={{0,4},{1,5},{2,6},{3,7},{4,8},{5,9},{6,10},{7,11},{8,12},{9,13},{1... | collective-permute-start | bytes 1572872 | tf_op jit(solution)/shard_map/ppermute | solution.py:20
  181.1 18.9 %collective-permute-start.10 = (bf16[2048,128]{1,0:T(8,128)(2,1)S(1)}, bf16[2048,128]{1,0:T(8,128)(2,1)S(1)}, u32[]{:S(2)}, u32[]{:S(2)}) collective-permute-start(bf16[2048,128]{1,0:T(8,128)(2,1)S(1)} %pick.14), channel_id=1, source_target_pairs={{0,2},{1,3},{2,0},{3,1},{4,6},{5,7},{6,4},{7,5},{8,10},{9,11},{10,... | collective-permute-start | bytes 1572872 | tf_op jit(solution)/shard_map/ppermute | solution.py:20
  183.9 16.0 %collective-permute-start.12 = (bf16[2048,128]{1,0:T(8,128)(2,1)S(1)}, bf16[2048,128]{1,0:T(8,128)(2,1)S(1)}, u32[]{:S(2)}, u32[]{:S(2)}) collective-permute-start(bf16[2048,128]{1,0:T(8,128)(2,1)S(1)} %pick.15), channel_id=1, source_target_pairs={{0,1},{1,0},{2,3},{3,2},{4,5},{5,4},{6,7},{7,6},{8,9},{9,8},{10,11... | collective-permute-start | bytes 1572872 | tf_op jit(solution)/shard_map/ppermute | solution.py:20
  184.0 27.9 %collective-permute-start.16 = (bf16[2048,256]{1,0:T(8,128)(2,1)S(1)}, bf16[2048,256]{1,0:T(8,128)(2,1)S(1)}, u32[]{:S(2)}, u32[]{:S(2)}) collective-permute-start(bf16[2048,256]{1,0:T(8,128)(2,1)S(1)} %copy-done.5), channel_id=1, source_target_pairs={{0,4},{1,5},{2,6},{3,7},{4,8},{5,9},{6,10},{7,11},{8,12},{9,13},{1... | collective-permute-start | bytes 3145736 | tf_op jit(solution)/shard_map/ppermute | solution.py:20
  184.4 28.5 %collective-permute-start.8 = (bf16[2048,256]{1,0:T(8,128)(2,1)S(1)}, bf16[2048,256]{1,0:T(8,128)(2,1)S(1)}, u32[]{:S(2)}, u32[]{:S(2)}) collective-permute-start(bf16[2048,256]{1,0:T(8,128)(2,1)S(1)} %pick.13), channel_id=1, source_target_pairs={{0,1},{1,0},{2,3},{3,2},{4,5},{5,4},{6,7},{7,6},{8,9},{9,8},{10,11... | collective-permute-start | bytes 3145736 | tf_op jit(solution)/shard_map/ppermute | solution.py:20
  191.0 21.8 %collective-permute-start.7 = (bf16[2048,256]{1,0:T(8,128)(2,1)S(1)}, bf16[2048,256]{1,0:T(8,128)(2,1)S(1)}, u32[]{:S(2)}, u32[]{:S(2)}) collective-permute-start(bf16[2048,256]{1,0:T(8,128)(2,1)S(1)} %collective-permute-done.6.v2_ref), channel_id=1, source_target_pairs={{0,1},{1,0},{2,3},{3,2},{4,5},{5,4},{6,7},{7,6},{8,9},{9,8},{10,11... | collective-permute-start | bytes 3145736 | tf_op jit(solution)/shard_map/ppermute | solution.py:20
  200.0 33.9 %collective-permute-start = (bf16[2048,256]{1,0:T(8,128)(2,1)S(1)}, bf16[2048,256]{1,0:T(8,128)(2,1)S(1)}, u32[]{:S(2)}, u32[]{:S(2)}) collective-permute-start(bf16[2048,256]{1,0:T(8,128)(2,1)S(1)} %copy-done.6), channel_id=1, source_target_pairs={{0,4},{1,5},{2,6},{3,7},{4,8},{5,9},{6,10},{7,11},{8,12},{9,13},{1... | collective-permute-start | bytes 3145736 | tf_op jit(solution)/shard_map/ppermute | solution.py:20
  200.0 2.0 collective-permute-start.11
  212.2 24.2 %collective-permute-start.17 = (bf16[2048,256]{1,0:T(8,128)(2,1)S(1)}, bf16[2048,256]{1,0:T(8,128)(2,1)S(1)}, u32[]{:S(2)}, u32[]{:S(2)}) collective-permute-start(bf16[2048,256]{1,0:T(8,128)(2,1)S(1)} %pick.18), channel_id=1, source_target_pairs={{0,2},{1,3},{2,0},{3,1},{4,6},{5,7},{6,4},{7,5},{8,10},{9,11},{10,... | collective-permute-start | bytes 3145736 | tf_op jit(solution)/shard_map/ppermute | solution.py:20
  234.1 24.7 %collective-permute-start.13 = (bf16[2048,256]{1,0:T(8,128)(2,1)S(1)}, bf16[2048,256]{1,0:T(8,128)(2,1)S(1)}, u32[]{:S(2)}, u32[]{:S(2)}) collective-permute-start(bf16[2048,256]{1,0:T(8,128)(2,1)S(1)} %pick.16), channel_id=1, source_target_pairs={{0,2},{1,3},{2,0},{3,1},{4,6},{5,7},{6,4},{7,5},{8,10},{9,11},{10,... | collective-permute-start | bytes 3145736 | tf_op jit(solution)/shard_map/ppermute | solution.py:20
  235.0 23.9 %collective-permute-start.19 = (bf16[2048,256]{1,0:T(8,128)(2,1)S(1)}, bf16[2048,256]{1,0:T(8,128)(2,1)S(1)}, u32[]{:S(2)}, u32[]{:S(2)}) collective-permute-start(bf16[2048,256]{1,0:T(8,128)(2,1)S(1)} %pick.19), channel_id=1, source_target_pairs={{0,1},{1,0},{2,3},{3,2},{4,5},{5,4},{6,7},{7,6},{8,9},{9,8},{10,11... | collective-permute-start | bytes 3145736 | tf_op jit(solution)/shard_map/ppermute | solution.py:20
  236.3 22.6 %collective-permute-start.18 = (bf16[2048,256]{1,0:T(8,128)(2,1)S(1)}, bf16[2048,256]{1,0:T(8,128)(2,1)S(1)}, u32[]{:S(2)}, u32[]{:S(2)}) collective-permute-start(bf16[2048,256]{1,0:T(8,128)(2,1)S(1)} %collective-permute-done.17.v2_ref), channel_id=1, source_target_pairs={{0,1},{1,0},{2,3},{3,2},{4,5},{5,4},{6,7},{7,6},{8,9},{9,8},{10,11... | collective-permute-start | bytes 3145736 | tf_op jit(solution)/shard_map/ppermute | solution.py:20
  236.8 28.8 %collective-permute-start.15 = (bf16[2048,256]{1,0:T(8,128)(2,1)S(1)}, bf16[2048,256]{1,0:T(8,128)(2,1)S(1)}, u32[]{:S(2)}, u32[]{:S(2)}) collective-permute-start(bf16[2048,256]{1,0:T(8,128)(2,1)S(1)} %pick.17), channel_id=1, source_target_pairs={{0,1},{1,0},{2,3},{3,2},{4,5},{5,4},{6,7},{7,6},{8,9},{9,8},{10,11... | collective-permute-start | bytes 3145736 | tf_op jit(solution)/shard_map/ppermute | solution.py:20
  258.8 11.3 %collective-permute-start.14 = (bf16[2048,256]{1,0:T(8,128)(2,1)S(1)}, bf16[2048,256]{1,0:T(8,128)(2,1)S(1)}, u32[]{:S(2)}, u32[]{:S(2)}) collective-permute-start(bf16[2048,256]{1,0:T(8,128)(2,1)S(1)} %collective-permute-done.13.first_ref), channel_id=1, source_target_pairs={{0,1},{1,0},{2,3},{3,2},{4,5},{5,4},{6,7},{7,6},{8,9},{9,8},{10,11... | collective-permute-start | bytes 3145736 | tf_op jit(solution)/shard_map/ppermute | solution.py:20

commit v4 on v3

--- a/solution.py
+++ b/solution.py
@@ -10,6 +10,7 @@
 
 
 ROUNDS = 4
+CHUNKS = 8
 VMEM_BYTES = 24 * 1024 * 1024
 UNIT = 1.0 / 512.0
 BAD = -32768
@@ -60,14 +61,15 @@
 
     @pl.when(step >= steps)
     def _():
-        base = (step - steps) * tile
-        unroll = 16
+        unroll = 32
+        count = slots_ref.shape[0] // 2
 
         def contacts(i, carry):
+            base = (step - steps) * tile + i * unroll
             for u in range(unroll):
                 c = i * unroll + u
-                first = slots_ref[0, base + c]
-                second = slots_ref[1, base + c]
+                first = slots_ref[base + u]
+                second = slots_ref[base + u + count]
                 squared = None
                 for row in (0, 8, 16):
                     offset = (atoms_ref[pl.ds(pl.multiple_of(first + row, 8), 8), :]
@@ -90,7 +92,7 @@
 
 def features_of(x, slots24, starts, widths, unit):
     groups, _, rows, frames = x.shape
-    contacts = slots24.shape[1]
+    contacts = slots24.shape[0] // 2
     per_step = largest_divisor(groups, max(1, 160 // rows))
     steps = groups // per_step
     tile = 512
@@ -151,61 +153,88 @@
     )(*fts)
 
 
-def pick_kernel(flag_ref, first_ref, second_ref, *refs):
-    out_ref, rows_ref, in_sems, out_sems = refs[-4:]
-    parts = in_sems.shape[0]
-    size = rows_ref.shape[0] // parts
-    spans = [pl.ds(k * size, size) for k in range(parts)]
-
-    def fetch(source_ref):
-        for k, span in enumerate(spans):
-            pltpu.make_async_copy(source_ref.at[span], rows_ref.at[span], in_sems.at[k]).start()
+def pick_kernel(flag_ref, *refs, count, rest):
+    first_refs, second_refs = refs[:count], refs[count:2 * count]
+    out_ref, rows_ref, in_sems, out_sems = refs[2 * count + rest:]
+    parts = in_sems.shape[1]
+    size = rows_ref.shape[1] // parts
+    spans = [(n, k, pl.ds(k * size, size)) for n in range(count) for k in range(parts)]
+
+    def fetch(source_refs):
+        return [pltpu.make_async_copy(source_refs[n].at[span], rows_ref.at[n, span], in_sems.at[n, k])
+                for n, k, span in spans]
 
     @pl.when(flag_ref[0] == 1)
     def _():
-        fetch(first_ref)
+        for copy in fetch(first_refs):
+            copy.start()
 
     @pl.when(flag_ref[0] != 1)
     def _():
-        fetch(second_ref)
-
-    for k, span in enumerate(spans):
-        pltpu.make_async_copy(first_ref.at[span], rows_ref.at[span], in_sems.at[k]).wait()
-        pltpu.make_async_copy(rows_ref.at[span], out_ref.at[span], out_sems.at[k]).start()
-    for k, span in enumerate(spans):
-        pltpu.make_async_copy(rows_ref.at[span], out_ref.at[span], out_sems.at[k]).wait()
-
-
-def pick(flag, first, second, after):
+        for copy in fetch(second_refs):
+            copy.start()
+
+    stores = [pltpu.make_async_copy(rows_ref.at[n, span], out_ref.at[n, span], out_sems.at[n, k])
+              for n, k, span in spans]
+    for copy, store in zip(fetch(first_refs), stores):
+        copy.wait()
+        store.start()
+    for store in stores:
+        store.wait()
+
+
+def pick(flag, firsts, seconds, after):
     anywhere = pl.BlockSpec(memory_space=pl.ANY)
-    return pl.pallas_call(
-        pick_kernel,
-        in_specs=[pl.BlockSpec(memory_space=pltpu.SMEM)] + [anywhere] * (2 + len(after)),
+    count = len(firsts)
+    shape = (count,) + firsts[0].shape
+    return pl.pallas_call(
+        functools.partial(pick_kernel, count=count, rest=len(after)),
+        in_specs=[pl.BlockSpec(memory_space=pltpu.SMEM)] + [anywhere] * (2 * count + len(after)),
         out_specs=anywhere,
-        out_shape=jax.ShapeDtypeStruct(first.shape, first.dtype),
-        scratch_shapes=[pltpu.VMEM(first.shape, first.dtype), pltpu.SemaphoreType.DMA((4,)),
-                        pltpu.SemaphoreType.DMA((4,))],
+        out_shape=jax.ShapeDtypeStruct(shape, firsts[0].dtype),
+        scratch_shapes=[pltpu.VMEM(shape, firsts[0].dtype), pltpu.SemaphoreType.DMA((count, 4)),
+                        pltpu.SemaphoreType.DMA((count, 4))],
         compiler_params=pltpu.CompilerParams(vmem_limit_bytes=VMEM_BYTES // 4),
         name="pick",
-    )(flag, first, second, *after)
-
-
-def distance_kernel(bit_ref, own_ref, norm_ref, v4_ref, v2_ref, vx_ref, vy_ref, *refs, aliased):
-    refs = refs[1:] if aliased else refs
-    out_ref, token_ref, vnorm_ref = refs
+    )(flag, *firsts, *seconds, *after)
+
+
+def side_by_side(refs):
+    return jnp.concatenate([ref[...].reshape(ref.shape[-2:]) for ref in refs], axis=1)
+
+
+def block_specs(arrays):
+    specs = []
+    for array in arrays:
+        zeros = (0,) * array.ndim
+        specs.append(pl.BlockSpec(array.shape, lambda *ids, zeros=zeros: zeros))
+    return specs
+
+
+def tanimoto(own_ref, norm_ref, visitor, visitor_norm):
+    inter = jnp.dot(own_ref[...], visitor, preferred_element_type=jnp.float32)
+    ratio = inter / (norm_ref[...] + visitor_norm - inter + 1e-06)
+    return (1.0 - ratio).astype(jnp.bfloat16)
+
+
+def column_norms(features):
+    wide = features.astype(jnp.float32)
+    return jnp.sum(wide * wide, axis=0, keepdims=True)
+
+
+def distance_kernel(bit_ref, own_ref, norm_ref, *refs, aliased):
+    visitors = [refs[2 * r:2 * r + 2] for r in range(ROUNDS)]
+    out_ref, token_ref, vnorm_ref = refs[2 * ROUNDS + (1 if aliased else 0):]
 
     @pl.when(pl.program_id(0) == 0)
     def _():
-        for r, ref in enumerate((vx_ref, v2_ref, vy_ref, v4_ref)):
-            wide = ref[...].astype(jnp.float32)
-            vnorm_ref[r, 0:1, :] = jnp.sum(wide * wide, axis=0, keepdims=True)
+        for r, pair in enumerate(visitors):
+            vnorm_ref[r, 0:1, :] = column_norms(side_by_side(pair))
         token_ref[...] = jnp.zeros_like(token_ref)
 
     def rounds(places):
-        for r, ref in enumerate((vx_ref, v2_ref, vy_ref, v4_ref)):
-            inter = jnp.dot(own_ref[...], ref[...], preferred_element_type=jnp.float32)
-            ratio = inter / (norm_ref[...] + vnorm_ref[r, 0:1, :] - inter + 1e-06)
-            out_ref[places[r]] = (1.0 - ratio).astype(jnp.bfloat16)
+        for r, pair in enumerate(visitors):
+            out_ref[places[r]] = tanimoto(own_ref, norm_ref, side_by_side(pair), vnorm_ref[r, 0:1, :])
 
     @pl.when(bit_ref[0] == 1)
     def _():
@@ -216,18 +245,18 @@
         rounds((0, 1, 2, 3))
 
 
-def distance_chunk(bit, own, norms, v4, v2, vx, vy, out, start):
+def distance_pair(bit, own, norms, vx, v2, vy, v4, out, block):
     frames, contacts = own.shape
-    width = v4.shape[1]
+    width = 2 * v4[0].shape[-1]
     tile = 256
-    block = start // width
+    visitors = [*vx, *v2, *vy, *v4]
     aliased = out is not None
     in_specs = [
         pl.BlockSpec(memory_space=pltpu.SMEM),
         pl.BlockSpec((tile, contacts), lambda i: (i, 0)),
         pl.BlockSpec((tile, 1), lambda i: (i, 0)),
-    ] + [pl.BlockSpec((contacts, width), lambda i: (0, 0))] * 4
-    args = [bit, own, norms, v4, v2, vx, vy]
+    ] + block_specs(visitors)
+    args = [bit, own, norms, *visitors]
     if aliased:
         in_specs.append(pl.BlockSpec(memory_space=pl.ANY))
         args.append(out)
@@ -244,44 +273,36 @@
             jax.ShapeDtypeStruct((8, 128), jnp.float32),
         ],
         scratch_shapes=[pltpu.VMEM((ROUNDS, 8, width), jnp.float32)],
-        input_output_aliases={7: 0} if aliased else {},
+        input_output_aliases={len(args) - 1: 0} if aliased else {},
         compiler_params=pltpu.CompilerParams(vmem_limit_bytes=VMEM_BYTES),
     )(*args)
 
 
-def half_kernel(places_ref, own_ref, norm_ref, first_ref, second_ref, *refs, aliased):
-    refs = refs[1:] if aliased else refs
-    out_ref, token_ref, vnorm_ref = refs
+def half_kernel(places_ref, own_ref, norm_ref, *refs):
+    visitors = [refs[:2], refs[2:4]]
+    out_ref, token_ref, vnorm_ref = refs[5:]
     token_ref[...] = jnp.zeros_like(token_ref)
-    for which, ref in enumerate((first_ref, second_ref)):
+    for which, pair in enumerate(visitors):
         @pl.when(pl.program_id(0) == which)
-        def _():
+        def _(pair=pair):
             @pl.when(pl.program_id(1) == 0)
             def _():
-                wide = ref[...].astype(jnp.float32)
-                vnorm_ref[0:1, :] = jnp.sum(wide * wide, axis=0, keepdims=True)
-
-            inter = jnp.dot(own_ref[...], ref[...], preferred_element_type=jnp.float32)
-            ratio = inter / (norm_ref[...] + vnorm_ref[0:1, :] - inter + 1e-06)
-            out_ref[0] = (1.0 - ratio).astype(jnp.bfloat16)
-
-
-def distance_half(places, own, norms, first, second, out, start):
+                vnorm_ref[0:1, :] = column_norms(side_by_side(pair))
+
+            out_ref[0] = tanimoto(own_ref, norm_ref, side_by_side(pair), vnorm_ref[0:1, :])
+
+
+def distance_half(places, own, norms, first, second, out, block):
     frames, contacts = own.shape
-    width = first.shape[1]
+    width = 2 * first[0].shape[-1]
     tile = 512
-    block = start // width
-    aliased = out is not None
+    visitors = [*first, *second]
     in_specs = [
         pl.BlockSpec((tile, contacts), lambda r, i, p: (i, 0)),
         pl.BlockSpec((tile, 1), lambda r, i, p: (i, 0)),
-    ] + [pl.BlockSpec((contacts, width), lambda r, i, p: (0, 0))] * 2
-    args = [own, norms, first, second]
-    if aliased:
-        in_specs.append(pl.BlockSpec(memory_space=pl.ANY))
-        args.append(out)
-    return pl.pallas_call(
-        functools.partial(half_kernel, aliased=aliased),
+    ] + block_specs(visitors) + [pl.BlockSpec(memory_space=pl.ANY)]
+    return pl.pallas_call(
+        half_kernel,
         grid_spec=pltpu.PrefetchScalarGridSpec(
             num_scalar_prefetch=1,
             grid=(2, frames // tile),
@@ -296,9 +317,10 @@
             jax.ShapeDtypeStruct((ROUNDS, frames, frames), jnp.bfloat16),
             jax.ShapeDtypeStruct((8, 128), jnp.float32),
         ],
-        input_output_aliases={5: 0} if aliased else {},
+        input_output_aliases={7: 0},
         compiler_params=pltpu.CompilerParams(vmem_limit_bytes=VMEM_BYTES),
-    )(places, *args)
+        name="distances_half",
+    )(places, own, norms, *visitors, out)
 
 
 def contact_slots(pairs, res_slot):
@@ -378,11 +400,11 @@
 
 def shards(coords, pairs, res_slot):
     index = lax.axis_index("blocks")
-    lanes = coords.shape[2] // lax.axis_size("blocks") // 8
-    widths = [lanes * n for n in (1, 1, 2, 2, 2)]
-    starts = [lanes * n for n in (0, 1, 2, 4, 6)]
-
-    slots24 = contact_slots(pairs, res_slot) * 24
+    lanes = coords.shape[2] // lax.axis_size("blocks") // CHUNKS
+    widths = [lanes] * CHUNKS
+    starts = [lanes * n for n in range(CHUNKS)]
+
+    slots24 = contact_slots(pairs, res_slot).reshape(-1) * 24
     fts = contact_features(coords, slots24, starts, widths)
 
     bit = (index & 1).astype(jnp.int32).reshape(1)
@@ -396,23 +418,28 @@
 
     out = None
     tokens = []
-    for j, (ft, v4) in enumerate(zip(fts, v4s)):
-        after = tokens[j - 2:j - 1] if j >= 2 else [norms]
-        sent = pick(low_pair, ft, v4, after)
-        v2 = permuted(sent, "blocks", swap2)
-        sent = pick(low_core, ft, v4, [])
+    for p in range(CHUNKS // 2):
+        both = (2 * p, 2 * p + 1)
+        after = tokens[p - 2:p - 1] if p >= 2 else [norms]
+        v2 = []
+        for k in both:
+            sent = pick(low_pair, [fts[k]], [v4s[k]], after)
+            v2.append(permuted(sent, "blocks", swap2))
+        sent = pick(low_core, [fts[k] for k in both], [v4s[k] for k in both], [])
         vy = permuted(sent, "blocks", swap1)
-        vx = permuted(v2, "blocks", swap1)
-        if j + 1 < len(fts):
-            out, token = distance_chunk(bit, own, norms, v4, v2, vx, vy, out, starts[j])
+        vy = [vy[0], vy[1]]
+        vx = []
+        for k in both:
+            vx.append(permuted(v2[k - 2 * p], "blocks", swap1))
+        v4 = [v4s[k] for k in both]
+        if p + 1 < CHUNKS // 2:
+            out, token = distance_pair(bit, own, norms, vx, v2, vy, v4, out, p)
+            tokens.append(token)
         else:
-            three = jnp.full((1,), 3, jnp.int32)
-            one = jnp.full((1,), 1, jnp.int32)
-            places = jnp.concatenate([three, 2 - 2 * bit])
-            out, token = distance_half(places, own, norms, v4, vy, out, starts[j])
-            places = jnp.concatenate([one, 2 * bit])
-            out, token = distance_half(places, own, norms, v2, vx, out, starts[j])
-        tokens.append(token)
+            places = jnp.concatenate([jnp.full((1,), 3, jnp.int32), 2 - 2 * bit])
+            out, _ = distance_half(places, own, norms, v4, vy, out, p)
+            places = jnp.concatenate([jnp.full((1,), 1, jnp.int32), 2 * bit])
+            out, _ = distance_half(places, own, norms, v2, vx, out, p)
     return out
 
 

time: 275 us -> 324 us (1.18)
  starting transfers between devices: 32.1 us -> 54.9 us
  waiting for transfers between devices: 164 us -> 183 us
  Pallas kernels: 70.5 us -> 81 us
  local copies, waits for them, and re-layouts: 4.23 us -> 0.29 us
    ppermute x20 -> x28, starting transfers between devices: 24.7 us -> 47.4 us  [permuted(): return lax.ppermute(shard, axis, [(i, to(i, count)) for i in range(count)])]
    ppermute x20 -> x28, waiting for transfers between devices: 92.5 us -> 112 us  [permuted(): return lax.ppermute(shard, axis, [(i, to(i, count)) for i in range(count)])]
    pallas_call x16 -> x17, Pallas kernels: 42.9 us -> 56.2 us  [the longest x3 23.9 us: distance_pair(): pl.pallas_call(functools.partial(distance_kernel, aliased=aliased), grid=...]
    unnamed x20 -> x9, local copies, waits for them, and re-layouts: 4.23 us -> 0.02 us
  transfers between devices with their start and end apart: 21 -> 29, of which waited for: 13 -> 16; matrix products, arithmetic and copies ran while one was open for 1% -> 1% of each run, Pallas kernels for 15% -> 17%
where the time goes in v4:
time: 324 us
  waiting for transfers between devices  183 us (56%)
  Pallas kernels  81 us (25%)
  starting transfers between devices  54.9 us (17%)
    ppermute x28, waiting for transfers between devices, permuted(): return lax.ppermute(shard, axis, [(i, to(i, count)) for i in range(count)])  112 us
    all_to_all x1, waiting for transfers between devices, exchanged(): lax.all_to_all(pieces, 'blocks', split_axis=0, concat_axis=0, tiled=True)  71.3 us
    ppermute x28, starting transfers between devices, permuted(): return lax.ppermute(shard, axis, [(i, to(i, count)) for i in range(count)])  47.4 us
    pallas_call x3, Pallas kernels, distance_pair(): pl.pallas_call(functools.partial(distance_kernel, aliased=aliased), grid=...  23.9 us
    pallas_call x12, Pallas kernels, pick(): pl.pallas_call(functools.partial(pick_kernel, count=count, rest=len(after...  22.4 us
    pallas_call x1, Pallas kernels, features_of(): pl.pallas_call(functools.partial(features_kernel, steps=steps, tile=tile,...  13.4 us
    pallas_call x2, Pallas kernels, distance_half(): pl.pallas_call(half_kernel, grid_spec=pltpu.PrefetchScalarGridSpec(num_sc...  9.84 us
    all_to_all x1, starting transfers between devices, exchanged(): lax.all_to_all(pieces, 'blocks', split_axis=0, concat_axis=0, tiled=True)  7.46 us
  transfers between devices with their start and end apart: 29, of which 16 were waited for; matrix products, arithmetic and copies ran while one was open for 1% of the time, Pallas kernels for 17%

profile of v4, /device:TPU:0, one launch (start us, length us, event | category | flops | bytes accessed | tf_op | source)
XLA Modules:
  0.0 323.7 jit_solution(868860783785076449)
XLA Ops:
  0.0 7.0 %split_blocks.1 = s16[16,3,40,1024]{3,2,1,0:T(8,128)(2,1)} custom-call(f32[3,40,16384]{2,1,0:T(8,128)} %bitcast.29), custom_call_target="tpu_custom_call" | custom-call | tf_op jit(solution)/shard_map/split_blocks/pallas_call | solution.py:365
  7.0 7.5 %all-to-all-start.1 = ((s16[16,3,40,1024]{3,2,1,0:T(8,128)(2,1)}), s16[16,3,40,1024]{3,2,1,0:T(8,128)(2,1)}, u32[]{:S(2)}, u32[]{:S(2)}) async-start(s16[16,3,40,1024]{3,2,1,0:T(8,128)(2,1)} %split_blocks.1), calls=%async_computation.1 | async-start | bytes 7864320 | tf_op jit(solution)/shard_map/all_to_all | solution.py:378
  14.5 1.6 select_reduce_fusion
  16.2 71.3 %all-to-all-done.1 = s16[16,3,40,1024]{3,2,1,0:T(8,128)(2,1)} async-done(((s16[16,3,40,1024]{3,2,1,0:T(8,128)(2,1)}), s16[16,3,40,1024]{3,2,1,0:T(8,128)(2,1)}, u32[]{:S(2)}, u32[]{:S(2)}) %all-to-all-start.1) | async-done | bytes 3932192 | tf_op jit(solution)/shard_map/all_to_all | solution.py:378
  87.4 1.4 compare_reduce_fusion
  89.5 13.4 %conditional.1 = ((bf16[2048,128]{1,0:T(8,128)(2,1)}, bf16[2048,128]{1,0:T(8,128)(2,1)}, bf16[2048,128]{1,0:T(8,128)(2,1)}, bf16[2048,128]{1,0:T(8,128)(2,1)}, b...) conditional(s32[]{:T(128)} %convert_element_type.3, ...), branch_computations={%region_2.3_spmd, %region_3.4_spmd} | conditional | bytes 31457288 | solution.py:398
  89.5 13.4 %features.3 = (bf16[2048,128]{1,0:T(8,128)(2,1)}, bf16[2048,128]{1,0:T(8,128)(2,1)}, bf16[2048,128]{1,0:T(8,128)(2,1)}, bf16[2048,128]{1,0:T(8,128)(2,1)}, bf16[...) custom-call(s32[4096]{0:T(1024)S(1)} %get-tuple-element.15.slots_ref, ...), custom_call_target="tpu_custom_call" | custom-call | tf_op jit(solution)/shard_map/cond/branch_1_fun/features/pallas_call | solution.py:100
  102.9 14.1 %collective-permute-start.1 = (bf16[2048,128]{1,0:T(8,128)(2,1)}, bf16[2048,128]{1,0:T(8,128)(2,1)S(1)}, u32[]{:S(2)}, u32[]{:S(2)}) collective-permute-start(bf16[2048,128]{1,0:T(8,128)(2,1)} %get-tuple-element.36.refs_2_.refs_0_), channel_id=1, source_target_pairs={{0,4},{1,5},{2,6},{3,7},{4,8},{5,9},{6,10},{7,11},{8,12},{9,13},{1... | collective-permute-start | bytes 1572872 | tf_op jit(solution)/shard_map/ppermute | solution.py:21
  117.0 3.3 %collective-permute-start.4 = (bf16[2048,128]{1,0:T(8,128)(2,1)}, bf16[2048,128]{1,0:T(8,128)(2,1)S(1)}, u32[]{:S(2)}, u32[]{:S(2)}) collective-permute-start(bf16[2048,128]{1,0:T(8,128)(2,1)} %get-tuple-element.37.refs_3_.refs_0_.refs_1_), channel_id=1, source_target_pairs={{0,4},{1,5},{2,6},{3,7},{4,8},{5,9},{6,10},{7,11},{8,12},{9,13},{1... | collective-permute-start | bytes 1572872 | tf_op jit(solution)/shard_map/ppermute | solution.py:21
  120.5 1.5 collective-permute-start
  121.9 7.7 %collective-permute-done.1.refs_1_.refs_2_.refs_6_ = bf16[2048,128]{1,0:T(8,128)(2,1)S(1)} collective-permute-done((bf16[2048,128]{1,0:T(8,128)(2,1)}, bf16[2048,128]{1,0:T(8,128)(2,1)S(1)}, u32[]{:S(2)}, u32[]{:S(2)}) %collective-permute-start.1) | collective-permute-done | bytes 524320 | tf_op jit(solution)/shard_map/ppermute | solution.py:21
  129.6 3.3 %collective-permute-start.16 = (bf16[2048,128]{1,0:T(8,128)(2,1)}, bf16[2048,128]{1,0:T(8,128)(2,1)S(1)}, u32[]{:S(2)}, u32[]{:S(2)}) collective-permute-start(bf16[2048,128]{1,0:T(8,128)(2,1)} %get-tuple-element.41.refs_7_.refs_0_.refs_1_), channel_id=1, source_target_pairs={{0,4},{1,5},{2,6},{3,7},{4,8},{5,9},{6,10},{7,11},{8,12},{9,13},{1... | collective-permute-start | bytes 1572872 | tf_op jit(solution)/shard_map/ppermute | solution.py:21
  133.0 7.9 %collective-permute-done.4.refs_1_.refs_3_.refs_7_ = bf16[2048,128]{1,0:T(8,128)(2,1)S(1)} collective-permute-done((bf16[2048,128]{1,0:T(8,128)(2,1)}, bf16[2048,128]{1,0:T(8,128)(2,1)S(1)}, u32[]{:S(2)}, u32[]{:S(2)}) %collective-permute-start.4) | collective-permute-done | bytes 524320 | tf_op jit(solution)/shard_map/ppermute | solution.py:21
  140.9 3.3 %collective-permute-start.21 = (bf16[2048,128]{1,0:T(8,128)(2,1)}, bf16[2048,128]{1,0:T(8,128)(2,1)}, u32[]{:S(2)}, u32[]{:S(2)}) collective-permute-start(bf16[2048,128]{1,0:T(8,128)(2,1)} %get-tuple-element.38.refs_4_.refs_0_), channel_id=1, source_target_pairs={{0,4},{1,5},{2,6},{3,7},{4,8},{5,9},{6,10},{7,11},{8,12},{9,13},{1... | collective-permute-start | bytes 1572872 | tf_op jit(solution)/shard_map/ppermute | solution.py:21
  144.2 7.9 %collective-permute-done.8.refs_1_.refs_2_.refs_6_ = bf16[2048,128]{1,0:T(8,128)(2,1)S(1)} collective-permute-done((bf16[2048,128]{1,0:T(8,128)(2,1)}, bf16[2048,128]{1,0:T(8,128)(2,1)S(1)}, u32[]{:S(2)}, u32[]{:S(2)}) %collective-permute-start.8) | collective-permute-done | bytes 524320 | tf_op jit(solution)/shard_map/ppermute | solution.py:21
  152.1 3.3 %collective-permute-start.24 = (bf16[2048,128]{1,0:T(8,128)(2,1)}, bf16[2048,128]{1,0:T(8,128)(2,1)}, u32[]{:S(2)}, u32[]{:S(2)}) collective-permute-start(bf16[2048,128]{1,0:T(8,128)(2,1)} %get-tuple-element.39.refs_5_.refs_0_.refs_1_), channel_id=1, source_target_pairs={{0,4},{1,5},{2,6},{3,7},{4,8},{5,9},{6,10},{7,11},{8,12},{9,13},{1... | collective-permute-start | bytes 1572872 | tf_op jit(solution)/shard_map/ppermute | solution.py:21
  155.4 4.4 %own_features.1 = (bf16[1024,2048]{1,0:T(8,128)(2,1)S(1)}, f32[1024,1]{1,0:T(8,128)S(1)}) custom-call(bf16[2048,128]{1,0:T(8,128)(2,1)} %get-tuple-element.34.refs_0_, bf16[2048,128]{1,0:T(8,128)(2,1)} %get-tuple-element.35.refs_1_.refs_0_, bf16[2048,128]{1,0:T(8,128)(2,1)} %get-tuple-element.36.refs_2_.refs_0_, ...), custom_call_target="tpu_custom_call" | custom-call | tf_op jit(solution)/shard_map/own_features/pallas_call | solution.py:139
  159.9 1.7 pick.12
  161.6 2.4 pick.14
  164.0 3.4 %collective-permute-start.2 = (bf16[1,2048,128]{2,1,0:T(8,128)(2,1)S(1)}, bf16[1,2048,128]{2,1,0:T(8,128)(2,1)S(1)}, u32[]{:S(2)}, u32[]{:S(2)}) collective-permute-start(bf16[1,2048,128]{2,1,0:T(8,128)(2,1)S(1)} %pick.12), channel_id=1, source_target_pairs={{0,2},{1,3},{2,0},{3,1},{4,6},{5,7},{6,4},{7,5},{8,10},{9,11},{10,... | collective-permute-start | bytes 1572872 | tf_op jit(solution)/shard_map/ppermute | solution.py:21
  167.4 2.4 pick.17
  169.8 4.8 %collective-permute-done.refs_1_.refs_2_.refs_0_ = bf16[2048,128]{1,0:T(8,128)(2,1)S(1)} collective-permute-done((bf16[2048,128]{1,0:T(8,128)(2,1)}, bf16[2048,128]{1,0:T(8,128)(2,1)S(1)}, u32[]{:S(2)}, u32[]{:S(2)}) %collective-permute-start) | collective-permute-done | bytes 524320 | tf_op jit(solution)/shard_map/ppermute | solution.py:21
  174.6 11.2 %collective-permute-done.16.refs_1_.refs_3_ = bf16[2048,128]{1,0:T(8,128)(2,1)S(1)} collective-permute-done((bf16[2048,128]{1,0:T(8,128)(2,1)}, bf16[2048,128]{1,0:T(8,128)(2,1)S(1)}, u32[]{:S(2)}, u32[]{:S(2)}) %collective-permute-start.16) | collective-permute-done | bytes 524320 | tf_op jit(solution)/shard_map/ppermute | solution.py:21
  185.8 1.6 pick.13
  187.4 9.6 %collective-permute-done.21.refs_1_.refs_2_.refs_6_ = bf16[2048,128]{1,0:T(8,128)(2,1)} collective-permute-done((bf16[2048,128]{1,0:T(8,128)(2,1)}, bf16[2048,128]{1,0:T(8,128)(2,1)}, u32[]{:S(2)}, u32[]{:S(2)}) %collective-permute-start.21) | collective-permute-done | bytes 524320 | tf_op jit(solution)/shard_map/ppermute | solution.py:21
  197.0 4.2 %collective-permute-start.5 = (bf16[1,2048,128]{2,1,0:T(8,128)(2,1)S(1)}, bf16[1,2048,128]{2,1,0:T(8,128)(2,1)S(1)}, u32[]{:S(2)}, u32[]{:S(2)}) collective-permute-start(bf16[1,2048,128]{2,1,0:T(8,128)(2,1)S(1)} %pick.13), channel_id=1, source_target_pairs={{0,2},{1,3},{2,0},{3,1},{4,6},{5,7},{6,4},{7,5},{8,10},{9,11},{10,... | collective-permute-start | bytes 1572872 | tf_op jit(solution)/shard_map/ppermute | solution.py:21
  201.2 1.6 pick.15
  202.8 4.0 %collective-permute-done.24.refs_1_.refs_3_.refs_7_ = bf16[2048,128]{1,0:T(8,128)(2,1)} collective-permute-done((bf16[2048,128]{1,0:T(8,128)(2,1)}, bf16[2048,128]{1,0:T(8,128)(2,1)}, u32[]{:S(2)}, u32[]{:S(2)}) %collective-permute-start.24) | collective-permute-done | bytes 524320 | tf_op jit(solution)/shard_map/ppermute | solution.py:21
  206.8 5.3 %collective-permute-start.9 = (bf16[1,2048,128]{2,1,0:T(8,128)(2,1)S(1)}, bf16[1,2048,128]{2,1,0:T(8,128)(2,1)S(1)}, u32[]{:S(2)}, u32[]{:S(2)}) collective-permute-start(bf16[1,2048,128]{2,1,0:T(8,128)(2,1)S(1)} %pick.15), channel_id=1, source_target_pairs={{0,2},{1,3},{2,0},{3,1},{4,6},{5,7},{6,4},{7,5},{8,10},{9,11},{10,... | collective-permute-start | bytes 1572872 | tf_op jit(solution)/shard_map/ppermute | solution.py:21
  212.1 1.6 pick.16
  213.8 0.1 collective-permute-start.12
  213.9 2.4 pick.20
  216.3 0.1 collective-permute-start.20
  216.4 8.5 %collective-permute-done.9.refs_2_ = bf16[1,2048,128]{2,1,0:T(8,128)(2,1)S(1)} collective-permute-done((bf16[1,2048,128]{2,1,0:T(8,128)(2,1)S(1)}, bf16[1,2048,128]{2,1,0:T(8,128)(2,1)S(1)}, u32[]{:S(2)}, u32[]{:S(2)}) %collective-permute-start.9) | collective-permute-done | bytes 524320 | tf_op jit(solution)/shard_map/ppermute | solution.py:21
  224.9 2.4 pick.23
  227.3 8.0 %collective-permute-done.12.refs_3_ = bf16[1,2048,128]{2,1,0:T(8,128)(2,1)S(1)} collective-permute-done((bf16[1,2048,128]{2,1,0:T(8,128)(2,1)S(1)}, bf16[1,2048,128]{2,1,0:T(8,128)(2,1)S(1)}, u32[]{:S(2)}, u32[]{:S(2)}) %collective-permute-start.12) | collective-permute-done | bytes 524320 | tf_op jit(solution)/shard_map/ppermute | solution.py:21
  235.3 0.5 collective-permute-start.6
  235.8 0.1 collective-permute-start.13
  235.9 0.1 slice_bitcast_fusion.6
  235.9 0.5 collective-permute-start.27
  236.5 0.1 slice_bitcast_fusion.4
  236.5 2.2 collective-permute-done.13.refs_1_
  238.7 7.6 %shard_map.37 = (bf16[4,1024,1024]{2,1,0:T(8,128)(2,1)}, f32[8,128]{1,0:T(8,128)S(1)}) custom-call(s32[1]{0:T(128)} %bitcast.1.bit_ref, bf16[1024,2048]{1,0:T(8,128)(2,1)S(1)} %get-tuple-element.42.own_ref, f32[1024,1]{1,0:T(8,128)S(1)} %get-tuple-element.43.refs_2_.norm_ref, bf16[1,2048,128]{2,1,0:T(8,128)(2,1)S(1)} %collective-permute-done.10.refs_0_, ...), custom_call_target="tpu_custom_call" | custom-call | tf_op jit(solution)/shard_map/pallas_call | solution.py:263
  246.3 7.6 %shard_map.38 = (bf16[4,1024,1024]{2,1,0:T(8,128)(2,1)}, f32[8,128]{1,0:T(8,128)S(1)}) custom-call(s32[1]{0:T(128)} %bitcast.1.bit_ref, bf16[1024,2048]{1,0:T(8,128)(2,1)S(1)} %get-tuple-element.42.own_ref, f32[1024,1]{1,0:T(8,128)S(1)} %get-tuple-element.43.refs_2_.norm_ref, ...), custom_call_target="tpu_custom_call", output_to_operand_aliasing={{0}: (11, {})} | custom-call | tf_op jit(solution)/shard_map/pallas_call | solution.py:263
  253.8 1.6 pick.18
  255.5 1.6 collective-permute-start.15
  257.0 1.4 pick.19
  258.5 0.6 collective-permute-start.17
  259.0 1.6 pick.21
  260.6 1.6 collective-permute-start.22
  262.2 1.6 pick.22
  263.9 0.6 collective-permute-start.25
  264.4 0.1 pad_add_fusion.places_ref
  264.5 0.1 pad_add_fusion.1.places_ref
  264.6 5.7 %collective-permute-done.15.refs_0_ = bf16[1,2048,128]{2,1,0:T(8,128)(2,1)S(1)} collective-permute-done((bf16[1,2048,128]{2,1,0:T(8,128)(2,1)S(1)}, bf16[1,2048,128]{2,1,0:T(8,128)(2,1)S(1)}, u32[]{:S(2)}, u32[]{:S(2)}) %collective-permute-start.15) | collective-permute-done | bytes 524320 | tf_op jit(solution)/shard_map/ppermute | solution.py:21
  270.3 11.2 %collective-permute-done.17.refs_1_ = bf16[1,2048,128]{2,1,0:T(8,128)(2,1)S(1)} collective-permute-done((bf16[1,2048,128]{2,1,0:T(8,128)(2,1)S(1)}, bf16[1,2048,128]{2,1,0:T(8,128)(2,1)S(1)}, u32[]{:S(2)}, u32[]{:S(2)}) %collective-permute-start.17) | collective-permute-done | bytes 524320 | tf_op jit(solution)/shard_map/ppermute | solution.py:21
  281.6 11.2 %collective-permute-done.22.refs_2_ = bf16[1,2048,128]{2,1,0:T(8,128)(2,1)S(1)} collective-permute-done((bf16[1,2048,128]{2,1,0:T(8,128)(2,1)S(1)}, bf16[1,2048,128]{2,1,0:T(8,128)(2,1)S(1)}, u32[]{:S(2)}, u32[]{:S(2)}) %collective-permute-start.22) | collective-permute-done | bytes 524320 | tf_op jit(solution)/shard_map/ppermute | solution.py:21
  292.8 10.4 %collective-permute-done.25.refs_3_ = bf16[1,2048,128]{2,1,0:T(8,128)(2,1)S(1)} collective-permute-done((bf16[1,2048,128]{2,1,0:T(8,128)(2,1)S(1)}, bf16[1,2048,128]{2,1,0:T(8,128)(2,1)S(1)}, u32[]{:S(2)}, u32[]{:S(2)}) %collective-permute-start.25) | collective-permute-done | bytes 524320 | tf_op jit(solution)/shard_map/ppermute | solution.py:21
  303.1 0.1 slice_bitcast_fusion.2
  303.2 0.1 slice_bitcast_fusion
  303.3 1.7 collective-permute-done.26.refs_1_
  305.1 8.8 %shard_map.39 = (bf16[4,1024,1024]{2,1,0:T(8,128)(2,1)}, f32[8,128]{1,0:T(8,128)}) custom-call(s32[1]{0:T(128)} %bitcast.1.bit_ref, bf16[1024,2048]{1,0:T(8,128)(2,1)S(1)} %get-tuple-element.42.own_ref, f32[1024,1]{1,0:T(8,128)S(1)} %get-tuple-element.43.refs_2_.norm_ref, ...), custom_call_target="tpu_custom_call", output_to_operand_aliasing={{0}: (11, {})} | custom-call | tf_op jit(solution)/shard_map/pallas_call | solution.py:263
  313.9 4.9 %distances_half.2 = (bf16[4,1024,1024]{2,1,0:T(8,128)(2,1)}, f32[8,128]{1,0:T(8,128)}) custom-call(s32[2]{0:T(128)S(1)} %pad_add_fusion.1.places_ref, bf16[1024,2048]{1,0:T(8,128)(2,1)S(1)} %get-tuple-element.42.own_ref, f32[1024,1]{1,0:T(8,128)S(1)} %get-tuple-element.43.refs_2_.norm_ref, ...), custom_call_target="tpu_custom_call", output_to_operand_aliasing={{0}: (7, {})} | custom-call | tf_op jit(solution)/shard_map/distances_half/pallas_call | solution.py:304
  318.8 4.9 %distances_half.3 = (bf16[4,1024,1024]{2,1,0:T(8,128)(2,1)}, f32[8,128]{1,0:T(8,128)}) custom-call(s32[2]{0:T(128)S(1)} %pad_add_fusion.places_ref, bf16[1024,2048]{1,0:T(8,128)(2,1)S(1)} %get-tuple-element.42.own_ref, f32[1024,1]{1,0:T(8,128)S(1)} %get-tuple-element.43.refs_2_.norm_ref, ...), custom_call_target="tpu_custom_call", output_to_operand_aliasing={{0}: (7, {})} | custom-call | tf_op jit(solution)/shard_map/distances_half/pallas_call | solution.py:304
  (33 shorter events, 0.2 us)
Async XLA Ops:
  0.0 14.5 %copy-start.2 = (s32[2,2048]{1,0:T(2,128)S(1)}, s32[2,2048]{1,0:T(2,128)}, u32[]{:S(2)}) copy-start(s32[2,2048]{1,0:T(2,128)} %param.6) | copy-start | bytes 49156
  0.0 14.5 %copy-start.3 = (s32[640]{0:T(1024)S(1)}, s32[640]{0:T(1024)}, u32[]{:S(2)}) copy-start(s32[640]{0:T(1024)} %param.7) | copy-start | bytes 7684
  7.0 80.5 %all-to-all-start.1 = ((s16[16,3,40,1024]{3,2,1,0:T(8,128)(2,1)}), s16[16,3,40,1024]{3,2,1,0:T(8,128)(2,1)}, u32[]{:S(2)}, u32[]{:S(2)}) async-start(s16[16,3,40,1024]{3,2,1,0:T(8,128)(2,1)} %split_blocks.1), calls=%async_computation.1 | async-start | bytes 7864320 | tf_op jit(solution)/shard_map/all_to_all | solution.py:378
  102.9 26.7 %collective-permute-start.1 = (bf16[2048,128]{1,0:T(8,128)(2,1)}, bf16[2048,128]{1,0:T(8,128)(2,1)S(1)}, u32[]{:S(2)}, u32[]{:S(2)}) collective-permute-start(bf16[2048,128]{1,0:T(8,128)(2,1)} %get-tuple-element.36.refs_2_.refs_0_), channel_id=1, source_target_pairs={{0,4},{1,5},{2,6},{3,7},{4,8},{5,9},{6,10},{7,11},{8,12},{9,13},{1... | collective-permute-start | bytes 1572872 | tf_op jit(solution)/shard_map/ppermute | solution.py:21
  117.0 23.9 %collective-permute-start.4 = (bf16[2048,128]{1,0:T(8,128)(2,1)}, bf16[2048,128]{1,0:T(8,128)(2,1)S(1)}, u32[]{:S(2)}, u32[]{:S(2)}) collective-permute-start(bf16[2048,128]{1,0:T(8,128)(2,1)} %get-tuple-element.37.refs_3_.refs_0_.refs_1_), channel_id=1, source_target_pairs={{0,4},{1,5},{2,6},{3,7},{4,8},{5,9},{6,10},{7,11},{8,12},{9,13},{1... | collective-permute-start | bytes 1572872 | tf_op jit(solution)/shard_map/ppermute | solution.py:21
  120.3 31.8 %collective-permute-start.8 = (bf16[2048,128]{1,0:T(8,128)(2,1)}, bf16[2048,128]{1,0:T(8,128)(2,1)S(1)}, u32[]{:S(2)}, u32[]{:S(2)}) collective-permute-start(bf16[2048,128]{1,0:T(8,128)(2,1)} %get-tuple-element.34.refs_0_), channel_id=1, source_target_pairs={{0,4},{1,5},{2,6},{3,7},{4,8},{5,9},{6,10},{7,11},{8,12},{9,13},{1... | collective-permute-start | bytes 1572872 | tf_op jit(solution)/shard_map/ppermute | solution.py:21
  120.4 43.6 %collective-permute-start.11 = (bf16[2048,128]{1,0:T(8,128)(2,1)}, bf16[2048,128]{1,0:T(8,128)(2,1)S(1)}, u32[]{:S(2)}, u32[]{:S(2)}) collective-permute-start(bf16[2048,128]{1,0:T(8,128)(2,1)} %get-tuple-element.35.refs_1_.refs_0_), channel_id=1, source_target_pairs={{0,4},{1,5},{2,6},{3,7},{4,8},{5,9},{6,10},{7,11},{8,12},{9,13},{1... | collective-permute-start | bytes 1572872 | tf_op jit(solution)/shard_map/ppermute | solution.py:21
  120.5 54.1 %collective-permute-start = (bf16[2048,128]{1,0:T(8,128)(2,1)}, bf16[2048,128]{1,0:T(8,128)(2,1)S(1)}, u32[]{:S(2)}, u32[]{:S(2)}) collective-permute-start(bf16[2048,128]{1,0:T(8,128)(2,1)} %get-tuple-element.40.refs_6_.refs_0_), channel_id=1, source_target_pairs={{0,4},{1,5},{2,6},{3,7},{4,8},{5,9},{6,10},{7,11},{8,12},{9,13},{1... | collective-permute-start | bytes 1572872 | tf_op jit(solution)/shard_map/ppermute | solution.py:21
  129.6 56.2 %collective-permute-start.16 = (bf16[2048,128]{1,0:T(8,128)(2,1)}, bf16[2048,128]{1,0:T(8,128)(2,1)S(1)}, u32[]{:S(2)}, u32[]{:S(2)}) collective-permute-start(bf16[2048,128]{1,0:T(8,128)(2,1)} %get-tuple-element.41.refs_7_.refs_0_.refs_1_), channel_id=1, source_target_pairs={{0,4},{1,5},{2,6},{3,7},{4,8},{5,9},{6,10},{7,11},{8,12},{9,13},{1... | collective-permute-start | bytes 1572872 | tf_op jit(solution)/shard_map/ppermute | solution.py:21
  140.9 56.2 %collective-permute-start.21 = (bf16[2048,128]{1,0:T(8,128)(2,1)}, bf16[2048,128]{1,0:T(8,128)(2,1)}, u32[]{:S(2)}, u32[]{:S(2)}) collective-permute-start(bf16[2048,128]{1,0:T(8,128)(2,1)} %get-tuple-element.38.refs_4_.refs_0_), channel_id=1, source_target_pairs={{0,4},{1,5},{2,6},{3,7},{4,8},{5,9},{6,10},{7,11},{8,12},{9,13},{1... | collective-permute-start | bytes 1572872 | tf_op jit(solution)/shard_map/ppermute | solution.py:21
  152.1 54.8 %collective-permute-start.24 = (bf16[2048,128]{1,0:T(8,128)(2,1)}, bf16[2048,128]{1,0:T(8,128)(2,1)}, u32[]{:S(2)}, u32[]{:S(2)}) collective-permute-start(bf16[2048,128]{1,0:T(8,128)(2,1)} %get-tuple-element.39.refs_5_.refs_0_.refs_1_), channel_id=1, source_target_pairs={{0,4},{1,5},{2,6},{3,7},{4,8},{5,9},{6,10},{7,11},{8,12},{9,13},{1... | collective-permute-start | bytes 1572872 | tf_op jit(solution)/shard_map/ppermute | solution.py:21
  159.8 54.0 %copy-start.1 = (bf16[2048,128]{1,0:T(8,128)(2,1)S(1)}, bf16[2048,128]{1,0:T(8,128)(2,1)}, u32[]{:S(2)}) copy-start(bf16[2048,128]{1,0:T(8,128)(2,1)} %get-tuple-element.41.refs_7_.refs_0_.refs_1_) | copy-start | bytes 1572868
  161.5 63.4 %copy-start = (bf16[2048,128]{1,0:T(8,128)(2,1)S(1)}, bf16[2048,128]{1,0:T(8,128)(2,1)}, u32[]{:S(2)}) copy-start(bf16[2048,128]{1,0:T(8,128)(2,1)} %get-tuple-element.39.refs_5_.refs_0_.refs_1_) | copy-start | bytes 1572868
  164.0 49.8 %collective-permute-start.2 = (bf16[1,2048,128]{2,1,0:T(8,128)(2,1)S(1)}, bf16[1,2048,128]{2,1,0:T(8,128)(2,1)S(1)}, u32[]{:S(2)}, u32[]{:S(2)}) collective-permute-start(bf16[1,2048,128]{2,1,0:T(8,128)(2,1)S(1)} %pick.12), channel_id=1, source_target_pairs={{0,2},{1,3},{2,0},{3,1},{4,6},{5,7},{6,4},{7,5},{8,10},{9,11},{10,... | collective-permute-start | bytes 1572872 | tf_op jit(solution)/shard_map/ppermute | solution.py:21
  174.6 60.7 %collective-permute-start.7 = (bf16[2,2048,128]{2,1,0:T(8,128)(2,1)S(1)}, bf16[2,2048,128]{2,1,0:T(8,128)(2,1)S(1)}, u32[]{:S(2)}, u32[]{:S(2)}) collective-permute-start(bf16[2,2048,128]{2,1,0:T(8,128)(2,1)S(1)} %pick.14), channel_id=1, source_target_pairs={{0,1},{1,0},{2,3},{3,2},{4,5},{5,4},{6,7},{7,6},{8,9},{9,8},{10,11... | collective-permute-start | bytes 3145736 | tf_op jit(solution)/shard_map/ppermute | solution.py:21
  185.8 50.0 %collective-permute-start.14 = (bf16[2,2048,128]{2,1,0:T(8,128)(2,1)S(1)}, bf16[2,2048,128]{2,1,0:T(8,128)(2,1)S(1)}, u32[]{:S(2)}, u32[]{:S(2)}) collective-permute-start(bf16[2,2048,128]{2,1,0:T(8,128)(2,1)S(1)} %pick.17), channel_id=1, source_target_pairs={{0,1},{1,0},{2,3},{3,2},{4,5},{5,4},{6,7},{7,6},{8,9},{9,8},{10,11... | collective-permute-start | bytes 3145736 | tf_op jit(solution)/shard_map/ppermute | solution.py:21
  197.0 19.2 %collective-permute-start.5 = (bf16[1,2048,128]{2,1,0:T(8,128)(2,1)S(1)}, bf16[1,2048,128]{2,1,0:T(8,128)(2,1)S(1)}, u32[]{:S(2)}, u32[]{:S(2)}) collective-permute-start(bf16[1,2048,128]{2,1,0:T(8,128)(2,1)S(1)} %pick.13), channel_id=1, source_target_pairs={{0,2},{1,3},{2,0},{3,1},{4,6},{5,7},{6,4},{7,5},{8,10},{9,11},{10,... | collective-permute-start | bytes 1572872 | tf_op jit(solution)/shard_map/ppermute | solution.py:21
  206.8 18.1 %collective-permute-start.9 = (bf16[1,2048,128]{2,1,0:T(8,128)(2,1)S(1)}, bf16[1,2048,128]{2,1,0:T(8,128)(2,1)S(1)}, u32[]{:S(2)}, u32[]{:S(2)}) collective-permute-start(bf16[1,2048,128]{2,1,0:T(8,128)(2,1)S(1)} %pick.15), channel_id=1, source_target_pairs={{0,2},{1,3},{2,0},{3,1},{4,6},{5,7},{6,4},{7,5},{8,10},{9,11},{10,... | collective-permute-start | bytes 1572872 | tf_op jit(solution)/shard_map/ppermute | solution.py:21
  213.8 21.5 %collective-permute-start.12 = (bf16[1,2048,128]{2,1,0:T(8,128)(2,1)S(1)}, bf16[1,2048,128]{2,1,0:T(8,128)(2,1)S(1)}, u32[]{:S(2)}, u32[]{:S(2)}) collective-permute-start(bf16[1,2048,128]{2,1,0:T(8,128)(2,1)S(1)} %pick.16), channel_id=1, source_target_pairs={{0,2},{1,3},{2,0},{3,1},{4,6},{5,7},{6,4},{7,5},{8,10},{9,11},{10,... | collective-permute-start | bytes 1572872 | tf_op jit(solution)/shard_map/ppermute | solution.py:21
  216.3 47.6 %collective-permute-start.20 = (bf16[2,2048,128]{2,1,0:T(8,128)(2,1)S(1)}, bf16[2,2048,128]{2,1,0:T(8,128)(2,1)S(1)}, u32[]{:S(2)}, u32[]{:S(2)}) collective-permute-start(bf16[2,2048,128]{2,1,0:T(8,128)(2,1)S(1)} %pick.20), channel_id=1, source_target_pairs={{0,1},{1,0},{2,3},{3,2},{4,5},{5,4},{6,7},{7,6},{8,9},{9,8},{10,11... | collective-permute-start | bytes 3145736 | tf_op jit(solution)/shard_map/ppermute | solution.py:21
  224.9 11.0 %collective-permute-start.10 = (bf16[1,2048,128]{2,1,0:T(8,128)(2,1)S(1)}, bf16[1,2048,128]{2,1,0:T(8,128)(2,1)S(1)}, u32[]{:S(2)}, u32[]{:S(2)}) collective-permute-start(bf16[1,2048,128]{2,1,0:T(8,128)(2,1)S(1)} %collective-permute-done.9.refs_2_), channel_id=1, source_target_pairs={{0,1},{1,0},{2,3},{3,2},{4,5},{5,4},{6,7},{7,6},{8,9},{9,8},{10,11... | collective-permute-start | bytes 1572872 | tf_op jit(solution)/shard_map/ppermute | solution.py:21
  235.3 11.0 %collective-permute-start.3 = (bf16[1,2048,128]{2,1,0:T(8,128)(2,1)S(1)}, bf16[1,2048,128]{2,1,0:T(8,128)(2,1)S(1)}, u32[]{:S(2)}, u32[]{:S(2)}) collective-permute-start(bf16[1,2048,128]{2,1,0:T(8,128)(2,1)S(1)} %collective-permute-done.2.refs_2_), channel_id=1, source_target_pairs={{0,1},{1,0},{2,3},{3,2},{4,5},{5,4},{6,7},{7,6},{8,9},{9,8},{10,11... | collective-permute-start | bytes 1572872 | tf_op jit(solution)/shard_map/ppermute | solution.py:21
  235.3 11.0 %collective-permute-start.6 = (bf16[1,2048,128]{2,1,0:T(8,128)(2,1)S(1)}, bf16[1,2048,128]{2,1,0:T(8,128)(2,1)S(1)}, u32[]{:S(2)}, u32[]{:S(2)}) collective-permute-start(bf16[1,2048,128]{2,1,0:T(8,128)(2,1)S(1)} %collective-permute-done.5.refs_3_), channel_id=1, source_target_pairs={{0,1},{1,0},{2,3},{3,2},{4,5},{5,4},{6,7},{7,6},{8,9},{9,8},{10,11... | collective-permute-start | bytes 1572872 | tf_op jit(solution)/shard_map/ppermute | solution.py:21
  235.8 2.9 collective-permute-start.13
  235.9 67.3 %collective-permute-start.27 = (bf16[2,2048,128]{2,1,0:T(8,128)(2,1)S(1)}, bf16[2,2048,128]{2,1,0:T(8,128)(2,1)S(1)}, u32[]{:S(2)}, u32[]{:S(2)}) collective-permute-start(bf16[2,2048,128]{2,1,0:T(8,128)(2,1)S(1)} %pick.23), channel_id=1, source_target_pairs={{0,1},{1,0},{2,3},{3,2},{4,5},{5,4},{6,7},{7,6},{8,9},{9,8},{10,11... | collective-permute-start | bytes 3145736 | tf_op jit(solution)/shard_map/ppermute | solution.py:21
  255.5 14.9 %collective-permute-start.15 = (bf16[1,2048,128]{2,1,0:T(8,128)(2,1)S(1)}, bf16[1,2048,128]{2,1,0:T(8,128)(2,1)S(1)}, u32[]{:S(2)}, u32[]{:S(2)}) collective-permute-start(bf16[1,2048,128]{2,1,0:T(8,128)(2,1)S(1)} %pick.18), channel_id=1, source_target_pairs={{0,2},{1,3},{2,0},{3,1},{4,6},{5,7},{6,4},{7,5},{8,10},{9,11},{10,... | collective-permute-start | bytes 1572872 | tf_op jit(solution)/shard_map/ppermute | solution.py:21
  258.5 23.1 %collective-permute-start.17 = (bf16[1,2048,128]{2,1,0:T(8,128)(2,1)S(1)}, bf16[1,2048,128]{2,1,0:T(8,128)(2,1)S(1)}, u32[]{:S(2)}, u32[]{:S(2)}) collective-permute-start(bf16[1,2048,128]{2,1,0:T(8,128)(2,1)S(1)} %pick.19), channel_id=1, source_target_pairs={{0,2},{1,3},{2,0},{3,1},{4,6},{5,7},{6,4},{7,5},{8,10},{9,11},{10,... | collective-permute-start | bytes 1572872 | tf_op jit(solution)/shard_map/ppermute | solution.py:21
  260.6 32.1 %collective-permute-start.22 = (bf16[1,2048,128]{2,1,0:T(8,128)(2,1)S(1)}, bf16[1,2048,128]{2,1,0:T(8,128)(2,1)S(1)}, u32[]{:S(2)}, u32[]{:S(2)}) collective-permute-start(bf16[1,2048,128]{2,1,0:T(8,128)(2,1)S(1)} %pick.21), channel_id=1, source_target_pairs={{0,2},{1,3},{2,0},{3,1},{4,6},{5,7},{6,4},{7,5},{8,10},{9,11},{10,... | collective-permute-start | bytes 1572872 | tf_op jit(solution)/shard_map/ppermute | solution.py:21
  263.9 39.3 %collective-permute-start.25 = (bf16[1,2048,128]{2,1,0:T(8,128)(2,1)S(1)}, bf16[1,2048,128]{2,1,0:T(8,128)(2,1)S(1)}, u32[]{:S(2)}, u32[]{:S(2)}) collective-permute-start(bf16[1,2048,128]{2,1,0:T(8,128)(2,1)S(1)} %pick.22), channel_id=1, source_target_pairs={{0,2},{1,3},{2,0},{3,1},{4,6},{5,7},{6,4},{7,5},{8,10},{9,11},{10,... | collective-permute-start | bytes 1572872 | tf_op jit(solution)/shard_map/ppermute | solution.py:21
  270.3 48.5 %collective-permute-start.18 = (bf16[1,2048,128]{2,1,0:T(8,128)(2,1)S(1)}, bf16[1,2048,128]{2,1,0:T(8,128)(2,1)S(1)}, u32[]{:S(2)}, u32[]{:S(2)}) collective-permute-start(bf16[1,2048,128]{2,1,0:T(8,128)(2,1)S(1)} %collective-permute-done.15.refs_0_), channel_id=1, source_target_pairs={{0,1},{1,0},{2,3},{3,2},{4,5},{5,4},{6,7},{7,6},{8,9},{9,8},{10,11... | collective-permute-start | bytes 1572872 | tf_op jit(solution)/shard_map/ppermute | solution.py:21
  281.6 37.2 %collective-permute-start.19 = (bf16[1,2048,128]{2,1,0:T(8,128)(2,1)S(1)}, bf16[1,2048,128]{2,1,0:T(8,128)(2,1)S(1)}, u32[]{:S(2)}, u32[]{:S(2)}) collective-permute-start(bf16[1,2048,128]{2,1,0:T(8,128)(2,1)S(1)} %collective-permute-done.17.refs_1_), channel_id=1, source_target_pairs={{0,1},{1,0},{2,3},{3,2},{4,5},{5,4},{6,7},{7,6},{8,9},{9,8},{10,11... | collective-permute-start | bytes 1572872 | tf_op jit(solution)/shard_map/ppermute | solution.py:21
  292.8 10.5 %collective-permute-start.23 = (bf16[1,2048,128]{2,1,0:T(8,128)(2,1)S(1)}, bf16[1,2048,128]{2,1,0:T(8,128)(2,1)S(1)}, u32[]{:S(2)}, u32[]{:S(2)}) collective-permute-start(bf16[1,2048,128]{2,1,0:T(8,128)(2,1)S(1)} %collective-permute-done.22.refs_2_), channel_id=1, source_target_pairs={{0,1},{1,0},{2,3},{3,2},{4,5},{5,4},{6,7},{7,6},{8,9},{9,8},{10,11... | collective-permute-start | bytes 1572872 | tf_op jit(solution)/shard_map/ppermute | solution.py:21
  303.1 1.9 collective-permute-start.26
